TPU v7x, 32 devices: a whole 2x2x4 slice. The times are simulated.
32 devices in a mesh: ens: 2 (over core), lat: 4 (over z), lon: 4 (over y, x).
Axes of the slice: x: 2, y: 2, z: 4, core: 2. Of those that a mesh axis runs over, the one named last changes fastest.
Arguments:
- grad_tokens: bfloat16 [104, 32768], P(None, ('lat', 'lon')), may hold values from -6 to 6
- token_index: int32 [64, 512], P('lat', 'lon'), may hold values from 0 to 32767, as said below
- members: bfloat16 [4, 104, 64, 512], P('ens', None, 'lat', 'lon'), may hold values from -6 to 6
- lat_taps: float32 [17], replicated, may hold values from 0.05 to 1
- lon_taps: float32 [17], replicated, may hold values from 0.05 to 1
Outputs:
- increment: float32 [104, 64, 512], P('ens', 'lat', 'lon')
Inputs may be any that keep to these rules, and one draw needn't show every extreme that they name: `token_index`: every token is the token of exactly one cell. With grid blocks numbered b = (latitude block) * (longitude blocks) + (longitude block), each of 16 x 128 cells, the cells of block b that take tokens from s * 2048 .. (s + 1) * 2048 - 1 take exactly the tokens s * 2048 + b * 128 + k for k = 0 .. 127, in any order over the block's cells.
All inputs are finite; a program needn't handle non-finite values.
Results may differ from a plain program's by a relative error of at most 0.0003.
Values may be sent and summed in bfloat16 or wider, within the bound.
No kernel may reach another device: no remote copies, remote signals or barrier semaphores. Data moves between devices by JAX's collectives and lax.ppermute only.
A program may use at most 64 MiB of HBM per device.

v0:
```python
import jax
import jax.numpy as jnp
from jax import lax
from jax.sharding import PartitionSpec as P


def with_halo(shard, sides, width):
    for axis, dim in sides:
        size, length = (lax.axis_size(axis), shard.shape[dim])
        up = [(i, (i + 1) % size) for i in range(size)]
        down = [(j, i) for i, j in up]
        last = lax.slice_in_dim(shard, length - width, length, axis=dim)
        first = lax.slice_in_dim(shard, 0, width, axis=dim)
        before = lax.ppermute(last, axis, up)
        after = lax.ppermute(first, axis, down)
        shard = jnp.concatenate([before, shard, after], axis=dim)
    return shard


def banded(taps, length, radius):
    upper = jnp.arange(length + 2 * radius, dtype=jnp.int32)[:, None]
    lower = jnp.arange(length, dtype=jnp.int32)[None, :]
    offset = upper - lower
    picks = (
        offset[:, :, None] == jnp.arange(2 * radius + 1, dtype=jnp.int32)[None, None, :]
    ).astype(jnp.float32)
    return jnp.einsum("uiq,q->ui", picks, taps, precision=lax.Precision.HIGHEST)


def edge_keep(rows, radius):
    lat_pos = lax.axis_index("lat")
    lat_count = lax.axis_size("lat")
    row_ids = jnp.arange(rows, dtype=jnp.int32)
    keep_top = jnp.where(lat_pos > 0, 1.0, 0.0)
    keep_bottom = jnp.where(lat_pos < lat_count - 1, 1.0, 0.0)
    keep = jnp.where(
        row_ids < radius, keep_top, jnp.where(row_ids >= rows - radius, keep_bottom, 1.0)
    )
    return keep.astype(jnp.float32)


def localize(field, lat_w, lon_w):
    radius = (lat_w.shape[0] - 1) // 2
    lat_rows = field.shape[2]
    lon_cols = field.shape[3]
    lat_matrix = banded(lat_w, lat_rows, radius)
    lon_matrix = banded(lon_w, lon_cols, radius)
    padded = with_halo(field, (("lat", 2),), radius)
    padded = padded * edge_keep(padded.shape[2], radius)[:, None]
    middle = jnp.einsum("mcul,ui->mcil", padded, lat_matrix, precision=lax.Precision.HIGHEST)
    widened = with_halo(middle, (("lon", 3),), radius)
    return jnp.einsum("mciu,uj->mcij", widened, lon_matrix, precision=lax.Precision.HIGHEST)


def local(grad_tokens, token_index, members, lat_taps, lon_taps):
    channels, cells = grad_tokens.shape
    lat_rows, lon_cols = token_index.shape
    lon_count = lax.axis_size("lon")
    blocks = lax.axis_size("lat") * lon_count
    piece = cells // blocks
    block_id = lax.axis_index("lat") * lon_count + lax.axis_index("lon")
    wanted = token_index.reshape(-1)
    source = wanted // cells
    offset = source * piece + wanted % cells - block_id * piece
    moved = lax.all_to_all(
        grad_tokens.reshape(channels, blocks, piece),
        ("lat", "lon"),
        split_axis=1,
        concat_axis=1,
        tiled=True,
    )
    grid = jnp.take(moved.reshape(channels, cells), offset, axis=1)
    grid_plain = grid.reshape(channels, lat_rows, lon_cols)
    weighted = members.astype(jnp.float32) * grid_plain.astype(jnp.float32)[None]
    control = localize(weighted, lat_taps[::-1], lon_taps[::-1])
    smoothed = localize(control, lat_taps, lon_taps)
    partial_total = jnp.sum(members.astype(jnp.float32) * smoothed, axis=0)
    summed = lax.psum_scatter(partial_total, "ens", scatter_dimension=0, tiled=True)
    return summed / (lax.axis_size("ens") * members.shape[0] - 1)


def solution(mesh):
    in_specs = (P(None, ("lat", "lon")), P("lat", "lon"), P("ens", None, "lat", "lon"), P(), P())
    out_specs = P("ens", "lat", "lon")
    return jax.shard_map(local, mesh=mesh, in_specs=in_specs, out_specs=out_specs, check_vma=False)
```

profile of v0, /device:TPU:0, one launch (start us, length us, event | category | flops | bytes accessed | tf_op | source)
XLA Modules:
  0.0 191.1 jit_solution(9024980644403303808)
XLA Ops:
  8.4 8.3 %all-to-all-start = ((bf16[104,16,128]{2,0,1:T(8,128)(2,1)}), bf16[104,16,128]{2,0,1:T(8,128)(2,1)S(1)}, u32[]{:S(2)}, u32[]{:S(2)}) async-start(bf16[104,16,128]{2,0,1:T(8,128)(2,1)} %copy_bitcast_fusion), calls=%async_computation | async-start | bytes 851968 | tf_op jit(solution)/shard_map/all_to_all | solution.py:65
  16.9 13.0 %all-to-all-done = bf16[104,16,128]{2,0,1:T(8,128)(2,1)S(1)} async-done(((bf16[104,16,128]{2,0,1:T(8,128)(2,1)}), bf16[104,16,128]{2,0,1:T(8,128)(2,1)S(1)}, u32[]{:S(2)}, u32[]{:S(2)}) %all-to-all-start) | async-done | bytes 426016 | tf_op jit(solution)/shard_map/all_to_all | solution.py:65
  30.2 6.2 %gather_fusion = bf16[2048,104]{1,0:T(8,128)(2,1)S(1)} fusion(bf16[104,2048]{0,1:T(8,128)(2,1)S(1)} %bitcast.55, s32[2048]{0:T(1024)S(1)} %broadcast_clamp_fusion), kind=kCustom, calls=%fused_computation | custom fusion | bytes 860160 | tf_op jit(solution)/shard_map/jit(_take)/gather | solution.py:72
  37.8 1.4 fusion.56
  39.5 1.1 collective-permute-start
  40.6 2.7 %collective-permute-start.1 = (f32[2,104,8,128]{3,2,1,0:T(8,128)}, f32[2,104,8,128]{3,2,1,0:T(8,128)S(1)}, u32[]{:S(2)}, u32[]{:S(2)}) collective-permute-start(f32[2,104,8,128]{3,2,1,0:T(8,128)} %get-tuple-element.12), channel_id=1, source_target_pairs={{4,0},{8,4},{12,8},{0,12},{5,1},{9,5},{13,9},{1,13},{6,2},{10,6},{... | collective-permute-start | bytes 2555912 | tf_op jit(solution)/shard_map/ppermute | solution.py:15
  43.5 1.1 fusion.33
  44.8 18.5 %collective-permute-done = f32[2,104,8,128]{3,2,1,0:T(8,128)S(1)} collective-permute-done((f32[2,104,8,128]{3,2,1,0:T(8,128)}, f32[2,104,8,128]{3,2,1,0:T(8,128)S(1)}, u32[]{:S(2)}, u32[]{:S(2)}) %collective-permute-start) | collective-permute-done | bytes 852000 | tf_op jit(solution)/shard_map/ppermute | solution.py:14
  63.3 14.6 %collective-permute-done.1 = f32[2,104,8,128]{3,2,1,0:T(8,128)S(1)} collective-permute-done((f32[2,104,8,128]{3,2,1,0:T(8,128)}, f32[2,104,8,128]{3,2,1,0:T(8,128)S(1)}, u32[]{:S(2)}, u32[]{:S(2)}) %collective-permute-start.1) | collective-permute-done | bytes 852000 | tf_op jit(solution)/shard_map/ppermute | solution.py:15
  78.8 3.5 %fusion.32 = f32[2,104,16,128]{3,2,1,0:T(8,128)S(1)} fusion(f32[32,16,1,1]{1,0,3,2:T(8,128)S(1)} %bitcast.61, f32[2,104,8,128]{3,2,1,0:T(8,128)} %copy-done.4, f32[2,104,16,128]{3,2,1,0:T(8,128)} %copy-done.1, f32[2,104,8,128]{3,2,1,0:T(8,128)} %copy-done.3, f32[32]{0:T(128)S(1)} %compare_select_fusion.6), kind=kOutput, calls=%fused_computation.35 | convolution fusion | flops 166133760 | bytes 5113984 | tf_op jit(solution)/shard_map/mcul,ui->mcil/dot_general | solution.py:50
  82.3 2.3 %fusion.55 = (f32[2,104,16,8]{3,2,1,0:T(8,128)}, f32[2,104,16,8]{3,2,1,0:T(8,128)}) fusion(f32[2,104,16,128]{3,2,1,0:T(8,128)S(1)} %fusion.32), kind=kLoop, calls=%fused_computation.82 | loop fusion | bytes 425984 | tf_op jit(solution)/shard_map/slice | solution.py:12
  84.6 2.7 %copy.32 = f32[2,104,16,8]{1,3,2,0:T(8,128)} copy(f32[2,104,16,8]{3,2,1,0:T(8,128)} %get-tuple-element.9) | data formatting | bytes 212992 | tf_op jit(solution)/shard_map/slice | solution.py:12
  87.3 2.0 %copy.33 = f32[2,104,16,8]{1,3,2,0:T(8,128)S(1)} copy(f32[2,104,16,8]{3,2,1,0:T(8,128)} %get-tuple-element.10) | data formatting | bytes 212992 | tf_op jit(solution)/shard_map/slice | solution.py:13
  89.3 1.3 collective-permute-start.3
  92.0 6.3 %collective-permute-done.2 = f32[2,104,16,8]{1,3,2,0:T(8,128)} collective-permute-done((f32[2,104,16,8]{1,3,2,0:T(8,128)}, f32[2,104,16,8]{1,3,2,0:T(8,128)}, u32[]{:S(2)}, u32[]{:S(2)}) %collective-permute-start.2) | collective-permute-done | bytes 106528 | tf_op jit(solution)/shard_map/ppermute | solution.py:14
  98.3 2.7 %copy.34 = f32[2,104,16,8]{3,2,1,0:T(8,128)} copy(f32[2,104,16,8]{1,3,2,0:T(8,128)} %collective-permute-done.2) | data formatting | bytes 212992 | tf_op jit(solution)/shard_map/ppermute | solution.py:14
  101.0 2.7 %copy.35 = f32[2,104,16,8]{3,2,1,0:T(8,128)} copy(f32[2,104,16,8]{1,3,2,0:T(8,128)} %collective-permute-done.3) | data formatting | bytes 212992 | tf_op jit(solution)/shard_map/ppermute | solution.py:15
  103.7 5.3 %fusion.5 = f32[2,104,16,128]{3,2,1,0:T(8,128)S(1)} fusion(f32[144,128,1,1]{1,0,3,2:T(8,128)S(1)} %bitcast.57, f32[2,104,16,8]{3,2,1,0:T(8,128)} %copy.35, f32[2,104,16,128]{3,2,1,0:T(8,128)S(1)} %fusion.32, f32[2,104,16,8]{3,2,1,0:T(8,128)} %copy.34), kind=kOutput, calls=%fused_computation.7 | convolution fusion | flops 737058816 | bytes 3694592 | tf_op jit(solution)/shard_map/mciu,uj->mcij/dot_general | solution.py:52
  109.8 3.3 %collective-permute-start.5 = (f32[2,104,8,128]{3,2,1,0:T(8,128)S(1)}, f32[2,104,8,128]{3,2,1,0:T(8,128)S(1)}, u32[]{:S(2)}, u32[]{:S(2)}) collective-permute-start(f32[2,104,8,128]{3,2,1,0:T(8,128)S(1)} %get-tuple-element.8), channel_id=1, source_target_pairs={{4,0},{8,4},{12,8},{0,12},{5,1},{9,5},{13,9},{1,13},{6,2},{10,6},{... | collective-permute-start | bytes 2555912 | tf_op jit(solution)/shard_map/ppermute | solution.py:15
  114.1 18.7 %collective-permute-done.4 = f32[2,104,8,128]{3,2,1,0:T(8,128)S(1)} collective-permute-done((f32[2,104,8,128]{3,2,1,0:T(8,128)S(1)}, f32[2,104,8,128]{3,2,1,0:T(8,128)S(1)}, u32[]{:S(2)}, u32[]{:S(2)}) %collective-permute-start.4) | collective-permute-done | bytes 852000 | tf_op jit(solution)/shard_map/ppermute | solution.py:14
  132.9 14.9 %collective-permute-done.5 = f32[2,104,8,128]{3,2,1,0:T(8,128)S(1)} collective-permute-done((f32[2,104,8,128]{3,2,1,0:T(8,128)S(1)}, f32[2,104,8,128]{3,2,1,0:T(8,128)S(1)}, u32[]{:S(2)}, u32[]{:S(2)}) %collective-permute-start.5) | collective-permute-done | bytes 852000 | tf_op jit(solution)/shard_map/ppermute | solution.py:15
  147.8 1.9 %fusion.31 = f32[2,104,16,128]{3,2,1,0:T(8,128)S(1)} fusion(f32[32,16,1,1]{1,0,3,2:T(8,128)S(1)} %bitcast.62, f32[2,104,8,128]{3,2,1,0:T(8,128)S(1)} %collective-permute-done.5, f32[2,104,16,128]{3,2,1,0:T(8,128)S(1)} %fusion.5, f32[2,104,8,128]{3,2,1,0:T(8,128)S(1)} %collective-permute-done.4, f32[32]{0:T(128)S(1)} %compare_select_fusion.6), kind=kOutput, calls=%fused_computation.34 | convolution fusion | flops 166133760 | bytes 5113984 | tf_op jit(solution)/shard_map/mcul,ui->mcil/dot_general | solution.py:50
  149.7 2.3 %fusion.53 = (f32[2,104,16,8]{3,2,1,0:T(8,128)}, f32[2,104,16,8]{3,2,1,0:T(8,128)}) fusion(f32[2,104,16,128]{3,2,1,0:T(8,128)S(1)} %fusion.31), kind=kLoop, calls=%fused_computation.80 | loop fusion | bytes 425984 | tf_op jit(solution)/shard_map/slice | solution.py:12
  152.0 2.7 %copy.36 = f32[2,104,16,8]{1,3,2,0:T(8,128)} copy(f32[2,104,16,8]{3,2,1,0:T(8,128)} %get-tuple-element.5) | data formatting | bytes 212992 | tf_op jit(solution)/shard_map/slice | solution.py:12
  154.7 2.0 %copy.37 = f32[2,104,16,8]{1,3,2,0:T(8,128)S(1)} copy(f32[2,104,16,8]{3,2,1,0:T(8,128)} %get-tuple-element.6) | data formatting | bytes 212992 | tf_op jit(solution)/shard_map/slice | solution.py:13
  156.7 1.6 collective-permute-start.7
  159.4 5.7 %collective-permute-done.6 = f32[2,104,16,8]{1,3,2,0:T(8,128)} collective-permute-done((f32[2,104,16,8]{1,3,2,0:T(8,128)}, f32[2,104,16,8]{1,3,2,0:T(8,128)}, u32[]{:S(2)}, u32[]{:S(2)}) %collective-permute-start.6) | collective-permute-done | bytes 106528 | tf_op jit(solution)/shard_map/ppermute | solution.py:14
  165.2 2.7 %copy.38 = f32[2,104,16,8]{3,2,1,0:T(8,128)} copy(f32[2,104,16,8]{1,3,2,0:T(8,128)} %collective-permute-done.6) | data formatting | bytes 212992 | tf_op jit(solution)/shard_map/ppermute | solution.py:14
  167.9 2.7 %copy.39 = f32[2,104,16,8]{3,2,1,0:T(8,128)} copy(f32[2,104,16,8]{1,3,2,0:T(8,128)} %collective-permute-done.7) | data formatting | bytes 212992 | tf_op jit(solution)/shard_map/ppermute | solution.py:15
  170.6 6.2 %fusion.22 = f32[104,16,128]{2,1,0:T(8,128)} fusion(bf16[2,104,16,128]{3,2,1,0:T(8,128)(2,1)S(1)} %copy-done.2, f32[144,128,1,1]{1,0,3,2:T(8,128)S(1)} %bitcast.58, f32[2,104,16,8]{3,2,1,0:T(8,128)} %copy.39, f32[2,104,16,128]{3,2,1,0:T(8,128)S(1)} %fusion.31, f32[2,104,16,8]{3,2,1,0:T(8,128)} %copy.38), kind=kOutput, calls=%fused_computation.27 | convolution fusion | flops 738123776 | bytes 3694592 | tf_op jit(solution)/shard_map/mciu,uj->mcij/dot_general | solution.py:52
  176.8 5.6 %reduce-scatter.2.cloned.1.call-done = f32[52,16,128]{2,1,0:T(8,128)} async-done(((f32[104,16,128]{2,1,0:T(8,128)}), f32[52,16,128]{2,1,0:T(8,128)}) %reduce-scatter.2.cloned.1.call-update) | async-done | bytes 426000 | tf_op jit(solution)/shard_map/reduce_scatter | solution.py:78
  182.4 1.8 broadcast_multiply_fusion
  (41 shorter events, 9.5 us)
Async XLA Ops:
  6.5 1.0 copy-start
  6.5 10.2 %copy-start.5 = (s32[16,128]{1,0:T(8,128)S(1)}, s32[16,128]{1,0:T(8,128)}, u32[]{:S(2)}) copy-start(s32[16,128]{1,0:T(8,128)} %param.6) | copy-start | bytes 24580
  8.4 21.6 %all-to-all-start = ((bf16[104,16,128]{2,0,1:T(8,128)(2,1)}), bf16[104,16,128]{2,0,1:T(8,128)(2,1)S(1)}, u32[]{:S(2)}, u32[]{:S(2)}) async-start(bf16[104,16,128]{2,0,1:T(8,128)(2,1)} %copy_bitcast_fusion), calls=%async_computation | async-start | bytes 851968 | tf_op jit(solution)/shard_map/all_to_all | solution.py:65
  16.7 165.7 %reduce-scatter.2.cloned.1.call-start = ((), (), s32[]{:S(2)}) async-start(), calls=%async_computation.2 | async-start | bytes 1277952 | tf_op jit(solution)/shard_map/reduce_scatter | solution.py:78
  36.4 1.2 copy-start.2
  37.7 1.7 copy-start.1
  37.8 5.5 %copy-start.6 = (f32[17]{0:T(128)S(1)}, f32[17]{0:T(128)}, u32[]{:S(2)}) copy-start(f32[17]{0:T(128)} %param.8) | copy-start | bytes 208
  37.8 5.6 %copy-start.7 = (f32[17]{0:T(128)S(1)}, f32[17]{0:T(128)}, u32[]{:S(2)}) copy-start(f32[17]{0:T(128)} %param.9) | copy-start | bytes 208
  39.5 23.8 %collective-permute-start = (f32[2,104,8,128]{3,2,1,0:T(8,128)}, f32[2,104,8,128]{3,2,1,0:T(8,128)S(1)}, u32[]{:S(2)}, u32[]{:S(2)}) collective-permute-start(f32[2,104,8,128]{3,2,1,0:T(8,128)} %get-tuple-element.11), channel_id=1, source_target_pairs={{0,4},{4,8},{8,12},{12,0},{1,5},{5,9},{9,13},{13,1},{2,6},{6,10},{... | collective-permute-start | bytes 2555912 | tf_op jit(solution)/shard_map/ppermute | solution.py:14
  40.6 37.3 %collective-permute-start.1 = (f32[2,104,8,128]{3,2,1,0:T(8,128)}, f32[2,104,8,128]{3,2,1,0:T(8,128)S(1)}, u32[]{:S(2)}, u32[]{:S(2)}) collective-permute-start(f32[2,104,8,128]{3,2,1,0:T(8,128)} %get-tuple-element.12), channel_id=1, source_target_pairs={{4,0},{8,4},{12,8},{0,12},{5,1},{9,5},{13,9},{1,13},{6,2},{10,6},{... | collective-permute-start | bytes 2555912 | tf_op jit(solution)/shard_map/ppermute | solution.py:15
  63.3 14.6 %copy-start.3 = (f32[2,104,8,128]{3,2,1,0:T(8,128)}, f32[2,104,8,128]{3,2,1,0:T(8,128)S(1)}, u32[]{:S(2)}) copy-start(f32[2,104,8,128]{3,2,1,0:T(8,128)S(1)} %collective-permute-done) | copy-start | bytes 2555908
  77.9 0.9 copy-start.4
  89.3 11.7 %collective-permute-start.3 = (f32[2,104,16,8]{1,3,2,0:T(8,128)S(1)}, f32[2,104,16,8]{1,3,2,0:T(8,128)}, u32[]{:S(2)}, u32[]{:S(2)}) collective-permute-start(f32[2,104,16,8]{1,3,2,0:T(8,128)S(1)} %copy.33), channel_id=1, source_target_pairs={{1,0},{2,1},{3,2},{0,3},{5,4},{6,5},{7,6},{4,7},{9,8},{10,9},{11,1... | collective-permute-start | bytes 319496 | tf_op jit(solution)/shard_map/ppermute | solution.py:15
  90.6 7.7 %collective-permute-start.2 = (f32[2,104,16,8]{1,3,2,0:T(8,128)}, f32[2,104,16,8]{1,3,2,0:T(8,128)}, u32[]{:S(2)}, u32[]{:S(2)}) collective-permute-start(f32[2,104,16,8]{1,3,2,0:T(8,128)} %copy.32), channel_id=1, source_target_pairs={{0,1},{1,2},{2,3},{3,0},{4,5},{5,6},{6,7},{7,4},{8,9},{9,10},{10,1... | collective-permute-start | bytes 319496 | tf_op jit(solution)/shard_map/ppermute | solution.py:14
  109.2 23.7 %collective-permute-start.4 = (f32[2,104,8,128]{3,2,1,0:T(8,128)S(1)}, f32[2,104,8,128]{3,2,1,0:T(8,128)S(1)}, u32[]{:S(2)}, u32[]{:S(2)}) collective-permute-start(f32[2,104,8,128]{3,2,1,0:T(8,128)S(1)} %get-tuple-element.7), channel_id=1, source_target_pairs={{0,4},{4,8},{8,12},{12,0},{1,5},{5,9},{9,13},{13,1},{2,6},{6,10},{... | collective-permute-start | bytes 2555912 | tf_op jit(solution)/shard_map/ppermute | solution.py:14
  109.8 38.0 %collective-permute-start.5 = (f32[2,104,8,128]{3,2,1,0:T(8,128)S(1)}, f32[2,104,8,128]{3,2,1,0:T(8,128)S(1)}, u32[]{:S(2)}, u32[]{:S(2)}) collective-permute-start(f32[2,104,8,128]{3,2,1,0:T(8,128)S(1)} %get-tuple-element.8), channel_id=1, source_target_pairs={{4,0},{8,4},{12,8},{0,12},{5,1},{9,5},{13,9},{1,13},{6,2},{10,6},{... | collective-permute-start | bytes 2555912 | tf_op jit(solution)/shard_map/ppermute | solution.py:15
  156.7 11.2 %collective-permute-start.7 = (f32[2,104,16,8]{1,3,2,0:T(8,128)S(1)}, f32[2,104,16,8]{1,3,2,0:T(8,128)}, u32[]{:S(2)}, u32[]{:S(2)}) collective-permute-start(f32[2,104,16,8]{1,3,2,0:T(8,128)S(1)} %copy.37), channel_id=1, source_target_pairs={{1,0},{2,1},{3,2},{0,3},{5,4},{6,5},{7,6},{4,7},{9,8},{10,9},{11,1... | collective-permute-start | bytes 319496 | tf_op jit(solution)/shard_map/ppermute | solution.py:15
  158.3 6.9 %collective-permute-start.6 = (f32[2,104,16,8]{1,3,2,0:T(8,128)}, f32[2,104,16,8]{1,3,2,0:T(8,128)}, u32[]{:S(2)}, u32[]{:S(2)}) collective-permute-start(f32[2,104,16,8]{1,3,2,0:T(8,128)} %copy.36), channel_id=1, source_target_pairs={{0,1},{1,2},{2,3},{3,0},{4,5},{5,6},{6,7},{7,4},{8,9},{9,10},{10,1... | collective-permute-start | bytes 319496 | tf_op jit(solution)/shard_map/ppermute | solution.py:14
Sparse Core Ops, SparseCore 0:
  176.9 5.4 reduce-scatter.1
where the time goes:
time: 192 us; the launch traced here: 191 us
  waiting for transfers between devices  97.4 us (51%)
  local copies, waits for them, and re-layouts  37.2 us (19%)
  matrix products  20.4 us (11%)
  starting transfers between devices  20.2 us (11%)
  between operations  13.6 us (7%)
  other arithmetic  2.32 us (1%)
    ppermute x4, waiting for transfers between devices, with_halo(): before = lax.ppermute(last, axis, up)  49.3 us
    ppermute x4, waiting for transfers between devices, with_halo(): after = lax.ppermute(first, axis, down)  29.5 us
    all_to_all x1, waiting for transfers between devices, local(): lax.all_to_all(grad_tokens.reshape(channels, blocks, piece), ('lat', 'lon...  13 us
    dot_general x2, matrix products, localize(): jnp.einsum('mciu,uj->mcij', widened, lon_matrix, precision=lax.Precision....  11.5 us
    slice x6, local copies, waits for them, and re-layouts, with_halo(): last = lax.slice_in_dim(shard, length - width, length, axis=dim)  11.4 us
    ppermute x4, starting transfers between devices, with_halo(): after = lax.ppermute(first, axis, down)  8.83 us
    all_to_all x1, starting transfers between devices, local(): lax.all_to_all(grad_tokens.reshape(channels, blocks, piece), ('lat', 'lon...  8.34 us
    gather x2, local copies, waits for them, and re-layouts, local(): grid = jnp.take(moved.reshape(channels, cells), offset, axis=1)  6.56 us
  transfers between devices with their start and end apart: 10, of which 8 were waited for; matrix products, arithmetic and copies ran while one was open for 5% of the time, Pallas kernels for 0%

commit v1 on v0

v1 whole, which is shorter than its diff:
```python
import functools

import jax
import jax.numpy as jnp
from jax import lax
from jax.experimental import pallas as pl
from jax.experimental.pallas import tpu as pltpu
from jax.sharding import PartitionSpec as P

LANES = 128
F32 = jnp.float32
BF16 = jnp.bfloat16


def dot(a, b):
    return lax.dot_general(a, b, (((1,), (0,)), ((), ())), preferred_element_type=F32)


def split(v):
    hi = v.astype(BF16)
    return hi, (v - hi.astype(F32)).astype(BF16)


def split_outside(v):
    hi = lax.reduce_precision(v, 8, 7)
    return hi.astype(BF16), (v - hi).astype(BF16)


def band(taps, offset):
    total = jnp.zeros(offset.shape, F32)
    for k in range(taps.shape[0]):
        total = total + jnp.where(offset == k, taps[k], 0.0)
    return total


def lon_matrix(taps, cols, strip):
    count = taps.shape[0]
    radius2 = count - 1
    longer = jnp.concatenate([jnp.zeros(radius2, F32), taps, jnp.zeros(radius2, F32)])
    both = jnp.stack(
        [jnp.sum(taps * longer[radius2 - d : radius2 - d + count]) for d in range(-radius2, radius2 + 1)]
    )
    place = jnp.arange(2 * LANES, dtype=jnp.int32)[:, None]
    inner = place % strip
    source = jnp.where(
        place < cols,
        place,
        jnp.where(place < cols + LANES // 2, inner - strip, cols + inner),
    )
    target = jnp.arange(cols, dtype=jnp.int32)[None, :]
    matrix = band(both, source - target + radius2)
    hi, lo = split_outside(matrix)
    return jnp.concatenate([hi, lo], axis=1)


def lat_matrix(taps, rows, lat_pos, lat_count):
    radius = (taps.shape[0] - 1) // 2
    out_row = jnp.arange(3 * rows, dtype=jnp.int32)[:, None] - rows
    mid_row = jnp.arange(rows + 2 * radius, dtype=jnp.int32) - radius
    own_row = jnp.arange(rows, dtype=jnp.int32)[None, :]
    whole_row = lat_pos * rows + mid_row
    inside = (whole_row >= 0) & (whole_row < lat_count * rows)
    spread = band(taps, mid_row[None, :] - out_row + radius)
    gather = band(taps[::-1], own_row - mid_row[:, None] + radius)
    gather = jnp.where(inside[:, None], gather, 0.0)
    matrix = jnp.sum(spread[:, :, None] * gather[None, :, :], axis=1)
    hi, lo = split_outside(matrix)
    return jnp.concatenate([hi, lo, hi], axis=1)


def pick_matrix(slot, strip, cols):
    lane = lax.broadcasted_iota(jnp.int32, (cols, LANES), 1)
    row = lax.broadcasted_iota(jnp.int32, (cols, LANES), 0)
    here = lane // strip == slot
    first = here & (row == lane % strip)
    last = here & (row == cols - strip + lane % strip)
    one = jnp.concatenate([first.astype(F32), last.astype(F32)], axis=1)
    return one.astype(BF16)


def pack_kernel(strip, slots, w_ref, first_ref, last_ref):
    members, channels, rows, cols = w_ref.shape
    per = max(1, slots // members)
    for h in range(max(1, members // slots)):
        total = None
        for k in range(slots):
            c2, m = (k // members, k % members) if members <= slots else (0, h * slots + k)
            plane = w_ref[m].reshape(channels // per, per, rows, cols)[:, c2]
            part = dot(plane.reshape(-1, cols), pick_matrix(k, strip, cols))
            total = part if total is None else total + part
        total = total.astype(BF16)
        first_ref[h] = total[:, :LANES].reshape(channels // per, rows, LANES)
        last_ref[h] = total[:, LANES:].reshape(channels // per, rows, LANES)


def gather_kernel(strip, slots, moved_ref, offset_ref, grid_ref, first_ref, last_ref, scratch):
    pieces, channels, width = moved_ref.shape
    rows, cols = offset_ref.shape
    scratch[channels:] = jnp.zeros((scratch.shape[0] - channels, rows, cols), F32)
    tokens = jnp.concatenate([moved_ref[n] for n in range(pieces)], axis=1)
    token = lax.broadcasted_iota(jnp.int32, (pieces * width, 2 * cols), 0)
    for i in range(0, rows, 2):
        wanted = jnp.concatenate([offset_ref[i : i + 1], offset_ref[i + 1 : i + 2]], axis=1)
        chosen = jnp.where(token == wanted, 1.0, 0.0).astype(BF16)
        found = dot(tokens, chosen)
        scratch[:channels, i, :] = found[:, :cols]
        scratch[:channels, i + 1, :] = found[:, cols:]
    grid = scratch[...].astype(BF16)
    grid_ref[...] = grid[:channels]
    groups = scratch.shape[0] // slots
    planes = grid.reshape(groups, slots, rows, cols)
    total = None
    for k in range(slots):
        part = dot(planes[:, k].reshape(-1, cols), pick_matrix(k, strip, cols))
        total = part if total is None else total + part
    total = total.astype(BF16)
    first_ref[...] = total[:, :LANES].reshape(groups, rows, LANES)
    last_ref[...] = total[:, LANES:].reshape(groups, rows, LANES)


def smooth_kernel(
    strip, slots, start, count, own_ref, up_ref, down_ref, left_ref, right_ref,
    grid_ref, grid_left_ref, grid_right_ref, lon_ref, lat_ref, out_ref, out_up_ref, out_down_ref,
):
    members, channels, rows, cols = own_ref.shape
    per = max(1, slots // members)
    lon_both = lon_ref[...]
    lon_hi = lon_both[:, :cols]
    lat = lat_ref[...]
    lane = lax.broadcasted_iota(jnp.int32, (rows, LANES), 1)
    half = LANES // 2
    src = lax.broadcasted_iota(jnp.int32, (LANES, LANES), 0)
    dst = lax.broadcasted_iota(jnp.int32, (LANES, LANES), 1)
    dst_slot = dst // strip
    dst_channel = dst_slot // members if members <= slots else jnp.zeros_like(dst)
    low = lane < half
    slot_of = (lane % half) // strip

    def body(step, carry):
        group = start // per + step
        first = group * per
        expand = src == ((first + dst_channel) % slots) * strip + dst % strip
        expand = expand.astype(F32).astype(BF16)
        grid_left = dot(grid_left_ref[first // slots], expand)
        grid_right = dot(grid_right_ref[first // slots], expand)
        grids = [grid_ref[first + c].astype(F32) for c in range(per)]
        outs = [[None] * 3 for _ in range(per)]
        for h in range(max(1, members // slots)):
            left = left_ref[h, group].astype(F32) * grid_left
            right = right_ref[h, group].astype(F32) * grid_right
            sides = (
                split(jnp.where(low, left, pltpu.roll(right, half, 1))),
                split(jnp.where(low, pltpu.roll(left, half, 1), right)),
            )
            parts = ([], [])
            where = []
            for k in range(slots):
                c, m = (k // members, k % members) if members <= slots else (0, h * slots + k)
                where.append((c, m))
                mine = split(own_ref[m, first + c].astype(F32) * grids[c])
                side = sides[k * 2 // slots]
                keep = slot_of == k % (slots // 2)
                for p in range(2):
                    edge = jnp.where(keep, side[p], jnp.zeros_like(side[p]))
                    parts[p].append(jnp.concatenate([mine[p], edge], axis=1))
            big = dot(jnp.concatenate(parts[0], axis=0), lon_both)
            small = dot(jnp.concatenate(parts[1], axis=0), lon_hi)
            smoothed = big[:, :cols] + big[:, cols:] + small
            hi, lo = split(smoothed)
            stack = []
            for k in range(slots):
                a, b = hi[k * rows : (k + 1) * rows], lo[k * rows : (k + 1) * rows]
                stack.append(jnp.concatenate([a, a, b], axis=0))
            spread = dot(lat, jnp.concatenate(stack, axis=1))
            for k, (c, m) in enumerate(where):
                for r, ref in enumerate((up_ref, own_ref, down_ref)):
                    piece = spread[r * rows : (r + 1) * rows, k * cols : (k + 1) * cols]
                    term = piece * ref[m, first + c].astype(F32)
                    outs[c][r] = term if outs[c][r] is None else outs[c][r] + term
        for c in range(per):
            at = step * per + c
            out_up_ref[at] = outs[c][0]
            out_ref[at] = outs[c][1]
            out_down_ref[at] = outs[c][2]
        return carry

    lax.fori_loop(0, count // per, body, 0)


def whole(n):
    return [pl.BlockSpec(memory_space=pltpu.VMEM)] * n


def local(chunks, grad_tokens, token_index, members, lat_taps, lon_taps):
    ens, lat_count, lon_count = (lax.axis_size(a) for a in ("ens", "lat", "lon"))
    ens_pos, lat_pos, lon_pos = (lax.axis_index(a) for a in ("ens", "lat", "lon"))
    channels, cells = grad_tokens.shape
    rows, cols = token_index.shape
    own_channels = channels // ens
    blocks = lat_count * lon_count
    piece = cells // blocks
    strip = lon_taps.shape[0] - 1
    slots = LANES // strip
    assert cols == LANES and lat_taps.shape[0] - 1 <= rows

    tokens = lax.dynamic_slice_in_dim(grad_tokens, ens_pos * own_channels, own_channels, 0)
    tokens = tokens.reshape(own_channels, blocks, piece).transpose(1, 0, 2)
    moved = lax.all_to_all(tokens, ("lat", "lon"), split_axis=0, concat_axis=0, tiled=True)
    if piece != LANES:
        moved = moved.transpose(1, 0, 2).reshape(own_channels, cells // LANES, LANES).transpose(1, 0, 2)
    block_id = lat_pos * lon_count + lon_pos
    offset = (token_index // cells) * piece + token_index % cells - block_id * piece

    if ens == 2:
        given = lax.dynamic_slice_in_dim(members, (1 - ens_pos) * own_channels, own_channels, 1)
        kept = lax.dynamic_slice_in_dim(members, ens_pos * own_channels, own_channels, 1)
        taken = lax.ppermute(given, "ens", [(0, 1), (1, 0)])
        w = jnp.concatenate([kept, taken], axis=0)
    else:
        w = lax.all_to_all(members, "ens", split_axis=1, concat_axis=0, tiled=True)
    count = w.shape[0]
    per = max(1, slots // count)
    parts = max(1, count // slots)

    to_down = [(i, i + 1) for i in range(lat_count - 1)]
    to_up = [(i + 1, i) for i in range(lat_count - 1)]
    to_right = [(i, (i + 1) % lon_count) for i in range(lon_count)]
    to_left = [((i + 1) % lon_count, i) for i in range(lon_count)]
    w_up = lax.ppermute(w, "lat", to_down)
    w_down = lax.ppermute(w, "lat", to_up)

    strips = jax.ShapeDtypeStruct((parts, own_channels // per, rows, LANES), BF16)
    w_first, w_last = pl.pallas_call(
        functools.partial(pack_kernel, strip, slots),
        out_shape=(strips, strips), in_specs=whole(1), out_specs=whole(2), name="pack",
    )(w)
    w_left = lax.ppermute(w_last, "lon", to_right)
    w_right = lax.ppermute(w_first, "lon", to_left)

    lon_both = lon_matrix(lon_taps, cols, strip)
    lat = lat_matrix(lat_taps, rows, lat_pos, lat_count)

    padded = -(-own_channels // slots) * slots
    edges = jax.ShapeDtypeStruct((padded // slots, rows, LANES), BF16)
    grid, g_first, g_last = pl.pallas_call(
        functools.partial(gather_kernel, strip, slots),
        out_shape=(jax.ShapeDtypeStruct((own_channels, rows, cols), BF16), edges, edges),
        in_specs=whole(2), out_specs=whole(3),
        scratch_shapes=[pltpu.VMEM((padded, rows, cols), F32)], name="gather",
    )(moved, offset)
    g_left = lax.ppermute(g_last, "lon", to_right)
    g_right = lax.ppermute(g_first, "lon", to_left)

    chunks = chunks if own_channels % (chunks * per) == 0 else 1
    size = own_channels // chunks
    block = jax.ShapeDtypeStruct((size, rows, cols), F32)
    outs = []
    for n in range(chunks):
        own, up, down = pl.pallas_call(
            functools.partial(smooth_kernel, strip, slots, n * size, size),
            out_shape=(block,) * 3, in_specs=whole(10), out_specs=whole(3), name=f"smooth{n}",
        )(w, w_up, w_down, w_left, w_right, grid, g_left, g_right, lon_both, lat)
        from_up = lax.ppermute(down, "lat", to_down)
        from_down = lax.ppermute(up, "lat", to_up)
        outs.append((own + from_up + from_down) / (count - 1))
    return jnp.concatenate(outs, axis=0) if chunks > 1 else outs[0]


def solution(mesh):
    in_specs = (P(None, ("lat", "lon")), P("lat", "lon"), P("ens", None, "lat", "lon"), P(), P())
    out_specs = P("ens", "lat", "lon")
    return jax.shard_map(
        functools.partial(local, 2), mesh=mesh, in_specs=in_specs, out_specs=out_specs, check_vma=False
    )
```

time: 192 us -> 142 us (0.74)
  waiting for transfers between devices: 97.4 us -> 7.3 us
  other arithmetic: 2.32 us -> 69.6 us
  local copies, waits for them, and re-layouts: 37.2 us -> 6.17 us
  Pallas kernels: 0 us -> 25 us
  matrix products: 20.4 us -> 0 us
  between operations: 13.6 us -> 0.3 us
  starting transfers between devices: 20.2 us -> 31.7 us
    ppermute x8 -> x11, waiting for transfers between devices: 78.8 us -> 7.3 us  [the longest x1 2.59 us: local(): w_left = lax.ppermute(w_last, 'lon', to_right)]
    convert_element_type x1 -> x3, other arithmetic: 0.06 us -> 42.2 us  [split_outside(): return (hi.astype(BF16), (v - hi).astype(BF16))]
    pallas_call x0 -> x4, Pallas kernels: none -> 25 us  [the longest x2 18.8 us: local(): pl.pallas_call(functools.partial(smooth_kernel, strip, slots, n * size, s...]
    dot_general x8 -> x0, matrix products: 20.4 us -> none  [the longest x2 11.5 us: localize(): jnp.einsum('mciu,uj->mcij', widened, lon_matrix, precision=lax.Precision....]
    slice x8 -> x1, local copies, waits for them, and re-layouts: 15.5 us -> 0.71 us  [band(): total = total + jnp.where(offset == k, taps[k], 0.0)]
    all_to_all x1, waiting for transfers between devices: 13 us -> 0.01 us  [local(): lax.all_to_all(tokens, ('lat', 'lon'), split_axis=0, concat_axis=0, tiled...]
    ppermute x8 -> x11, starting transfers between devices: 11.8 us -> 23.9 us  [the longest x2 9.45 us: local(): from_up = lax.ppermute(down, 'lat', to_down)]
    ppermute x4 -> x0, local copies, waits for them, and re-layouts: 10.9 us -> none  [the longest x2 5.46 us: with_halo(): before = lax.ppermute(last, axis, up)]
  transfers between devices with their start and end apart: 10 -> 12, of which waited for: 8 -> 4; matrix products, arithmetic and copies ran while one was open for 5% -> 50% of each run, Pallas kernels for 0% -> 11%
where the time goes in v1:
time: 142 us; the launch traced here: 140 us
  other arithmetic  69.6 us (49%)
  starting transfers between devices  31.7 us (22%)
  Pallas kernels  25 us (18%)
  waiting for transfers between devices  7.3 us (5%)
  local copies, waits for them, and re-layouts  6.17 us (4%)
    convert_element_type x3, other arithmetic, split_outside(): return (hi.astype(BF16), (v - hi).astype(BF16))  42.2 us
    pallas_call x2, Pallas kernels, local(): pl.pallas_call(functools.partial(smooth_kernel, strip, slots, n * size, s...  18.8 us
    add x1, other arithmetic, band(): total = total + jnp.where(offset == k, taps[k], 0.0)  10.6 us
    select_n x1, other arithmetic, lat_matrix(): gather = jnp.where(inside[:, None], gather, 0.0)  10.6 us
    ppermute x2, starting transfers between devices, local(): from_up = lax.ppermute(down, 'lat', to_down)  9.45 us
    all_to_all x1, starting transfers between devices, local(): lax.all_to_all(tokens, ('lat', 'lon'), split_axis=0, concat_axis=0, tiled...  7.88 us
    ppermute x1, starting transfers between devices, local(): w_up = lax.ppermute(w, 'lat', to_down)  4.01 us
    pallas_call x1, Pallas kernels, local(): pl.pallas_call(functools.partial(gather_kernel, strip, slots), out_shape=...  3.83 us
  transfers between devices with their start and end apart: 12, of which 4 were waited for; matrix products, arithmetic and copies ran while one was open for 50% of the time, Pallas kernels for 11%

profile of v1, /device:TPU:0, one launch (start us, length us, event | category | flops | bytes accessed | tf_op | source)
XLA Modules:
  0.0 140.2 jit_solution(10966089167161024957)
XLA Ops:
  0.0 1.3 constant_dynamic-slice_fusion.2
  2.0 0.7 copy.16
  2.8 7.9 %all-to-all-start = ((bf16[16,52,128]{2,1,0:T(8,128)(2,1)}), bf16[16,52,128]{2,1,0:T(8,128)(2,1)S(1)}, u32[]{:S(2)}, u32[]{:S(2)}) async-start(bf16[16,52,128]{2,1,0:T(8,128)(2,1)} %bitcast.22), calls=%async_computation | async-start | bytes 458752 | tf_op jit(solution)/shard_map/all_to_all | solution.py:208
  11.3 0.7 fusion.76
  12.1 10.6 %add_select_fusion = f32[32,16]{1,0:T(8,128)S(1)} fusion(f32[]{:T(128)} %bitcast.1, f32[]{:T(128)} %bitcast.2, f32[]{:T(128)} %bitcast.3, f32[]{:T(128)} %bitcast.4, f32[]{:T(128)} %bitcast.5, f32[]{:T(128)} %bitcast.6, f32[]{:T(128)} %bitcast.7, f32[]{:T(128)} %bitcast.8, f32[]{:T(128)} %bitcast.9, f32[]{:T(128)} %bitcast.10, f32[]{:T(128)} %bitcast.11, ...), kind=kLoop, calls=%fused_computation.46 | loop fusion | flops 27136 | bytes 2276 | tf_op jit(solution)/shard_map/jit(_where)/select_n | solution.py:65
  22.7 10.6 %select_add_fusion.1 = f32[48,32]{0,1:T(8,128)S(1)} fusion(f32[]{:T(128)} %bitcast.17, f32[]{:T(128)} %bitcast.16, f32[]{:T(128)} %bitcast.15, f32[]{:T(128)} %bitcast.14, f32[]{:T(128)} %bitcast.13, f32[]{:T(128)} %bitcast.12, f32[]{:T(128)} %bitcast.11, f32[]{:T(128)} %bitcast.10, f32[]{:T(128)} %bitcast.9, f32[]{:T(128)} %bitcast.8, f32[]{:T(128)} %bitcast.7, ...), kind=kLoop, calls=%fused_computation.65 | loop fusion | flops 79872 | bytes 6532 | tf_op jit(solution)/shard_map/add | solution.py:32
  34.2 0.8 multiply_reduce_fusion.32
  34.9 0.8 multiply_reduce_fusion.31
  35.7 0.7 multiply_reduce_fusion.30
  36.5 0.8 multiply_reduce_fusion.33
  37.3 21.1 %fusion = bf16[256,128]{1,0:T(8,128)(2,1)S(1)} fusion(f32[]{:T(128)} %get-tuple-element.58, f32[]{:T(128)} %get-tuple-element.59, f32[]{:T(128)} %get-tuple-element.42, f32[]{:T(128)} %get-tuple-element.57, f32[]{:T(128)} %get-tuple-element.28, f32[]{:T(128)} %get-tuple-element.29, f32[]{:T(128)} %get-tuple-element.30, f32[]{:T(128)} %get-tuple-element.31, ...), kind=kLoop, calls=%fused_computation.8 | loop fusion | flops 3375104 | bytes 66692 | tf_op jit(solution)/shard_map/convert_element_type | solution.py:26
  58.5 4.0 %collective-permute-start.1 = (bf16[4,52,16,128]{3,2,1,0:T(8,128)(2,1)S(1)}, bf16[4,52,16,128]{3,2,1,0:T(8,128)(2,1)S(1)}, u32[]{:S(2)}, u32[]{:S(2)}) collective-permute-start(bf16[4,52,16,128]{3,2,1,0:T(8,128)(2,1)S(1)} %pad_maximum_fusion.w_ref.own_ref), channel_id=1, source_target_pairs={{0,4},{4,8},{8,12},{1,5},{5,9},{9,13},{2,6},{6,10},{10,14},{3,7},{... | collective-permute-start | bytes 2555912 | tf_op jit(solution)/shard_map/ppermute | solution.py:229
  62.6 1.3 collective-permute-start.2
  63.9 21.1 %reduce-precision_convert_fusion = bf16[256,128]{1,0:T(8,128)(2,1)S(1)} fusion(f32[]{:T(128)} %get-tuple-element.58, f32[]{:T(128)} %get-tuple-element.59, f32[]{:T(128)} %get-tuple-element.42, f32[]{:T(128)} %get-tuple-element.57, f32[]{:T(128)} %get-tuple-element.28, f32[]{:T(128)} %get-tuple-element.29, f32[]{:T(128)} %get-tuple-element.30, ...), kind=kLoop, calls=%fused_computation.7 | loop fusion | flops 3342336 | bytes 66692 | tf_op jit(solution)/shard_map/convert_element_type | solution.py:26
  85.6 0.7 copy-done.4
  86.3 3.8 %gather.1 = (bf16[52,16,128]{2,1,0:T(8,128)(2,1)}, bf16[7,16,128]{2,1,0:T(8,128)(2,1)}, bf16[7,16,128]{2,1,0:T(8,128)(2,1)}) custom-call(bf16[16,52,128]{2,1,0:T(8,128)(2,1)} %copy-done.4, s32[16,128]{1,0:T(8,128)} %fusion.70.offset_ref), custom_call_target="tpu_custom_call" | custom-call | tf_op jit(solution)/shard_map/gather/pallas_call | solution.py:245
  90.1 1.5 %collective-permute-start.5 = (bf16[7,16,128]{2,1,0:T(8,128)(2,1)}, bf16[7,16,128]{2,1,0:T(8,128)(2,1)S(1)}, u32[]{:S(2)}, u32[]{:S(2)}) collective-permute-start(bf16[7,16,128]{2,1,0:T(8,128)(2,1)} %get-tuple-element.19), channel_id=1, source_target_pairs={{0,1},{1,2},{2,3},{3,0},{4,5},{5,6},{6,7},{7,4},{8,9},{9,10},{10,1... | collective-permute-start | bytes 86024 | tf_op jit(solution)/shard_map/ppermute | solution.py:251
  92.3 1.5 %collective-permute-start.6 = (bf16[7,16,128]{2,1,0:T(8,128)(2,1)S(1)}, bf16[7,16,128]{2,1,0:T(8,128)(2,1)S(1)}, u32[]{:S(2)}, u32[]{:S(2)}) collective-permute-start(bf16[7,16,128]{2,1,0:T(8,128)(2,1)S(1)} %copy-done.14), channel_id=1, source_target_pairs={{1,0},{2,1},{3,2},{0,3},{5,4},{6,5},{7,6},{4,7},{9,8},{10,9},{11,1... | collective-permute-start | bytes 86024 | tf_op jit(solution)/shard_map/ppermute | solution.py:252
  93.7 2.4 %pack.1 = (bf16[1,26,16,128]{3,2,1,0:T(8,128)(2,1)}, bf16[1,26,16,128]{3,2,1,0:T(8,128)(2,1)}) custom-call(bf16[4,52,16,128]{3,2,1,0:T(8,128)(2,1)} %copy-done.1), custom_call_target="tpu_custom_call" | custom-call | tf_op jit(solution)/shard_map/pack/pallas_call | solution.py:233
  96.7 2.4 %collective-permute-start.4 = (bf16[1,26,16,128]{3,2,1,0:T(8,128)(2,1)}, bf16[1,26,16,128]{3,2,1,0:T(8,128)(2,1)S(1)}, u32[]{:S(2)}, u32[]{:S(2)}) collective-permute-start(bf16[1,26,16,128]{3,2,1,0:T(8,128)(2,1)} %get-tuple-element.17), channel_id=1, source_target_pairs={{1,0},{2,1},{3,2},{0,3},{5,4},{6,5},{7,6},{4,7},{9,8},{10,9},{11,1... | collective-permute-start | bytes 319496 | tf_op jit(solution)/shard_map/ppermute | solution.py:238
  99.1 0.7 pad_maximum_fusion.3.lat_ref
  99.8 2.6 %collective-permute-done.3.left_ref = bf16[1,26,16,128]{3,2,1,0:T(8,128)(2,1)S(1)} collective-permute-done((bf16[1,26,16,128]{3,2,1,0:T(8,128)(2,1)}, bf16[1,26,16,128]{3,2,1,0:T(8,128)(2,1)S(1)}, u32[]{:S(2)}, u32[]{:S(2)}) %collective-permute-start.3) | collective-permute-done | bytes 106528 | tf_op jit(solution)/shard_map/ppermute | solution.py:237
  102.3 1.1 collective-permute-done.4.right_ref
  104.7 9.4 %smooth0.1 = (f32[26,16,128]{2,1,0:T(8,128)}, f32[26,16,128]{2,1,0:T(8,128)}, f32[26,16,128]{2,1,0:T(8,128)}) custom-call(bf16[4,52,16,128]{3,2,1,0:T(8,128)(2,1)} %copy-done.1, bf16[4,52,16,128]{3,2,1,0:T(8,128)(2,1)} %copy-done.2, bf16[4,52,16,128]{3,2,1,0:T(8,128)(2,1)} %copy-done.3, bf16[1,26,16,128]{3,2,1,0:T(8,128)(2,1)} %copy-done.5, ...), custom_call_target="tpu_custom_call" | custom-call | tf_op jit(solution)/shard_map/smooth0/pallas_call | solution.py:259
  114.1 4.3 %collective-permute-start.7 = (f32[26,16,128]{2,1,0:T(8,128)}, f32[26,16,128]{2,1,0:T(8,128)S(1)}, u32[]{:S(2)}, u32[]{:S(2)}) collective-permute-start(f32[26,16,128]{2,1,0:T(8,128)} %get-tuple-element.22), channel_id=1, source_target_pairs={{0,4},{4,8},{8,12},{1,5},{5,9},{9,13},{2,6},{6,10},{10,14},{3,7},{... | collective-permute-start | bytes 638984 | tf_op jit(solution)/shard_map/ppermute | solution.py:263
  118.4 1.4 %collective-permute-start.8 = (f32[26,16,128]{2,1,0:T(8,128)}, f32[26,16,128]{2,1,0:T(8,128)S(1)}, u32[]{:S(2)}, u32[]{:S(2)}) collective-permute-start(f32[26,16,128]{2,1,0:T(8,128)} %get-tuple-element.23), channel_id=1, source_target_pairs={{4,0},{8,4},{12,8},{5,1},{9,5},{13,9},{6,2},{10,6},{14,10},{7,3},{... | collective-permute-start | bytes 638984 | tf_op jit(solution)/shard_map/ppermute | solution.py:264
  119.8 9.4 %smooth1.1 = (f32[26,16,128]{2,1,0:T(8,128)}, f32[26,16,128]{2,1,0:T(8,128)}, f32[26,16,128]{2,1,0:T(8,128)}) custom-call(bf16[4,52,16,128]{3,2,1,0:T(8,128)(2,1)} %copy-done.1, bf16[4,52,16,128]{3,2,1,0:T(8,128)(2,1)} %copy-done.2, bf16[4,52,16,128]{3,2,1,0:T(8,128)(2,1)} %copy-done.3, bf16[1,26,16,128]{3,2,1,0:T(8,128)(2,1)} %copy-done.5, ...), custom_call_target="tpu_custom_call" | custom-call | tf_op jit(solution)/shard_map/smooth1/pallas_call | solution.py:259
  129.2 1.3 collective-permute-start.10
  130.5 5.2 %collective-permute-start.9 = (f32[26,16,128]{2,1,0:T(8,128)}, f32[26,16,128]{2,1,0:T(8,128)S(1)}, u32[]{:S(2)}, u32[]{:S(2)}) collective-permute-start(f32[26,16,128]{2,1,0:T(8,128)} %get-tuple-element.25), channel_id=1, source_target_pairs={{0,4},{4,8},{8,12},{1,5},{5,9},{9,13},{2,6},{6,10},{10,14},{3,7},{... | collective-permute-start | bytes 638984 | tf_op jit(solution)/shard_map/ppermute | solution.py:263
  135.8 2.0 %collective-permute-done.10 = f32[26,16,128]{2,1,0:T(8,128)S(1)} collective-permute-done((f32[26,16,128]{2,1,0:T(8,128)}, f32[26,16,128]{2,1,0:T(8,128)S(1)}, u32[]{:S(2)}, u32[]{:S(2)}) %collective-permute-start.10) | collective-permute-done | bytes 213024 | tf_op jit(solution)/shard_map/ppermute | solution.py:264
  137.8 1.6 %collective-permute-done.9 = f32[26,16,128]{2,1,0:T(8,128)S(1)} collective-permute-done((f32[26,16,128]{2,1,0:T(8,128)}, f32[26,16,128]{2,1,0:T(8,128)S(1)}, u32[]{:S(2)}, u32[]{:S(2)}) %collective-permute-start.9) | collective-permute-done | bytes 213024 | tf_op jit(solution)/shard_map/ppermute | solution.py:263
  139.4 0.8 pad_maximum_fusion.1
  (56 shorter events, 5.5 us)
Async XLA Ops:
  0.0 1.9 %copy-start = (bf16[104,2048]{1,0:T(8,128)(2,1)S(1)}, bf16[104,2048]{1,0:T(8,128)(2,1)}, u32[]{:S(2)}) copy-start(bf16[104,2048]{1,0:T(8,128)(2,1)} %param.5) | copy-start | bytes 1277956
  1.3 57.1 %collective-permute-start = (bf16[2,52,16,128]{3,2,1,0:T(8,128)(2,1)S(1)}, bf16[2,52,16,128]{3,2,1,0:T(8,128)(2,1)S(1)}, u32[]{:S(2)}, u32[]{:S(2)}) collective-permute-start(bf16[2,52,16,128]{3,2,1,0:T(8,128)(2,1)S(1)} %get-tuple-element.61), channel_id=1, source_target_pairs={{0,16},{16,0},{1,17},{17,1},{2,18},{18,2},{3,19},{19,3},{4,20},{20... | collective-permute-start | bytes 1277960 | tf_op jit(solution)/shard_map/ppermute | solution.py:217
  2.8 82.8 %all-to-all-start = ((bf16[16,52,128]{2,1,0:T(8,128)(2,1)}), bf16[16,52,128]{2,1,0:T(8,128)(2,1)S(1)}, u32[]{:S(2)}, u32[]{:S(2)}) async-start(bf16[16,52,128]{2,1,0:T(8,128)(2,1)} %bitcast.22), calls=%async_computation | async-start | bytes 458752 | tf_op jit(solution)/shard_map/all_to_all | solution.py:208
  10.7 0.7 copy-start.9
  33.5 0.7 copy-start.13
  58.5 35.2 %copy-start.1 = (bf16[4,52,16,128]{3,2,1,0:T(8,128)(2,1)}, bf16[4,52,16,128]{3,2,1,0:T(8,128)(2,1)S(1)}, u32[]{:S(2)}) copy-start(bf16[4,52,16,128]{3,2,1,0:T(8,128)(2,1)S(1)} %pad_maximum_fusion.w_ref.own_ref) | copy-start | bytes 2555908
  58.5 26.4 %copy-start.12 = (s32[16,128]{1,0:T(8,128)S(1)}, s32[16,128]{1,0:T(8,128)}, u32[]{:S(2)}) copy-start(s32[16,128]{1,0:T(8,128)} %param.6) | copy-start | bytes 24580
  58.5 45.0 %collective-permute-start.1 = (bf16[4,52,16,128]{3,2,1,0:T(8,128)(2,1)S(1)}, bf16[4,52,16,128]{3,2,1,0:T(8,128)(2,1)S(1)}, u32[]{:S(2)}, u32[]{:S(2)}) collective-permute-start(bf16[4,52,16,128]{3,2,1,0:T(8,128)(2,1)S(1)} %pad_maximum_fusion.w_ref.own_ref), channel_id=1, source_target_pairs={{0,4},{4,8},{8,12},{1,5},{5,9},{9,13},{2,6},{6,10},{10,14},{3,7},{... | collective-permute-start | bytes 2555912 | tf_op jit(solution)/shard_map/ppermute | solution.py:229
  62.6 40.9 %collective-permute-start.2 = (bf16[4,52,16,128]{3,2,1,0:T(8,128)(2,1)S(1)}, bf16[4,52,16,128]{3,2,1,0:T(8,128)(2,1)S(1)}, u32[]{:S(2)}, u32[]{:S(2)}) collective-permute-start(bf16[4,52,16,128]{3,2,1,0:T(8,128)(2,1)S(1)} %pad_maximum_fusion.w_ref.own_ref), channel_id=1, source_target_pairs={{4,0},{8,4},{12,8},{5,1},{9,5},{13,9},{6,2},{10,6},{14,10},{7,3},{... | collective-permute-start | bytes 2555912 | tf_op jit(solution)/shard_map/ppermute | solution.py:230
  85.6 0.7 copy-start.4
  90.1 2.1 %copy-start.14 = (bf16[7,16,128]{2,1,0:T(8,128)(2,1)S(1)}, bf16[7,16,128]{2,1,0:T(8,128)(2,1)}, u32[]{:S(2)}) copy-start(bf16[7,16,128]{2,1,0:T(8,128)(2,1)} %get-tuple-element.20) | copy-start | bytes 86020
  90.1 6.6 %collective-permute-start.5 = (bf16[7,16,128]{2,1,0:T(8,128)(2,1)}, bf16[7,16,128]{2,1,0:T(8,128)(2,1)S(1)}, u32[]{:S(2)}, u32[]{:S(2)}) collective-permute-start(bf16[7,16,128]{2,1,0:T(8,128)(2,1)} %get-tuple-element.19), channel_id=1, source_target_pairs={{0,1},{1,2},{2,3},{3,0},{4,5},{5,6},{6,7},{7,4},{8,9},{9,10},{10,1... | collective-permute-start | bytes 86024 | tf_op jit(solution)/shard_map/ppermute | solution.py:251
  92.3 7.5 %collective-permute-start.6 = (bf16[7,16,128]{2,1,0:T(8,128)(2,1)S(1)}, bf16[7,16,128]{2,1,0:T(8,128)(2,1)S(1)}, u32[]{:S(2)}, u32[]{:S(2)}) collective-permute-start(bf16[7,16,128]{2,1,0:T(8,128)(2,1)S(1)} %copy-done.14), channel_id=1, source_target_pairs={{1,0},{2,1},{3,2},{0,3},{5,4},{6,5},{7,6},{4,7},{9,8},{10,9},{11,1... | collective-permute-start | bytes 86024 | tf_op jit(solution)/shard_map/ppermute | solution.py:252
  96.1 6.2 %collective-permute-start.3 = (bf16[1,26,16,128]{3,2,1,0:T(8,128)(2,1)}, bf16[1,26,16,128]{3,2,1,0:T(8,128)(2,1)S(1)}, u32[]{:S(2)}, u32[]{:S(2)}) collective-permute-start(bf16[1,26,16,128]{3,2,1,0:T(8,128)(2,1)} %get-tuple-element.16), channel_id=1, source_target_pairs={{0,1},{1,2},{2,3},{3,0},{4,5},{5,6},{6,7},{7,4},{8,9},{9,10},{10,1... | collective-permute-start | bytes 319496 | tf_op jit(solution)/shard_map/ppermute | solution.py:237
  96.7 6.8 %copy-start.10 = (bf16[7,16,128]{2,1,0:T(8,128)(2,1)}, bf16[7,16,128]{2,1,0:T(8,128)(2,1)S(1)}, u32[]{:S(2)}) copy-start(bf16[7,16,128]{2,1,0:T(8,128)(2,1)S(1)} %collective-permute-done.5.grid_left_ref) | copy-start | bytes 86020
  96.7 6.8 %collective-permute-start.4 = (bf16[1,26,16,128]{3,2,1,0:T(8,128)(2,1)}, bf16[1,26,16,128]{3,2,1,0:T(8,128)(2,1)S(1)}, u32[]{:S(2)}, u32[]{:S(2)}) collective-permute-start(bf16[1,26,16,128]{3,2,1,0:T(8,128)(2,1)} %get-tuple-element.17), channel_id=1, source_target_pairs={{1,0},{2,1},{3,2},{0,3},{5,4},{6,5},{7,6},{4,7},{9,8},{10,9},{11,1... | collective-permute-start | bytes 319496 | tf_op jit(solution)/shard_map/ppermute | solution.py:238
  99.8 3.8 %copy-start.11 = (bf16[7,16,128]{2,1,0:T(8,128)(2,1)}, bf16[7,16,128]{2,1,0:T(8,128)(2,1)S(1)}, u32[]{:S(2)}) copy-start(bf16[7,16,128]{2,1,0:T(8,128)(2,1)S(1)} %collective-permute-done.6.grid_right_ref) | copy-start | bytes 86020
  102.3 1.2 copy-start.5
  103.5 0.6 copy-start.6
  103.5 1.0 copy-start.2
  103.5 1.2 copy-start.3
  114.1 21.6 %collective-permute-start.7 = (f32[26,16,128]{2,1,0:T(8,128)}, f32[26,16,128]{2,1,0:T(8,128)S(1)}, u32[]{:S(2)}, u32[]{:S(2)}) collective-permute-start(f32[26,16,128]{2,1,0:T(8,128)} %get-tuple-element.22), channel_id=1, source_target_pairs={{0,4},{4,8},{8,12},{1,5},{5,9},{9,13},{2,6},{6,10},{10,14},{3,7},{... | collective-permute-start | bytes 638984 | tf_op jit(solution)/shard_map/ppermute | solution.py:263
  118.4 17.3 %copy-start.8 = (f32[26,16,128]{2,1,0:T(8,128)S(1)}, f32[26,16,128]{2,1,0:T(8,128)}, u32[]{:S(2)}) copy-start(f32[26,16,128]{2,1,0:T(8,128)} %get-tuple-element.21) | copy-start | bytes 638980
  118.4 17.3 %collective-permute-start.8 = (f32[26,16,128]{2,1,0:T(8,128)}, f32[26,16,128]{2,1,0:T(8,128)S(1)}, u32[]{:S(2)}, u32[]{:S(2)}) collective-permute-start(f32[26,16,128]{2,1,0:T(8,128)} %get-tuple-element.23), channel_id=1, source_target_pairs={{4,0},{8,4},{12,8},{5,1},{9,5},{13,9},{6,2},{10,6},{14,10},{7,3},{... | collective-permute-start | bytes 638984 | tf_op jit(solution)/shard_map/ppermute | solution.py:264
  129.2 8.6 %collective-permute-start.10 = (f32[26,16,128]{2,1,0:T(8,128)}, f32[26,16,128]{2,1,0:T(8,128)S(1)}, u32[]{:S(2)}, u32[]{:S(2)}) collective-permute-start(f32[26,16,128]{2,1,0:T(8,128)} %get-tuple-element.26), channel_id=1, source_target_pairs={{4,0},{8,4},{12,8},{5,1},{9,5},{13,9},{6,2},{10,6},{14,10},{7,3},{... | collective-permute-start | bytes 638984 | tf_op jit(solution)/shard_map/ppermute | solution.py:264
  130.5 8.8 %collective-permute-start.9 = (f32[26,16,128]{2,1,0:T(8,128)}, f32[26,16,128]{2,1,0:T(8,128)S(1)}, u32[]{:S(2)}, u32[]{:S(2)}) collective-permute-start(f32[26,16,128]{2,1,0:T(8,128)} %get-tuple-element.25), channel_id=1, source_target_pairs={{0,4},{4,8},{8,12},{1,5},{5,9},{9,13},{2,6},{6,10},{10,14},{3,7},{... | collective-permute-start | bytes 638984 | tf_op jit(solution)/shard_map/ppermute | solution.py:263
  135.7 3.6 %copy-start.7 = (f32[26,16,128]{2,1,0:T(8,128)S(1)}, f32[26,16,128]{2,1,0:T(8,128)}, u32[]{:S(2)}) copy-start(f32[26,16,128]{2,1,0:T(8,128)} %get-tuple-element.24) | copy-start | bytes 638980

commit v2 on v1

v2 whole, which is shorter than its diff:
```python
import functools

import jax
import jax.numpy as jnp
from jax import lax
from jax.experimental import pallas as pl
from jax.experimental.pallas import tpu as pltpu
from jax.sharding import PartitionSpec as P

LANES = 128
F32 = jnp.float32
BF16 = jnp.bfloat16
UNIT = 7
GRANT = 24 << 20


def dot(a, b):
    return lax.dot_general(a, b, (((1,), (0,)), ((), ())), preferred_element_type=F32)


def split(v):
    hi = v.astype(BF16)
    return hi, (v - hi.astype(F32)).astype(BF16)


def band(taps, offset):
    total = jnp.zeros(offset.shape, F32)
    for k, tap in enumerate(taps):
        total = jnp.where(offset == k, tap, total)
    return total


def matrix_kernel(strip, lat_count, lat_taps_ref, lon_taps_ref, lon_ref, lat_ref):
    cols, rows = lon_ref.shape[1] // 2, lat_ref.shape[0] // 3
    count = lon_taps_ref.shape[0]
    iota = lax.broadcasted_iota
    taps = [lon_taps_ref[k] for k in range(count)]
    half = [sum(taps[a] * taps[a - d] for a in range(d, count)) for d in range(count)]
    both = half[:0:-1] + half
    place = iota(jnp.int32, (2 * LANES, cols), 0)
    inner = place % strip
    source = jnp.where(
        place < cols, place, jnp.where(place < cols + LANES // 2, inner - strip, cols + inner)
    )
    hi, lo = split(band(both, source - iota(jnp.int32, (2 * LANES, cols), 1) + count - 1))
    lon_ref[...] = jnp.concatenate([hi, lo], axis=1)
    count = lat_taps_ref.shape[0]
    radius = (count - 1) // 2
    taps = [lat_taps_ref[k] for k in range(count)]
    middle = rows + 2 * radius
    out_row = iota(jnp.int32, (3 * rows, middle), 0) - rows
    mid_row = iota(jnp.int32, (3 * rows, middle), 1) - radius
    spread = band(taps, mid_row - out_row + radius)
    mid_row = iota(jnp.int32, (middle, rows), 0) - radius
    gather = band(taps[::-1], iota(jnp.int32, (middle, rows), 1) - mid_row + radius)
    whole_row = lax.axis_index("lat") * rows + mid_row
    gather = jnp.where((whole_row >= 0) & (whole_row < lat_count * rows), gather, 0.0)
    hi, lo = split(jnp.dot(spread, gather, precision=lax.Precision.HIGHEST, preferred_element_type=F32))
    lat_ref[...] = jnp.concatenate([hi, lo, hi], axis=1)


def pick_matrix(slot, strip, cols):
    lane = lax.broadcasted_iota(jnp.int32, (cols, LANES), 1)
    row = lax.broadcasted_iota(jnp.int32, (cols, LANES), 0)
    here = lane // strip == slot
    first = here & (row == lane % strip)
    last = here & (row == cols - strip + lane % strip)
    one = jnp.concatenate([first.astype(F32), last.astype(F32)], axis=1)
    return one.astype(BF16)


def pack_kernel(strip, slots, w_ref, first_ref, last_ref):
    members, channels, rows, cols = w_ref.shape
    per = max(1, slots // members)
    for h in range(max(1, members // slots)):
        total = None
        for k in range(slots):
            c2, m = (k // members, k % members) if members <= slots else (0, h * slots + k)
            plane = w_ref[m].reshape(channels // per, per, rows, cols)[:, c2]
            part = dot(plane.reshape(-1, cols), pick_matrix(k, strip, cols))
            total = part if total is None else total + part
        total = total.astype(BF16)
        first_ref[h] = total[:, :LANES].reshape(channels // per, rows, LANES)
        last_ref[h] = total[:, LANES:].reshape(channels // per, rows, LANES)


def gather_kernel(strip, slots, moved_ref, offset_ref, grid_ref, first_ref, last_ref, scratch):
    pieces, channels, width = moved_ref.shape
    rows, cols = offset_ref.shape
    scratch[channels:] = jnp.zeros((scratch.shape[0] - channels, rows, cols), F32)
    tokens = jnp.concatenate([moved_ref[n] for n in range(pieces)], axis=1)
    token = lax.broadcasted_iota(jnp.int32, (pieces * width, 2 * cols), 0)
    for i in range(0, rows, 2):
        wanted = jnp.concatenate([offset_ref[i : i + 1], offset_ref[i + 1 : i + 2]], axis=1)
        chosen = jnp.where(token == wanted, 1.0, 0.0).astype(BF16)
        found = dot(tokens, chosen)
        scratch[:channels, i, :] = found[:, :cols]
        scratch[:channels, i + 1, :] = found[:, cols:]
    grid = scratch[...].astype(BF16)
    grid_ref[...] = grid[:channels]
    groups = scratch.shape[0] // slots
    planes = grid.reshape(groups, slots, rows, cols)
    total = None
    for k in range(slots):
        part = dot(planes[:, k].reshape(-1, cols), pick_matrix(k, strip, cols))
        total = part if total is None else total + part
    total = total.astype(BF16)
    first_ref[...] = total[:, :LANES].reshape(groups, rows, LANES)
    last_ref[...] = total[:, LANES:].reshape(groups, rows, LANES)


def smooth_kernel(
    strip, slots, start, unit, own_ref, up_ref, down_ref, left_ref, right_ref,
    grid_ref, grid_left_ref, grid_right_ref, lon_ref, lat_ref, out_up_ref, out_ref, out_down_ref,
    hi_ref, lo_ref, mid_ref,
):
    members, channels, rows, cols = own_ref.shape
    per, parts = max(1, slots // members), max(1, members // slots)
    groups = out_ref.shape[0] // per * parts
    half = LANES // 2
    height = slots * rows
    src = lax.broadcasted_iota(jnp.int32, (LANES, LANES), 0)
    dst = lax.broadcasted_iota(jnp.int32, (LANES, LANES), 1)
    lane = lax.broadcasted_iota(jnp.int32, (rows, LANES), 1)
    low = lane < half
    slot_of = (lane % half) // strip

    def place(n):
        first, h = start + n // parts * per, n % parts
        where = [(k // members, k % members) if parts == 1 else (0, h * slots + k) for k in range(slots)]
        return first, h, where

    def weigh(n):
        first, h, where = place(n)
        dst_channel = dst // strip // members if parts == 1 else jnp.zeros_like(dst)
        expand = src == ((first + dst_channel) % slots) * strip + dst % strip
        expand = jnp.where(expand, 1.0, 0.0).astype(BF16)
        left = left_ref[h, first // per].astype(F32) * dot(grid_left_ref[first // slots], expand)
        right = right_ref[h, first // per].astype(F32) * dot(grid_right_ref[first // slots], expand)
        sides = (
            split(jnp.where(low, left, pltpu.roll(right, half, 1))),
            split(jnp.where(low, pltpu.roll(left, half, 1), right)),
        )
        for k, (c, m) in enumerate(where):
            mine = split(own_ref[m, first + c].astype(F32) * grid_ref[first + c].astype(F32))
            side = sides[k * 2 // slots]
            keep = slot_of == k % (slots // 2)
            at = pl.ds(n * height + k * rows, rows)
            for p, ref in enumerate((hi_ref, lo_ref)):
                ref[at, :cols] = mine[p]
                ref[at, cols:] = jnp.where(keep, side[p], jnp.zeros_like(side[p]))

    def along_lon(n, many):
        at = pl.ds(n * height, many * height)
        big = dot(hi_ref[at, :], lon_ref[...])
        small = dot(lo_ref[at, :], lon_ref[:, :cols])
        hi, lo = split(big[:, :cols] + big[:, cols:] + small)
        for k in range(many * slots):
            to = pl.ds((n * slots + k) * cols, cols)
            rest = slice(k * rows, (k + 1) * rows)
            mid_ref[:rows, to] = hi[rest]
            mid_ref[rows : 2 * rows, to] = hi[rest]
            mid_ref[2 * rows :, to] = lo[rest]

    def along_lat(n):
        first, h, where = place(n)
        spread = dot(lat_ref[...], mid_ref[:, pl.ds(n * slots * cols, slots * cols)])
        for r, (ref, out) in enumerate(((up_ref, out_up_ref), (own_ref, out_ref), (down_ref, out_down_ref))):
            sums = {}
            for k, (c, m) in enumerate(where):
                piece = spread[r * rows : (r + 1) * rows, k * cols : (k + 1) * cols]
                term = piece * ref[m, first + c].astype(F32)
                sums[c] = sums[c] + term if c in sums else term
            for c, total in sums.items():
                at = first - start + c
                out[at] = total if h == 0 else out[at] + total

    units = [range(n, min(n + unit, groups)) for n in range(0, groups, unit)]
    for n in range(len(units) + 2):
        if n < len(units):
            for g in units[n]:
                weigh(g)
        if 0 <= n - 1 < len(units):
            along_lon(units[n - 1][0], len(units[n - 1]))
        if 0 <= n - 2:
            for g in units[n - 2]:
                along_lat(g)


def whole(n):
    return [pl.BlockSpec(memory_space=pltpu.VMEM)] * n


def smooth_call(strip, slots, members, rows, cols, start, size, unit=UNIT):
    block = jax.ShapeDtypeStruct((size, rows, cols), F32)
    planes = size * members
    return pl.pallas_call(
        functools.partial(smooth_kernel, strip, slots, start, unit),
        out_shape=(block,) * 3, in_specs=whole(10), out_specs=whole(3), name=f"smooth{start}",
        scratch_shapes=[
            pltpu.VMEM((planes * rows, cols + LANES), BF16),
            pltpu.VMEM((planes * rows, cols + LANES), BF16),
            pltpu.VMEM((3 * rows, planes * cols), BF16),
        ],
        compiler_params=pltpu.CompilerParams(vmem_limit_bytes=GRANT),
    )


def local(chunks, grad_tokens, token_index, members, lat_taps, lon_taps):
    ens, lat_count, lon_count = (lax.axis_size(a) for a in ("ens", "lat", "lon"))
    ens_pos, lat_pos, lon_pos = (lax.axis_index(a) for a in ("ens", "lat", "lon"))
    channels, cells = grad_tokens.shape
    rows, cols = token_index.shape
    own_channels = channels // ens
    blocks = lat_count * lon_count
    piece = cells // blocks
    strip = lon_taps.shape[0] - 1
    slots = LANES // strip
    assert cols == LANES and lat_taps.shape[0] - 1 <= rows

    tokens = lax.dynamic_slice_in_dim(grad_tokens, ens_pos * own_channels, own_channels, 0)
    tokens = tokens.reshape(own_channels, blocks, piece).transpose(1, 0, 2)
    moved = lax.all_to_all(tokens, ("lat", "lon"), split_axis=0, concat_axis=0, tiled=True)
    if piece != LANES:
        moved = moved.transpose(1, 0, 2).reshape(own_channels, cells // LANES, LANES).transpose(1, 0, 2)
    block_id = lat_pos * lon_count + lon_pos
    offset = (token_index // cells) * piece + token_index % cells - block_id * piece

    if ens == 2:
        given = lax.dynamic_slice_in_dim(members, (1 - ens_pos) * own_channels, own_channels, 1)
        kept = lax.dynamic_slice_in_dim(members, ens_pos * own_channels, own_channels, 1)
        taken = lax.ppermute(given, "ens", [(0, 1), (1, 0)])
        w = jnp.concatenate([kept, taken], axis=0)
    else:
        w = lax.all_to_all(members, "ens", split_axis=1, concat_axis=0, tiled=True)
    count = w.shape[0]
    per = max(1, slots // count)
    parts = max(1, count // slots)

    to_down = [(i, i + 1) for i in range(lat_count - 1)]
    to_up = [(i + 1, i) for i in range(lat_count - 1)]
    to_right = [(i, (i + 1) % lon_count) for i in range(lon_count)]
    to_left = [((i + 1) % lon_count, i) for i in range(lon_count)]
    w_up = lax.ppermute(w, "lat", to_down)
    w_down = lax.ppermute(w, "lat", to_up)

    strips = jax.ShapeDtypeStruct((parts, own_channels // per, rows, LANES), BF16)
    w_first, w_last = pl.pallas_call(
        functools.partial(pack_kernel, strip, slots),
        out_shape=(strips, strips), in_specs=whole(1), out_specs=whole(2), name="pack",
        compiler_params=pltpu.CompilerParams(vmem_limit_bytes=GRANT),
    )(w)
    w_left = lax.ppermute(w_last, "lon", to_right)
    w_right = lax.ppermute(w_first, "lon", to_left)

    lon_both, lat = pl.pallas_call(
        functools.partial(matrix_kernel, strip, lat_count),
        out_shape=(
            jax.ShapeDtypeStruct((2 * LANES, 2 * cols), BF16),
            jax.ShapeDtypeStruct((3 * rows, 3 * rows), BF16),
        ),
        in_specs=[pl.BlockSpec(memory_space=pltpu.SMEM)] * 2, out_specs=whole(2), name="matrices",
        compiler_params=pltpu.CompilerParams(vmem_limit_bytes=GRANT),
    )(lat_taps, lon_taps)

    padded = -(-own_channels // slots) * slots
    edges = jax.ShapeDtypeStruct((padded // slots, rows, LANES), BF16)
    grid, g_first, g_last = pl.pallas_call(
        functools.partial(gather_kernel, strip, slots),
        out_shape=(jax.ShapeDtypeStruct((own_channels, rows, cols), BF16), edges, edges),
        in_specs=whole(2), out_specs=whole(3),
        scratch_shapes=[pltpu.VMEM((padded, rows, cols), F32)], name="gather",
        compiler_params=pltpu.CompilerParams(vmem_limit_bytes=GRANT),
    )(moved, offset)
    g_left = lax.ppermute(g_last, "lon", to_right)
    g_right = lax.ppermute(g_first, "lon", to_left)

    chunks = chunks if own_channels % (chunks * per) == 0 else 1
    size = own_channels // chunks
    smooth = functools.partial(smooth_call, strip, slots, count, rows, cols)
    outs = []
    for n in range(chunks):
        up, own, down = smooth(n * size, size)(w, w_up, w_down, w_left, w_right, grid, g_left, g_right, lon_both, lat)
        from_up = lax.ppermute(down, "lat", to_down)
        from_down = lax.ppermute(up, "lat", to_up)
        outs.append((own + from_up + from_down) / (count - 1))
    return jnp.concatenate(outs, axis=0) if chunks > 1 else outs[0]


def solution(mesh):
    in_specs = (P(None, ("lat", "lon")), P("lat", "lon"), P("ens", None, "lat", "lon"), P(), P())
    out_specs = P("ens", "lat", "lon")
    return jax.shard_map(
        functools.partial(local, 2), mesh=mesh, in_specs=in_specs, out_specs=out_specs, check_vma=False
    )
```

time: 142 us -> 66.9 us (0.47); the launches traced: 140 us -> 66.6 us
  other arithmetic: 69.6 us -> 0.98 us
  waiting for transfers between devices: 7.3 us -> 26.8 us
  Pallas kernels: 25 us -> 7.17 us
  local copies, waits for them, and re-layouts: 6.17 us -> 2.22 us
  starting transfers between devices: 31.7 us -> 29.2 us
    convert_element_type x3 -> x0, other arithmetic: 42.2 us -> none  [split_outside(): return (hi.astype(BF16), (v - hi).astype(BF16))]
    all_to_all x1, waiting for transfers between devices: 0.01 us -> 15.4 us  [local(): lax.all_to_all(tokens, ('lat', 'lon'), split_axis=0, concat_axis=0, tiled...]
    pallas_call x2 -> x3, Pallas kernels: 18.8 us -> 3.66 us  [the longest x2 2.46 us: local(): smooth(n * size, size)]
    select_n x2 -> x0, other arithmetic: 10.6 us -> none  [the longest x1 10.6 us: lat_matrix(): gather = jnp.where(inside[:, None], gather, 0.0)]
    add x1 -> x0, other arithmetic: 10.6 us -> none  [band(): total = total + jnp.where(offset == k, taps[k], 0.0)]
    ppermute x1, waiting for transfers between devices: 0.01 us -> 4.08 us  [local(): g_left = lax.ppermute(g_last, 'lon', to_right)]
    reduce_sum x5 -> x0, other arithmetic: 3.18 us -> none  [the longest x4 3.05 us: lon_matrix(): jnp.sum(taps * longer[radius2 - d:radius2 - d + count])]
    unnamed x31 -> x9, local copies, waits for them, and re-layouts: 3.15 us -> 0.06 us
  transfers between devices with their start and end apart: 12 -> 12, of which waited for: 4 -> 6; matrix products, arithmetic and copies ran while one was open for 50% -> 1% of each run, Pallas kernels for 11% -> 9%
where the time goes in v2:
time: 66.9 us; the launch traced here: 66.6 us
  starting transfers between devices  29.2 us (44%)
  waiting for transfers between devices  26.8 us (40%)
  Pallas kernels  7.17 us (11%)
  local copies, waits for them, and re-layouts  2.22 us (3%)
  other arithmetic  0.98 us (1%)
    all_to_all x1, waiting for transfers between devices, local(): lax.all_to_all(tokens, ('lat', 'lon'), split_axis=0, concat_axis=0, tiled...  15.4 us
    ppermute x2, starting transfers between devices, local(): from_up = lax.ppermute(down, 'lat', to_down)  7.97 us
    all_to_all x1, starting transfers between devices, local(): lax.all_to_all(tokens, ('lat', 'lon'), split_axis=0, concat_axis=0, tiled...  7.93 us
    ppermute x1, starting transfers between devices, local(): w_up = lax.ppermute(w, 'lat', to_down)  4.89 us
    ppermute x1, waiting for transfers between devices, local(): g_left = lax.ppermute(g_last, 'lon', to_right)  4.08 us
    ppermute x1, waiting for transfers between devices, local(): g_right = lax.ppermute(g_first, 'lon', to_left)  2.66 us
    ppermute x2, starting transfers between devices, local(): from_down = lax.ppermute(up, 'lat', to_up)  2.58 us
    pallas_call x2, Pallas kernels, local(): smooth(n * size, size)  2.46 us
  transfers between devices with their start and end apart: 12, of which 6 were waited for; matrix products, arithmetic and copies ran while one was open for 1% of the time, Pallas kernels for 9%

profile of v2, /device:TPU:0, one launch (start us, length us, event | category | flops | bytes accessed | tf_op | source)
XLA Modules:
  0.0 66.6 jit_solution(3044364436644160108)
XLA Ops:
  0.0 1.3 %constant_dynamic-slice_fusion.2 = (bf16[2,52,16,128]{3,2,1,0:T(8,128)(2,1)S(1)}, bf16[2,52,16,128]{3,2,1,0:T(8,128)(2,1)S(1)}) fusion(bf16[2,104,16,128]{3,2,1,0:T(8,128)(2,1)} %param.7, s32[]{:T(128)S(6)} %select_n.19, s32[]{:T(128)S(6)} %select_n.20), kind=kLoop, calls=%fused_computation.20 | loop fusion | bytes 1703944 | tf_op jit(solution)/shard_map/dynamic_slice | solution.py:231
  1.3 0.6 collective-permute-start
  1.9 1.4 %collective-permute-done = bf16[2,52,16,128]{3,2,1,0:T(8,128)(2,1)S(1)} collective-permute-done((bf16[2,52,16,128]{3,2,1,0:T(8,128)(2,1)S(1)}, bf16[2,52,16,128]{3,2,1,0:T(8,128)(2,1)S(1)}, u32[]{:S(2)}, u32[]{:S(2)}) %collective-permute-start) | collective-permute-done | bytes 426016 | tf_op jit(solution)/shard_map/ppermute | solution.py:232
  3.3 0.1 pad_maximum_fusion.w_ref.own_ref
  3.4 4.9 %collective-permute-start.1 = (bf16[4,52,16,128]{3,2,1,0:T(8,128)(2,1)S(1)}, bf16[4,52,16,128]{3,2,1,0:T(8,128)(2,1)S(1)}, u32[]{:S(2)}, u32[]{:S(2)}) collective-permute-start(bf16[4,52,16,128]{3,2,1,0:T(8,128)(2,1)S(1)} %pad_maximum_fusion.w_ref.own_ref), channel_id=1, source_target_pairs={{0,4},{4,8},{8,12},{1,5},{5,9},{9,13},{2,6},{6,10},{10,14},{3,7},{... | collective-permute-start | bytes 2555912 | tf_op jit(solution)/shard_map/ppermute | solution.py:244
  8.3 1.3 %collective-permute-start.2 = (bf16[4,52,16,128]{3,2,1,0:T(8,128)(2,1)S(1)}, bf16[4,52,16,128]{3,2,1,0:T(8,128)(2,1)S(1)}, u32[]{:S(2)}, u32[]{:S(2)}) collective-permute-start(bf16[4,52,16,128]{3,2,1,0:T(8,128)(2,1)S(1)} %pad_maximum_fusion.w_ref.own_ref), channel_id=1, source_target_pairs={{4,0},{8,4},{12,8},{5,1},{9,5},{13,9},{6,2},{10,6},{14,10},{7,3},{... | collective-permute-start | bytes 2555912 | tf_op jit(solution)/shard_map/ppermute | solution.py:245
  9.6 0.1 constant_dynamic-slice_fusion
  9.7 0.7 %copy.9 = bf16[52,16,128]{2,0,1:T(8,128)(2,1)} copy(bf16[52,16,128]{2,1,0:T(8,128)(2,1)S(1)} %slice) | data formatting | bytes 425984 | tf_op jit(solution)/shard_map/reshape | solution.py:222
  10.5 7.9 %all-to-all-start = ((bf16[16,52,128]{2,1,0:T(8,128)(2,1)}), bf16[16,52,128]{2,1,0:T(8,128)(2,1)S(1)}, u32[]{:S(2)}, u32[]{:S(2)}) async-start(bf16[16,52,128]{2,1,0:T(8,128)(2,1)} %bitcast.5), calls=%async_computation | async-start | bytes 458752 | tf_op jit(solution)/shard_map/all_to_all | solution.py:223
  18.4 0.0 copy-start.3
  18.4 1.2 %pack.1 = (bf16[1,26,16,128]{3,2,1,0:T(8,128)(2,1)S(1)}, bf16[1,26,16,128]{3,2,1,0:T(8,128)(2,1)}) custom-call(bf16[4,52,16,128]{3,2,1,0:T(8,128)(2,1)S(1)} %pad_maximum_fusion.w_ref.own_ref), custom_call_target="tpu_custom_call" | custom-call | tf_op jit(solution)/shard_map/pack/pallas_call | solution.py:248
  19.7 1.9 %collective-permute-start.3 = (bf16[1,26,16,128]{3,2,1,0:T(8,128)(2,1)}, bf16[1,26,16,128]{3,2,1,0:T(8,128)(2,1)S(1)}, u32[]{:S(2)}, u32[]{:S(2)}) collective-permute-start(bf16[1,26,16,128]{3,2,1,0:T(8,128)(2,1)} %get-tuple-element.18), channel_id=1, source_target_pairs={{0,1},{1,2},{2,3},{3,0},{4,5},{5,6},{6,7},{7,4},{8,9},{9,10},{10,1... | collective-permute-start | bytes 319496 | tf_op jit(solution)/shard_map/ppermute | solution.py:253
  21.6 1.0 %collective-permute-start.4 = (bf16[1,26,16,128]{3,2,1,0:T(8,128)(2,1)S(1)}, bf16[1,26,16,128]{3,2,1,0:T(8,128)(2,1)S(1)}, u32[]{:S(2)}, u32[]{:S(2)}) collective-permute-start(bf16[1,26,16,128]{3,2,1,0:T(8,128)(2,1)S(1)} %get-tuple-element.19), channel_id=1, source_target_pairs={{1,0},{2,1},{3,2},{0,3},{5,4},{6,5},{7,6},{4,7},{9,8},{10,9},{11,1... | collective-permute-start | bytes 319496 | tf_op jit(solution)/shard_map/ppermute | solution.py:254
  22.6 15.4 %all-to-all-done.moved_ref = bf16[16,52,128]{2,1,0:T(8,128)(2,1)S(1)} async-done(((bf16[16,52,128]{2,1,0:T(8,128)(2,1)}), bf16[16,52,128]{2,1,0:T(8,128)(2,1)S(1)}, u32[]{:S(2)}, u32[]{:S(2)}) %all-to-all-start) | async-done | bytes 213024 | tf_op jit(solution)/shard_map/all_to_all | solution.py:223
  38.0 2.3 %gather.1 = (bf16[52,16,128]{2,1,0:T(8,128)(2,1)S(1)}, bf16[7,16,128]{2,1,0:T(8,128)(2,1)S(1)}, bf16[7,16,128]{2,1,0:T(8,128)(2,1)S(1)}) custom-call(bf16[16,52,128]{2,1,0:T(8,128)(2,1)S(1)} %all-to-all-done.moved_ref, s32[16,128]{1,0:T(8,128)S(1)} %fusion.2.offset_ref), custom_call_target="tpu_custom_call" | custom-call | tf_op jit(solution)/shard_map/gather/pallas_call | solution.py:268
  40.3 0.0 copy-start.1
  40.3 0.0 copy-start.2
  40.3 1.0 %collective-permute-start.5 = (bf16[7,16,128]{2,1,0:T(8,128)(2,1)S(1)}, bf16[7,16,128]{2,1,0:T(8,128)(2,1)S(1)}, u32[]{:S(2)}, u32[]{:S(2)}) collective-permute-start(bf16[7,16,128]{2,1,0:T(8,128)(2,1)S(1)} %get-tuple-element.21), channel_id=1, source_target_pairs={{0,1},{1,2},{2,3},{3,0},{4,5},{5,6},{6,7},{7,4},{8,9},{9,10},{10,1... | collective-permute-start | bytes 86024 | tf_op jit(solution)/shard_map/ppermute | solution.py:275
  41.4 4.1 %collective-permute-done.5.grid_left_ref = bf16[7,16,128]{2,1,0:T(8,128)(2,1)S(1)} collective-permute-done((bf16[7,16,128]{2,1,0:T(8,128)(2,1)S(1)}, bf16[7,16,128]{2,1,0:T(8,128)(2,1)S(1)}, u32[]{:S(2)}, u32[]{:S(2)}) %collective-permute-start.5) | collective-permute-done | bytes 28704 | tf_op jit(solution)/shard_map/ppermute | solution.py:275
  45.4 1.2 %matrices.1 = (bf16[256,256]{1,0:T(8,128)(2,1)S(1)}, bf16[48,48]{1,0:T(8,128)(2,1)S(1)}) custom-call(f32[17]{0:T(128)S(1)} %copy-done.1, f32[17]{0:T(128)S(1)} %copy-done.2), custom_call_target="tpu_custom_call" | custom-call | tf_op jit(solution)/shard_map/matrices/pallas_call | solution.py:256
  46.6 2.7 %collective-permute-done.6.grid_right_ref = bf16[7,16,128]{2,1,0:T(8,128)(2,1)S(1)} collective-permute-done((bf16[7,16,128]{2,1,0:T(8,128)(2,1)S(1)}, bf16[7,16,128]{2,1,0:T(8,128)(2,1)S(1)}, u32[]{:S(2)}, u32[]{:S(2)}) %collective-permute-start.6) | collective-permute-done | bytes 28704 | tf_op jit(solution)/shard_map/ppermute | solution.py:276
  49.3 0.0 collective-permute-done.3.left_ref
  49.3 1.2 %smooth0.1 = (f32[26,16,128]{2,1,0:T(8,128)S(1)}, f32[26,16,128]{2,1,0:T(8,128)S(1)}, f32[26,16,128]{2,1,0:T(8,128)S(1)}) custom-call(bf16[4,52,16,128]{3,2,1,0:T(8,128)(2,1)S(1)} %pad_maximum_fusion.w_ref.own_ref, bf16[4,52,16,128]{3,2,1,0:T(8,128)(2,1)S(1)} %collective-permute-done.1.up_ref, bf16[4,52,16,128]{3,2,1,0:T(8,128)(2,1)S(1)} %collective-permute-done.2.down_ref, ...), custom_call_target="tpu_custom_call" | custom-call | tf_op jit(solution)/shard_map/smooth0/pallas_call | solution.py:283
  50.6 2.8 %collective-permute-start.7 = (f32[26,16,128]{2,1,0:T(8,128)S(1)}, f32[26,16,128]{2,1,0:T(8,128)S(1)}, u32[]{:S(2)}, u32[]{:S(2)}) collective-permute-start(f32[26,16,128]{2,1,0:T(8,128)S(1)} %get-tuple-element.26), channel_id=1, source_target_pairs={{0,4},{4,8},{8,12},{1,5},{5,9},{9,13},{2,6},{6,10},{10,14},{3,7},{... | collective-permute-start | bytes 638984 | tf_op jit(solution)/shard_map/ppermute | solution.py:284
  53.4 1.3 %collective-permute-start.8 = (f32[26,16,128]{2,1,0:T(8,128)S(1)}, f32[26,16,128]{2,1,0:T(8,128)S(1)}, u32[]{:S(2)}, u32[]{:S(2)}) collective-permute-start(f32[26,16,128]{2,1,0:T(8,128)S(1)} %get-tuple-element.27), channel_id=1, source_target_pairs={{4,0},{8,4},{12,8},{5,1},{9,5},{13,9},{6,2},{10,6},{14,10},{7,3},{... | collective-permute-start | bytes 638984 | tf_op jit(solution)/shard_map/ppermute | solution.py:285
  54.7 1.2 %smooth26.1 = (f32[26,16,128]{2,1,0:T(8,128)S(1)}, f32[26,16,128]{2,1,0:T(8,128)S(1)}, f32[26,16,128]{2,1,0:T(8,128)S(1)}) custom-call(bf16[4,52,16,128]{3,2,1,0:T(8,128)(2,1)S(1)} %pad_maximum_fusion.w_ref.own_ref, bf16[4,52,16,128]{3,2,1,0:T(8,128)(2,1)S(1)} %collective-permute-done.1.up_ref, bf16[4,52,16,128]{3,2,1,0:T(8,128)(2,1)S(1)} %collective-permute-done.2.down_ref, ...), custom_call_target="tpu_custom_call" | custom-call | tf_op jit(solution)/shard_map/smooth26/pallas_call | solution.py:283
  55.9 1.3 %collective-permute-start.10 = (f32[26,16,128]{2,1,0:T(8,128)S(1)}, f32[26,16,128]{2,1,0:T(8,128)S(1)}, u32[]{:S(2)}, u32[]{:S(2)}) collective-permute-start(f32[26,16,128]{2,1,0:T(8,128)S(1)} %get-tuple-element.30), channel_id=1, source_target_pairs={{4,0},{8,4},{12,8},{5,1},{9,5},{13,9},{6,2},{10,6},{14,10},{7,3},{... | collective-permute-start | bytes 638984 | tf_op jit(solution)/shard_map/ppermute | solution.py:285
  57.2 5.2 %collective-permute-start.9 = (f32[26,16,128]{2,1,0:T(8,128)S(1)}, f32[26,16,128]{2,1,0:T(8,128)S(1)}, u32[]{:S(2)}, u32[]{:S(2)}) collective-permute-start(f32[26,16,128]{2,1,0:T(8,128)S(1)} %get-tuple-element.29), channel_id=1, source_target_pairs={{0,4},{4,8},{8,12},{1,5},{5,9},{9,13},{2,6},{6,10},{10,14},{3,7},{... | collective-permute-start | bytes 638984 | tf_op jit(solution)/shard_map/ppermute | solution.py:284
  62.4 0.1 add_multiply_fusion.1
  62.5 1.8 %collective-permute-done.10 = f32[26,16,128]{2,1,0:T(8,128)S(1)} collective-permute-done((f32[26,16,128]{2,1,0:T(8,128)S(1)}, f32[26,16,128]{2,1,0:T(8,128)S(1)}, u32[]{:S(2)}, u32[]{:S(2)}) %collective-permute-start.10) | collective-permute-done | bytes 213024 | tf_op jit(solution)/shard_map/ppermute | solution.py:285
  64.3 1.5 %collective-permute-done.9 = f32[26,16,128]{2,1,0:T(8,128)S(1)} collective-permute-done((f32[26,16,128]{2,1,0:T(8,128)S(1)}, f32[26,16,128]{2,1,0:T(8,128)S(1)}, u32[]{:S(2)}, u32[]{:S(2)}) %collective-permute-start.9) | collective-permute-done | bytes 213024 | tf_op jit(solution)/shard_map/ppermute | solution.py:284
  65.8 0.8 %pad_maximum_fusion.1 = f32[52,16,128]{2,1,0:T(8,128)} fusion(f32[26,16,128]{2,1,0:T(8,128)S(1)} %add_multiply_fusion, f32[26,16,128]{2,1,0:T(8,128)S(1)} %add_multiply_fusion.1), kind=kLoop, calls=%fused_computation.1 | loop fusion | flops 106496 | bytes 851968 | tf_op jit(solution)/shard_map/concatenate | solution.py:287
  (15 shorter events, 0.1 us)
Async XLA Ops:
  0.0 9.6 %copy-start = (bf16[104,2048]{1,0:T(8,128)(2,1)S(1)}, bf16[104,2048]{1,0:T(8,128)(2,1)}, u32[]{:S(2)}) copy-start(bf16[104,2048]{1,0:T(8,128)(2,1)} %param.5) | copy-start | bytes 1277956
  1.3 2.0 %collective-permute-start = (bf16[2,52,16,128]{3,2,1,0:T(8,128)(2,1)S(1)}, bf16[2,52,16,128]{3,2,1,0:T(8,128)(2,1)S(1)}, u32[]{:S(2)}, u32[]{:S(2)}) collective-permute-start(bf16[2,52,16,128]{3,2,1,0:T(8,128)(2,1)S(1)} %get-tuple-element.32), channel_id=1, source_target_pairs={{0,16},{16,0},{1,17},{17,1},{2,18},{18,2},{3,19},{19,3},{4,20},{20... | collective-permute-start | bytes 1277960 | tf_op jit(solution)/shard_map/ppermute | solution.py:232
  3.4 45.9 %collective-permute-start.1 = (bf16[4,52,16,128]{3,2,1,0:T(8,128)(2,1)S(1)}, bf16[4,52,16,128]{3,2,1,0:T(8,128)(2,1)S(1)}, u32[]{:S(2)}, u32[]{:S(2)}) collective-permute-start(bf16[4,52,16,128]{3,2,1,0:T(8,128)(2,1)S(1)} %pad_maximum_fusion.w_ref.own_ref), channel_id=1, source_target_pairs={{0,4},{4,8},{8,12},{1,5},{5,9},{9,13},{2,6},{6,10},{10,14},{3,7},{... | collective-permute-start | bytes 2555912 | tf_op jit(solution)/shard_map/ppermute | solution.py:244
  8.3 41.0 %collective-permute-start.2 = (bf16[4,52,16,128]{3,2,1,0:T(8,128)(2,1)S(1)}, bf16[4,52,16,128]{3,2,1,0:T(8,128)(2,1)S(1)}, u32[]{:S(2)}, u32[]{:S(2)}) collective-permute-start(bf16[4,52,16,128]{3,2,1,0:T(8,128)(2,1)S(1)} %pad_maximum_fusion.w_ref.own_ref), channel_id=1, source_target_pairs={{4,0},{8,4},{12,8},{5,1},{9,5},{13,9},{6,2},{10,6},{14,10},{7,3},{... | collective-permute-start | bytes 2555912 | tf_op jit(solution)/shard_map/ppermute | solution.py:245
  10.5 27.6 %all-to-all-start = ((bf16[16,52,128]{2,1,0:T(8,128)(2,1)}), bf16[16,52,128]{2,1,0:T(8,128)(2,1)S(1)}, u32[]{:S(2)}, u32[]{:S(2)}) async-start(bf16[16,52,128]{2,1,0:T(8,128)(2,1)} %bitcast.5), calls=%async_computation | async-start | bytes 458752 | tf_op jit(solution)/shard_map/all_to_all | solution.py:223
  18.4 4.2 %copy-start.3 = (s32[16,128]{1,0:T(8,128)S(1)}, s32[16,128]{1,0:T(8,128)}, u32[]{:S(2)}) copy-start(s32[16,128]{1,0:T(8,128)} %param.6) | copy-start | bytes 24580
  19.7 29.6 %collective-permute-start.3 = (bf16[1,26,16,128]{3,2,1,0:T(8,128)(2,1)}, bf16[1,26,16,128]{3,2,1,0:T(8,128)(2,1)S(1)}, u32[]{:S(2)}, u32[]{:S(2)}) collective-permute-start(bf16[1,26,16,128]{3,2,1,0:T(8,128)(2,1)} %get-tuple-element.18), channel_id=1, source_target_pairs={{0,1},{1,2},{2,3},{3,0},{4,5},{5,6},{6,7},{7,4},{8,9},{9,10},{10,1... | collective-permute-start | bytes 319496 | tf_op jit(solution)/shard_map/ppermute | solution.py:253
  21.6 27.7 %collective-permute-start.4 = (bf16[1,26,16,128]{3,2,1,0:T(8,128)(2,1)S(1)}, bf16[1,26,16,128]{3,2,1,0:T(8,128)(2,1)S(1)}, u32[]{:S(2)}, u32[]{:S(2)}) collective-permute-start(bf16[1,26,16,128]{3,2,1,0:T(8,128)(2,1)S(1)} %get-tuple-element.19), channel_id=1, source_target_pairs={{1,0},{2,1},{3,2},{0,3},{5,4},{6,5},{7,6},{4,7},{9,8},{10,9},{11,1... | collective-permute-start | bytes 319496 | tf_op jit(solution)/shard_map/ppermute | solution.py:254
  40.3 5.1 %copy-start.1 = (f32[17]{0:T(128)S(1)}, f32[17]{0:T(128)}, u32[]{:S(2)}) copy-start(f32[17]{0:T(128)} %lat_taps_ref.1) | copy-start | bytes 208
  40.3 5.1 %copy-start.2 = (f32[17]{0:T(128)S(1)}, f32[17]{0:T(128)}, u32[]{:S(2)}) copy-start(f32[17]{0:T(128)} %lon_taps_ref.1) | copy-start | bytes 208
  40.3 5.1 %collective-permute-start.5 = (bf16[7,16,128]{2,1,0:T(8,128)(2,1)S(1)}, bf16[7,16,128]{2,1,0:T(8,128)(2,1)S(1)}, u32[]{:S(2)}, u32[]{:S(2)}) collective-permute-start(bf16[7,16,128]{2,1,0:T(8,128)(2,1)S(1)} %get-tuple-element.21), channel_id=1, source_target_pairs={{0,1},{1,2},{2,3},{3,0},{4,5},{5,6},{6,7},{7,4},{8,9},{9,10},{10,1... | collective-permute-start | bytes 86024 | tf_op jit(solution)/shard_map/ppermute | solution.py:275
  45.4 3.9 %collective-permute-start.6 = (bf16[7,16,128]{2,1,0:T(8,128)(2,1)S(1)}, bf16[7,16,128]{2,1,0:T(8,128)(2,1)S(1)}, u32[]{:S(2)}, u32[]{:S(2)}) collective-permute-start(bf16[7,16,128]{2,1,0:T(8,128)(2,1)S(1)} %get-tuple-element.22), channel_id=1, source_target_pairs={{1,0},{2,1},{3,2},{0,3},{5,4},{6,5},{7,6},{4,7},{9,8},{10,9},{11,1... | collective-permute-start | bytes 86024 | tf_op jit(solution)/shard_map/ppermute | solution.py:276
  50.6 11.8 %collective-permute-start.7 = (f32[26,16,128]{2,1,0:T(8,128)S(1)}, f32[26,16,128]{2,1,0:T(8,128)S(1)}, u32[]{:S(2)}, u32[]{:S(2)}) collective-permute-start(f32[26,16,128]{2,1,0:T(8,128)S(1)} %get-tuple-element.26), channel_id=1, source_target_pairs={{0,4},{4,8},{8,12},{1,5},{5,9},{9,13},{2,6},{6,10},{10,14},{3,7},{... | collective-permute-start | bytes 638984 | tf_op jit(solution)/shard_map/ppermute | solution.py:284
  53.4 9.0 %collective-permute-start.8 = (f32[26,16,128]{2,1,0:T(8,128)S(1)}, f32[26,16,128]{2,1,0:T(8,128)S(1)}, u32[]{:S(2)}, u32[]{:S(2)}) collective-permute-start(f32[26,16,128]{2,1,0:T(8,128)S(1)} %get-tuple-element.27), channel_id=1, source_target_pairs={{4,0},{8,4},{12,8},{5,1},{9,5},{13,9},{6,2},{10,6},{14,10},{7,3},{... | collective-permute-start | bytes 638984 | tf_op jit(solution)/shard_map/ppermute | solution.py:285
  55.9 8.4 %collective-permute-start.10 = (f32[26,16,128]{2,1,0:T(8,128)S(1)}, f32[26,16,128]{2,1,0:T(8,128)S(1)}, u32[]{:S(2)}, u32[]{:S(2)}) collective-permute-start(f32[26,16,128]{2,1,0:T(8,128)S(1)} %get-tuple-element.30), channel_id=1, source_target_pairs={{4,0},{8,4},{12,8},{5,1},{9,5},{13,9},{6,2},{10,6},{14,10},{7,3},{... | collective-permute-start | bytes 638984 | tf_op jit(solution)/shard_map/ppermute | solution.py:285
  57.2 8.5 %collective-permute-start.9 = (f32[26,16,128]{2,1,0:T(8,128)S(1)}, f32[26,16,128]{2,1,0:T(8,128)S(1)}, u32[]{:S(2)}, u32[]{:S(2)}) collective-permute-start(f32[26,16,128]{2,1,0:T(8,128)S(1)} %get-tuple-element.29), channel_id=1, source_target_pairs={{0,4},{4,8},{8,12},{1,5},{5,9},{9,13},{2,6},{6,10},{10,14},{3,7},{... | collective-permute-start | bytes 638984 | tf_op jit(solution)/shard_map/ppermute | solution.py:284

commit v3 on v2

v3 whole, which is shorter than its diff:
```python
import functools

import jax
import jax.numpy as jnp
from jax import lax
from jax.experimental import pallas as pl
from jax.experimental.pallas import tpu as pltpu
from jax.sharding import PartitionSpec as P


LANES = 128
F32 = jnp.float32
BF16 = jnp.bfloat16
UNIT = 7
GRANT = 24 << 20


def dot(a, b):
    return lax.dot_general(a, b, (((1,), (0,)), ((), ())), preferred_element_type=F32)


def split(v):
    hi = v.astype(BF16)
    return hi, (v - hi.astype(F32)).astype(BF16)


def band(taps, offset):
    total = jnp.zeros(offset.shape, F32)
    for k, tap in enumerate(taps):
        total = jnp.where(offset == k, tap, total)
    return total


def fill_matrices(strip, lat_count, lat_taps_ref, lon_taps_ref, lon_ref, lat_ref):
    cols, rows = lon_ref.shape[1] // 2, lat_ref.shape[0] // 3
    count = lon_taps_ref.shape[0]
    iota = lax.broadcasted_iota
    taps = [lon_taps_ref[k] for k in range(count)]
    half = [sum(taps[a] * taps[a - d] for a in range(d, count)) for d in range(count)]
    both = half[:0:-1] + half
    place = iota(jnp.int32, (2 * LANES, cols), 0)
    inner = place % strip
    even = lax.rem(lax.axis_index("lon"), 2) == 0
    after = (place < cols + LANES // 2) == even
    source = jnp.where(place < cols, place, jnp.where(after, cols + inner, inner - strip))
    hi, lo = split(band(both, source - iota(jnp.int32, (2 * LANES, cols), 1) + count - 1))
    lon_ref[...] = jnp.concatenate([hi, lo], axis=1)
    count = lat_taps_ref.shape[0]
    radius = (count - 1) // 2
    taps = [lat_taps_ref[k] for k in range(count)]
    middle = rows + 2 * radius
    toward = jnp.where(lax.rem(lax.axis_index("lat"), 2) == 0, rows, -rows)
    place = iota(jnp.int32, (3 * rows, middle), 0)
    out_row = place % rows + (1 - place // rows) * toward
    mid_row = iota(jnp.int32, (3 * rows, middle), 1) - radius
    spread = band(taps, mid_row - out_row + radius)
    mid_row = iota(jnp.int32, (middle, rows), 0) - radius
    gather = band(taps[::-1], iota(jnp.int32, (middle, rows), 1) - mid_row + radius)
    whole_row = lax.axis_index("lat") * rows + mid_row
    gather = jnp.where((whole_row >= 0) & (whole_row < lat_count * rows), gather, 0.0)
    hi, lo = split(jnp.dot(spread, gather, precision=lax.Precision.HIGHEST, preferred_element_type=F32))
    lat_ref[...] = jnp.concatenate([hi, lo, hi], axis=1)


def pick_matrix(slot, strip, cols):
    even = lax.rem(lax.axis_index("lon"), 2) == 0
    last = cols - strip
    lane = lax.broadcasted_iota(jnp.int32, (cols, 2 * LANES), 1)
    row = lax.broadcasted_iota(jnp.int32, (cols, 2 * LANES), 0)
    first = jnp.where((lane < LANES) == even, last, 0)
    chosen = (lane % LANES // strip == slot) & (row == first + lane % strip)
    return jnp.where(chosen, 1.0, 0.0).astype(BF16)


def prepare_kernel(strip, slots, lat_count, parts, *refs):
    w_refs, (lat_taps_ref, lon_taps_ref, a_ref, b_ref, lon_ref, lat_ref) = refs[:parts], refs[parts:]
    fill_matrices(strip, lat_count, lat_taps_ref, lon_taps_ref, lon_ref, lat_ref)
    each, channels, rows, cols = w_refs[0].shape
    members = each * parts
    per = max(1, slots // members)
    for h in range(max(1, members // slots)):
        total = None
        for k in range(slots):
            c2, m = (k // members, k % members) if members <= slots else (0, h * slots + k)
            plane = w_refs[m // each][m % each].reshape(channels // per, per, rows, cols)[:, c2]
            part = dot(plane.reshape(-1, cols), pick_matrix(k, strip, cols))
            total = part if total is None else total + part
        total = total.astype(BF16)
        a_ref[h] = total[:, :LANES].reshape(channels // per, rows, LANES)
        b_ref[h] = total[:, LANES:].reshape(channels // per, rows, LANES)


def gather_kernel(strip, slots, moved_ref, offset_ref, grid_ref, a_ref, b_ref, scratch):
    pieces, channels, width = moved_ref.shape
    rows, cols = offset_ref.shape
    scratch[channels:] = jnp.zeros((scratch.shape[0] - channels, rows, cols), F32)
    tokens = jnp.concatenate([moved_ref[n] for n in range(pieces)], axis=1)
    token = lax.broadcasted_iota(jnp.int32, (pieces * width, 2 * cols), 0)
    for i in range(0, rows, 2):
        wanted = jnp.concatenate([offset_ref[i : i + 1], offset_ref[i + 1 : i + 2]], axis=1)
        chosen = jnp.where(token == wanted, 1.0, 0.0).astype(BF16)
        found = dot(tokens, chosen)
        scratch[:channels, i, :] = found[:, :cols]
        scratch[:channels, i + 1, :] = found[:, cols:]
    grid = scratch[...].astype(BF16)
    grid_ref[...] = grid[:channels]
    groups = scratch.shape[0] // slots
    planes = grid.reshape(groups, slots, rows, cols)
    total = None
    for k in range(slots):
        part = dot(planes[:, k].reshape(-1, cols), pick_matrix(k, strip, cols))
        total = part if total is None else total + part
    total = total.astype(BF16)
    a_ref[...] = total[:, :LANES].reshape(groups, rows, LANES)
    b_ref[...] = total[:, LANES:].reshape(groups, rows, LANES)


def smooth_kernel(strip, slots, start, unit, parts, *refs):
    own_refs, a_refs, b_refs = (refs[n * parts : (n + 1) * parts] for n in range(3))
    (strip_a_ref, strip_b_ref, grid_ref, grid_a_ref, grid_b_ref, lon_ref, lat_ref) = refs[3 * parts : 3 * parts + 7]
    out_a_ref, out_ref, out_b_ref, hi_ref, lo_ref, mid_ref = refs[3 * parts + 7 :]
    each, _, rows, cols = own_refs[0].shape
    members = each * parts

    def member(refs, m, c):
        return refs[m // each][m % each, c].astype(F32)

    per, folds = max(1, slots // members), max(1, members // slots)
    groups = out_ref.shape[0] // per * folds
    half = LANES // 2
    height = slots * rows
    src = lax.broadcasted_iota(jnp.int32, (LANES, LANES), 0)
    dst = lax.broadcasted_iota(jnp.int32, (LANES, LANES), 1)
    lane = lax.broadcasted_iota(jnp.int32, (rows, LANES), 1)
    low = lane < half
    slot_of = (lane % half) // strip

    def place(n):
        first, h = start + n // folds * per, n % folds
        where = [(k // members, k % members) if folds == 1 else (0, h * slots + k) for k in range(slots)]
        return first, h, where

    def weigh(n):
        first, h, where = place(n)
        dst_channel = dst // strip // members if folds == 1 else jnp.zeros_like(dst)
        expand = src == ((first + dst_channel) % slots) * strip + dst % strip
        expand = jnp.where(expand, 1.0, 0.0).astype(BF16)
        edge_a = strip_a_ref[h, first // per].astype(F32) * dot(grid_a_ref[first // slots], expand)
        edge_b = strip_b_ref[h, first // per].astype(F32) * dot(grid_b_ref[first // slots], expand)
        sides = (
            split(jnp.where(low, edge_a, pltpu.roll(edge_b, half, 1))),
            split(jnp.where(low, pltpu.roll(edge_a, half, 1), edge_b)),
        )
        for k, (c, m) in enumerate(where):
            mine = split(member(own_refs, m, first + c) * grid_ref[first + c].astype(F32))
            side = sides[k * 2 // slots]
            keep = slot_of == k % (slots // 2)
            at = pl.ds(n * height + k * rows, rows)
            for p, ref in enumerate((hi_ref, lo_ref)):
                ref[at, :cols] = mine[p]
                ref[at, cols:] = jnp.where(keep, side[p], jnp.zeros_like(side[p]))

    def along_lon(n, many):
        at = pl.ds(n * height, many * height)
        big = dot(hi_ref[at, :], lon_ref[...])
        small = dot(lo_ref[at, :], lon_ref[:, :cols])
        hi, lo = split(big[:, :cols] + big[:, cols:] + small)
        for k in range(many * slots):
            to = pl.ds((n * slots + k) * cols, cols)
            rest = slice(k * rows, (k + 1) * rows)
            mid_ref[:rows, to] = hi[rest]
            mid_ref[rows : 2 * rows, to] = hi[rest]
            mid_ref[2 * rows :, to] = lo[rest]

    def along_lat(n):
        first, h, where = place(n)
        spread = dot(lat_ref[...], mid_ref[:, pl.ds(n * slots * cols, slots * cols)])
        for r, (weights, out) in enumerate(((a_refs, out_a_ref), (own_refs, out_ref), (b_refs, out_b_ref))):
            sums = {}
            for k, (c, m) in enumerate(where):
                piece = spread[r * rows : (r + 1) * rows, k * cols : (k + 1) * cols]
                term = piece * member(weights, m, first + c)
                sums[c] = sums[c] + term if c in sums else term
            for c, total in sums.items():
                at = first - start + c
                out[at] = total if h == 0 else out[at] + total

    units = [range(n, min(n + unit, groups)) for n in range(0, groups, unit)]
    for n in range(len(units) + 2):
        if n < len(units):
            for g in units[n]:
                weigh(g)
        if 0 <= n - 1 < len(units):
            along_lon(units[n - 1][0], len(units[n - 1]))
        if 0 <= n - 2:
            for g in units[n - 2]:
                along_lat(g)


def whole(n):
    return [pl.BlockSpec(memory_space=pltpu.VMEM)] * n


def smooth_call(strip, slots, members, rows, cols, parts, start, size, unit=UNIT):
    block = jax.ShapeDtypeStruct((size, rows, cols), F32)
    planes = size * members
    return pl.pallas_call(
        functools.partial(smooth_kernel, strip, slots, start, unit, parts),
        out_shape=(block,) * 3, in_specs=whole(3 * parts + 7), out_specs=whole(3), name="smooth",
        scratch_shapes=[
            pltpu.VMEM((planes * rows, cols + LANES), BF16),
            pltpu.VMEM((planes * rows, cols + LANES), BF16),
            pltpu.VMEM((3 * rows, planes * cols), BF16),
        ],
        compiler_params=pltpu.CompilerParams(vmem_limit_bytes=GRANT),
    )


def partners(count, first, closed):
    pairs = [(i, (i + 1) % count) for i in range(first, count if closed else count - 1, 2)]
    return sorted(set(pairs + [(j, i) for i, j in pairs]))


def local(grad_tokens, token_index, members, lat_taps, lon_taps):
    ens, lat_count, lon_count = (lax.axis_size(a) for a in ("ens", "lat", "lon"))
    ens_pos, lat_pos, lon_pos = (lax.axis_index(a) for a in ("ens", "lat", "lon"))
    channels, cells = grad_tokens.shape
    rows, cols = token_index.shape
    own_channels = channels // ens
    blocks = lat_count * lon_count
    piece = cells // blocks
    strip = lon_taps.shape[0] - 1
    slots = LANES // strip
    assert cols == LANES and lon_count % 2 == 0 and lat_taps.shape[0] - 1 <= rows

    tokens = lax.dynamic_slice_in_dim(grad_tokens, ens_pos * own_channels, own_channels, 0)
    tokens = tokens.reshape(own_channels, blocks, piece).transpose(1, 0, 2)
    moved = lax.all_to_all(tokens, ("lat", "lon"), split_axis=0, concat_axis=0, tiled=True)
    if piece != LANES:
        moved = moved.transpose(1, 0, 2).reshape(own_channels, cells // LANES, LANES).transpose(1, 0, 2)
    block_id = lat_pos * lon_count + lon_pos
    offset = (token_index // cells) * piece + token_index % cells - block_id * piece

    lat_a, lat_b = partners(lat_count, 0, False), partners(lat_count, 1, False)
    lon_a, lon_b = partners(lon_count, 0, True), partners(lon_count, 1, True)
    if ens == 2:
        given = lax.dynamic_slice_in_dim(members, (1 - ens_pos) * own_channels, own_channels, 1)
        kept = lax.dynamic_slice_in_dim(members, ens_pos * own_channels, own_channels, 1)
        taken = lax.ppermute(given, "ens", [(0, 1), (1, 0)])
        w = [kept, taken]
    else:
        w = [lax.all_to_all(members, "ens", split_axis=1, concat_axis=0, tiled=True)]
    w_a, w_b = [], []
    for block in w:
        w_a.append(lax.ppermute(block, "lat", lat_a))
        w_b.append(lax.ppermute(block, "lat", lat_b))
    count = len(w) * w[0].shape[0]
    per = max(1, slots // count)

    strips = jax.ShapeDtypeStruct((max(1, count // slots), own_channels // per, rows, LANES), BF16)
    smem = pl.BlockSpec(memory_space=pltpu.SMEM)
    strip_a, strip_b, lon_both, lat = pl.pallas_call(
        functools.partial(prepare_kernel, strip, slots, lat_count, len(w)),
        out_shape=(
            strips,
            strips,
            jax.ShapeDtypeStruct((2 * LANES, 2 * cols), BF16),
            jax.ShapeDtypeStruct((3 * rows, 3 * rows), BF16),
        ),
        in_specs=whole(len(w)) + [smem] * 2, out_specs=whole(4), name="prepare",
        compiler_params=pltpu.CompilerParams(vmem_limit_bytes=GRANT),
    )(*w, lat_taps, lon_taps)
    strip_a = lax.ppermute(strip_a, "lon", lon_a)
    strip_b = lax.ppermute(strip_b, "lon", lon_b)

    padded = -(-own_channels // slots) * slots
    edges = jax.ShapeDtypeStruct((padded // slots, rows, LANES), BF16)
    grid, grid_a, grid_b = pl.pallas_call(
        functools.partial(gather_kernel, strip, slots),
        out_shape=(jax.ShapeDtypeStruct((own_channels, rows, cols), BF16), edges, edges),
        in_specs=whole(2), out_specs=whole(3),
        scratch_shapes=[pltpu.VMEM((padded, rows, cols), F32)], name="gather",
        compiler_params=pltpu.CompilerParams(vmem_limit_bytes=GRANT),
    )(moved, offset)
    grid_a = lax.ppermute(grid_a, "lon", lon_a)
    grid_b = lax.ppermute(grid_b, "lon", lon_b)

    out_a, out, out_b = smooth_call(strip, slots, count, rows, cols, len(w), 0, own_channels)(
        *w, *w_a, *w_b, strip_a, strip_b, grid, grid_a, grid_b, lon_both, lat
    )
    out = out + lax.ppermute(out_a, "lat", lat_a) + lax.ppermute(out_b, "lat", lat_b)
    return out / (count - 1)


def solution(mesh):
    in_specs = (P(None, ("lat", "lon")), P("lat", "lon"), P("ens", None, "lat", "lon"), P(), P())
    out_specs = P("ens", "lat", "lon")

    return jax.shard_map(local, mesh=mesh, in_specs=in_specs, out_specs=out_specs, check_vma=False)
```

time: 66.9 us -> 50.5 us (0.75)
  the two profiles are of different devices: /device:TPU:0 before, /device:TPU:8 now
where the time goes in v3:
time: 50.5 us; the launch traced here: 50.1 us
  starting transfers between devices  24 us (48%)
  waiting for transfers between devices  13.3 us (26%)
  Pallas kernels  7.03 us (14%)
  local copies, waits for them, and re-layouts  4.16 us (8%)
  other arithmetic  1.45 us (3%)
    ppermute x2, starting transfers between devices, local(): w_b.append(lax.ppermute(block, 'lat', lat_b))  6.86 us
    all_to_all x1, starting transfers between devices, local(): lax.all_to_all(tokens, ('lat', 'lon'), split_axis=0, concat_axis=0, tiled...  6.51 us
    ppermute x1, waiting for transfers between devices, local(): lax.ppermute(out_b, 'lat', lat_b)  3.78 us
    ppermute x1, waiting for transfers between devices, local(): lax.ppermute(out_a, 'lat', lat_a)  3.78 us
    ppermute x1, waiting for transfers between devices, local(): grid_b = lax.ppermute(grid_b, 'lon', lon_b)  3.3 us
    ppermute x1, starting transfers between devices, local(): lax.ppermute(out_b, 'lat', lat_b)  2.44 us
    pallas_call x1, Pallas kernels, local(): smooth_call(strip, slots, count, rows, cols, len(w), 0, own_channels)  2.43 us
    ppermute x1, waiting for transfers between devices, local(): grid_a = lax.ppermute(grid_a, 'lon', lon_a)  2.41 us
  transfers between devices with their start and end apart: 12, of which 4 were waited for; matrix products, arithmetic and copies ran while one was open for 3% of the time, Pallas kernels for 9%

profile of v3, /device:TPU:8, one launch (start us, length us, event | category | flops | bytes accessed | tf_op | source)
XLA Modules:
  0.0 50.1 jit_solution(5307166942374183806)
XLA Ops:
  0.0 1.3 %constant_dynamic-slice_fusion.1 = (bf16[2,52,16,128]{3,2,1,0:T(8,128)(2,1)S(1)}, bf16[2,52,16,128]{3,2,1,0:T(8,128)(2,1)S(1)}) fusion(bf16[2,104,16,128]{3,2,1,0:T(8,128)(2,1)} %param.7, s32[]{:T(128)S(6)} %select_n.20, s32[]{:T(128)S(6)} %select_n.19), kind=kLoop, calls=%fused_computation.16 | loop fusion | bytes 1703944 | tf_op jit(solution)/shard_map/dynamic_slice | solution.py:247
  1.3 0.1 collective-permute-start
  1.4 3.5 %collective-permute-start.3 = (bf16[2,52,16,128]{3,2,1,0:T(8,128)(2,1)S(1)}, bf16[2,52,16,128]{3,2,1,0:T(8,128)(2,1)S(1)}, u32[]{:S(2)}, u32[]{:S(2)}) collective-permute-start(bf16[2,52,16,128]{3,2,1,0:T(8,128)(2,1)S(1)} %get-tuple-element.26.refs_0_), channel_id=1, source_target_pairs={{4,8},{8,4},{5,9},{9,5},{6,10},{10,6},{7,11},{11,7},{20,24},{24,20... | collective-permute-start | bytes 1277960 | tf_op jit(solution)/shard_map/ppermute | solution.py:256
  4.9 0.1 collective-permute-start.1
  5.0 0.1 constant_dynamic-slice_fusion
  5.1 0.7 %copy.9 = bf16[52,16,128]{2,0,1:T(8,128)(2,1)} copy(bf16[52,16,128]{2,1,0:T(8,128)(2,1)S(1)} %slice) | data formatting | bytes 425984 | tf_op jit(solution)/shard_map/reshape | solution.py:237
  5.9 6.5 %all-to-all-start = ((bf16[16,52,128]{2,1,0:T(8,128)(2,1)}), bf16[16,52,128]{2,1,0:T(8,128)(2,1)S(1)}, u32[]{:S(2)}, u32[]{:S(2)}) async-start(bf16[16,52,128]{2,1,0:T(8,128)(2,1)} %bitcast.5), calls=%async_computation | async-start | bytes 458752 | tf_op jit(solution)/shard_map/all_to_all | solution.py:238
  12.4 0.0 collective-permute-done.refs_1_
  12.4 3.4 %collective-permute-start.4 = (bf16[2,52,16,128]{3,2,1,0:T(8,128)(2,1)S(1)}, bf16[2,52,16,128]{3,2,1,0:T(8,128)(2,1)S(1)}, u32[]{:S(2)}, u32[]{:S(2)}) collective-permute-start(bf16[2,52,16,128]{3,2,1,0:T(8,128)(2,1)S(1)} %collective-permute-done.refs_1_), channel_id=1, source_target_pairs={{4,8},{8,4},{5,9},{9,5},{6,10},{10,6},{7,11},{11,7},{20,24},{24,20... | collective-permute-start | bytes 1277960 | tf_op jit(solution)/shard_map/ppermute | solution.py:256
  15.8 0.1 collective-permute-start.2
  15.9 0.0 copy-start.4
  15.9 0.0 copy-start.5
  15.9 0.6 %copy-done.4 = f32[17]{0:T(128)S(1)} copy-done((f32[17]{0:T(128)S(1)}, f32[17]{0:T(128)}, u32[]{:S(2)}) %copy-start.4) | copy-done | bytes 92
  16.5 0.0 copy-done.5
  16.6 2.3 %prepare.1 = (bf16[1,26,16,128]{3,2,1,0:T(8,128)(2,1)}, bf16[1,26,16,128]{3,2,1,0:T(8,128)(2,1)}, bf16[256,256]{1,0:T(8,128)(2,1)S(1)}, bf16[48,48]{1,0:T(8,128)(2,1)S(1)}) custom-call(bf16[2,52,16,128]{3,2,1,0:T(8,128)(2,1)S(1)} %get-tuple-element.26.refs_0_, bf16[2,52,16,128]{3,2,1,0:T(8,128)(2,1)S(1)} %collective-permute-done.refs_1_, f32[17]{0:T(128)S(1)} %copy-done.4, ...), custom_call_target="tpu_custom_call" | custom-call | tf_op jit(solution)/shard_map/prepare/pallas_call | solution.py:262
  18.9 0.6 %copy-done.2 = bf16[48,48]{1,0:T(8,128)(2,1)} copy-done((bf16[48,48]{1,0:T(8,128)(2,1)}, bf16[48,48]{1,0:T(8,128)(2,1)S(1)}, u32[]{:S(2)}) %copy-start.2) | copy-done | bytes 4632
  19.5 1.5 %collective-permute-start.5 = (bf16[1,26,16,128]{3,2,1,0:T(8,128)(2,1)}, bf16[1,26,16,128]{3,2,1,0:T(8,128)(2,1)S(1)}, u32[]{:S(2)}, u32[]{:S(2)}) collective-permute-start(bf16[1,26,16,128]{3,2,1,0:T(8,128)(2,1)} %get-tuple-element.15), channel_id=1, source_target_pairs={{0,1},{1,0},{2,3},{3,2},{4,5},{5,4},{6,7},{7,6},{8,9},{9,8},{10,11... | collective-permute-start | bytes 319496 | tf_op jit(solution)/shard_map/ppermute | solution.py:273
  21.0 0.0 collective-permute-done.3.refs_4_
  21.0 1.5 %collective-permute-start.6 = (bf16[1,26,16,128]{3,2,1,0:T(8,128)(2,1)}, bf16[1,26,16,128]{3,2,1,0:T(8,128)(2,1)S(1)}, u32[]{:S(2)}, u32[]{:S(2)}) collective-permute-start(bf16[1,26,16,128]{3,2,1,0:T(8,128)(2,1)} %get-tuple-element.16), channel_id=1, source_target_pairs={{0,3},{1,2},{2,1},{3,0},{4,7},{5,6},{6,5},{7,4},{8,11},{9,10},{10,... | collective-permute-start | bytes 319496 | tf_op jit(solution)/shard_map/ppermute | solution.py:274
  22.4 0.6 %fusion.2.offset_ref = s32[16,128]{1,0:T(8,128)} fusion(s32[16,128]{1,0:T(8,128)S(1)} %copy-done.6, s32[]{:T(128)S(6)} %mul.24), kind=kLoop, calls=%fused_computation.9 | loop fusion | flops 45056 | bytes 16388 | tf_op jit(solution)/shard_map/sub | solution.py:242
  23.0 0.7 %copy-done.1 = s32[16,128]{1,0:T(8,128)S(1)} copy-done((s32[16,128]{1,0:T(8,128)S(1)}, s32[16,128]{1,0:T(8,128)}, u32[]{:S(2)}) %copy-start.1) | copy-done | bytes 8216
  23.7 2.3 %gather.1 = (bf16[52,16,128]{2,1,0:T(8,128)(2,1)S(1)}, bf16[7,16,128]{2,1,0:T(8,128)(2,1)S(1)}, bf16[7,16,128]{2,1,0:T(8,128)(2,1)S(1)}) custom-call(bf16[16,52,128]{2,1,0:T(8,128)(2,1)S(1)} %all-to-all-done.moved_ref, s32[16,128]{1,0:T(8,128)S(1)} %copy-done.1), custom_call_target="tpu_custom_call" | custom-call | tf_op jit(solution)/shard_map/gather/pallas_call | solution.py:278
  26.0 1.5 %collective-permute-start.7 = (bf16[7,16,128]{2,1,0:T(8,128)(2,1)S(1)}, bf16[7,16,128]{2,1,0:T(8,128)(2,1)S(1)}, u32[]{:S(2)}, u32[]{:S(2)}) collective-permute-start(bf16[7,16,128]{2,1,0:T(8,128)(2,1)S(1)} %get-tuple-element.18), channel_id=1, source_target_pairs={{0,1},{1,0},{2,3},{3,2},{4,5},{5,4},{6,7},{7,6},{8,9},{9,8},{10,11... | collective-permute-start | bytes 86024 | tf_op jit(solution)/shard_map/ppermute | solution.py:285
  27.5 2.4 %collective-permute-done.7.refs_9_ = bf16[7,16,128]{2,1,0:T(8,128)(2,1)S(1)} collective-permute-done((bf16[7,16,128]{2,1,0:T(8,128)(2,1)S(1)}, bf16[7,16,128]{2,1,0:T(8,128)(2,1)S(1)}, u32[]{:S(2)}, u32[]{:S(2)}) %collective-permute-start.7) | collective-permute-done | bytes 28704 | tf_op jit(solution)/shard_map/ppermute | solution.py:285
  30.0 1.5 %collective-permute-start.8 = (bf16[7,16,128]{2,1,0:T(8,128)(2,1)S(1)}, bf16[7,16,128]{2,1,0:T(8,128)(2,1)S(1)}, u32[]{:S(2)}, u32[]{:S(2)}) collective-permute-start(bf16[7,16,128]{2,1,0:T(8,128)(2,1)S(1)} %get-tuple-element.19), channel_id=1, source_target_pairs={{0,3},{1,2},{2,1},{3,0},{4,7},{5,6},{6,5},{7,4},{8,11},{9,10},{10,... | collective-permute-start | bytes 86024 | tf_op jit(solution)/shard_map/ppermute | solution.py:286
  31.4 3.3 %collective-permute-done.8.refs_10_ = bf16[7,16,128]{2,1,0:T(8,128)(2,1)S(1)} collective-permute-done((bf16[7,16,128]{2,1,0:T(8,128)(2,1)S(1)}, bf16[7,16,128]{2,1,0:T(8,128)(2,1)S(1)}, u32[]{:S(2)}, u32[]{:S(2)}) %collective-permute-start.8) | collective-permute-done | bytes 28704 | tf_op jit(solution)/shard_map/ppermute | solution.py:286
  34.8 2.4 %smooth.1 = (f32[52,16,128]{2,1,0:T(8,128)S(1)}, f32[52,16,128]{2,1,0:T(8,128)S(1)}, f32[52,16,128]{2,1,0:T(8,128)S(1)}) custom-call(bf16[2,52,16,128]{3,2,1,0:T(8,128)(2,1)S(1)} %get-tuple-element.26.refs_0_, bf16[2,52,16,128]{3,2,1,0:T(8,128)(2,1)S(1)} %collective-permute-done.refs_1_, bf16[2,52,16,128]{3,2,1,0:T(8,128)(2,1)S(1)} %collective-permute-done.1.refs_2_, ...), custom_call_target="tpu_custom_call" | custom-call | tf_op jit(solution)/shard_map/smooth/pallas_call | solution.py:288
  37.2 2.1 %collective-permute-start.9 = (f32[52,16,128]{2,1,0:T(8,128)S(1)}, f32[52,16,128]{2,1,0:T(8,128)S(1)}, u32[]{:S(2)}, u32[]{:S(2)}) collective-permute-start(f32[52,16,128]{2,1,0:T(8,128)S(1)} %get-tuple-element.23), channel_id=1, source_target_pairs={{0,4},{4,0},{8,12},{12,8},{1,5},{5,1},{9,13},{13,9},{2,6},{6,2},{1... | collective-permute-start | bytes 1277960 | tf_op jit(solution)/shard_map/ppermute | solution.py:291
  39.3 2.4 %collective-permute-start.10 = (f32[52,16,128]{2,1,0:T(8,128)S(1)}, f32[52,16,128]{2,1,0:T(8,128)S(1)}, u32[]{:S(2)}, u32[]{:S(2)}) collective-permute-start(f32[52,16,128]{2,1,0:T(8,128)S(1)} %get-tuple-element.24), channel_id=1, source_target_pairs={{4,8},{8,4},{5,9},{9,5},{6,10},{10,6},{7,11},{11,7},{20,24},{24,20... | collective-permute-start | bytes 1277960 | tf_op jit(solution)/shard_map/ppermute | solution.py:291
  41.7 3.8 %collective-permute-done.9 = f32[52,16,128]{2,1,0:T(8,128)S(1)} collective-permute-done((f32[52,16,128]{2,1,0:T(8,128)S(1)}, f32[52,16,128]{2,1,0:T(8,128)S(1)}, u32[]{:S(2)}, u32[]{:S(2)}) %collective-permute-start.9) | collective-permute-done | bytes 426016 | tf_op jit(solution)/shard_map/ppermute | solution.py:291
  45.5 3.8 %collective-permute-done.10 = f32[52,16,128]{2,1,0:T(8,128)S(1)} collective-permute-done((f32[52,16,128]{2,1,0:T(8,128)S(1)}, f32[52,16,128]{2,1,0:T(8,128)S(1)}, u32[]{:S(2)}, u32[]{:S(2)}) %collective-permute-start.10) | collective-permute-done | bytes 426016 | tf_op jit(solution)/shard_map/ppermute | solution.py:291
  49.3 0.8 %add_multiply_fusion = f32[52,16,128]{2,1,0:T(8,128)} fusion(f32[52,16,128]{2,1,0:T(8,128)S(1)} %collective-permute-done.10, f32[52,16,128]{2,1,0:T(8,128)S(1)} %get-tuple-element.22, f32[52,16,128]{2,1,0:T(8,128)S(1)} %collective-permute-done.9), kind=kLoop, calls=%fused_computation | loop fusion | flops 319488 | bytes 1703936 | tf_op jit(solution)/shard_map/div | solution.py:292
  (16 shorter events, 0.1 us)
Async XLA Ops:
  0.0 5.0 %copy-start = (bf16[104,2048]{1,0:T(8,128)(2,1)S(1)}, bf16[104,2048]{1,0:T(8,128)(2,1)}, u32[]{:S(2)}) copy-start(bf16[104,2048]{1,0:T(8,128)(2,1)} %param.5) | copy-start | bytes 1277956
  1.3 11.1 %collective-permute-start = (bf16[2,52,16,128]{3,2,1,0:T(8,128)(2,1)S(1)}, bf16[2,52,16,128]{3,2,1,0:T(8,128)(2,1)S(1)}, u32[]{:S(2)}, u32[]{:S(2)}) collective-permute-start(bf16[2,52,16,128]{3,2,1,0:T(8,128)(2,1)S(1)} %get-tuple-element.25), channel_id=1, source_target_pairs={{0,16},{16,0},{1,17},{17,1},{2,18},{18,2},{3,19},{19,3},{4,20},{20... | collective-permute-start | bytes 1277960 | tf_op jit(solution)/shard_map/ppermute | solution.py:249
  1.4 19.5 %collective-permute-start.3 = (bf16[2,52,16,128]{3,2,1,0:T(8,128)(2,1)S(1)}, bf16[2,52,16,128]{3,2,1,0:T(8,128)(2,1)S(1)}, u32[]{:S(2)}, u32[]{:S(2)}) collective-permute-start(bf16[2,52,16,128]{3,2,1,0:T(8,128)(2,1)S(1)} %get-tuple-element.26.refs_0_), channel_id=1, source_target_pairs={{4,8},{8,4},{5,9},{9,5},{6,10},{10,6},{7,11},{11,7},{20,24},{24,20... | collective-permute-start | bytes 1277960 | tf_op jit(solution)/shard_map/ppermute | solution.py:256
  4.9 21.1 %collective-permute-start.1 = (bf16[2,52,16,128]{3,2,1,0:T(8,128)(2,1)S(1)}, bf16[2,52,16,128]{3,2,1,0:T(8,128)(2,1)S(1)}, u32[]{:S(2)}, u32[]{:S(2)}) collective-permute-start(bf16[2,52,16,128]{3,2,1,0:T(8,128)(2,1)S(1)} %get-tuple-element.26.refs_0_), channel_id=1, source_target_pairs={{0,4},{4,0},{8,12},{12,8},{1,5},{5,1},{9,13},{13,9},{2,6},{6,2},{1... | collective-permute-start | bytes 1277960 | tf_op jit(solution)/shard_map/ppermute | solution.py:255
  5.9 17.1 %all-to-all-start = ((bf16[16,52,128]{2,1,0:T(8,128)(2,1)}), bf16[16,52,128]{2,1,0:T(8,128)(2,1)S(1)}, u32[]{:S(2)}, u32[]{:S(2)}) async-start(bf16[16,52,128]{2,1,0:T(8,128)(2,1)} %bitcast.5), calls=%async_computation | async-start | bytes 458752 | tf_op jit(solution)/shard_map/all_to_all | solution.py:238
  12.4 22.3 %collective-permute-start.4 = (bf16[2,52,16,128]{3,2,1,0:T(8,128)(2,1)S(1)}, bf16[2,52,16,128]{3,2,1,0:T(8,128)(2,1)S(1)}, u32[]{:S(2)}, u32[]{:S(2)}) collective-permute-start(bf16[2,52,16,128]{3,2,1,0:T(8,128)(2,1)S(1)} %collective-permute-done.refs_1_), channel_id=1, source_target_pairs={{4,8},{8,4},{5,9},{9,5},{6,10},{10,6},{7,11},{11,7},{20,24},{24,20... | collective-permute-start | bytes 1277960 | tf_op jit(solution)/shard_map/ppermute | solution.py:256
  15.8 18.9 %collective-permute-start.2 = (bf16[2,52,16,128]{3,2,1,0:T(8,128)(2,1)S(1)}, bf16[2,52,16,128]{3,2,1,0:T(8,128)(2,1)S(1)}, u32[]{:S(2)}, u32[]{:S(2)}) collective-permute-start(bf16[2,52,16,128]{3,2,1,0:T(8,128)(2,1)S(1)} %collective-permute-done.refs_1_), channel_id=1, source_target_pairs={{0,4},{4,0},{8,12},{12,8},{1,5},{5,1},{9,13},{13,9},{2,6},{6,2},{1... | collective-permute-start | bytes 1277960 | tf_op jit(solution)/shard_map/ppermute | solution.py:255
  15.9 0.7 %copy-start.4 = (f32[17]{0:T(128)S(1)}, f32[17]{0:T(128)}, u32[]{:S(2)}) copy-start(f32[17]{0:T(128)} %refs_2_.1) | copy-start | bytes 208
  15.9 0.7 %copy-start.5 = (f32[17]{0:T(128)S(1)}, f32[17]{0:T(128)}, u32[]{:S(2)}) copy-start(f32[17]{0:T(128)} %refs_3_.1) | copy-start | bytes 208
  16.6 5.9 %copy-start.6 = (s32[16,128]{1,0:T(8,128)S(1)}, s32[16,128]{1,0:T(8,128)}, u32[]{:S(2)}) copy-start(s32[16,128]{1,0:T(8,128)} %param.6) | copy-start | bytes 24580
  18.9 0.6 %copy-start.2 = (bf16[48,48]{1,0:T(8,128)(2,1)}, bf16[48,48]{1,0:T(8,128)(2,1)S(1)}, u32[]{:S(2)}) copy-start(bf16[48,48]{1,0:T(8,128)(2,1)S(1)} %get-tuple-element.21.refs_12_) | copy-start | bytes 13828
  19.5 15.2 %collective-permute-start.5 = (bf16[1,26,16,128]{3,2,1,0:T(8,128)(2,1)}, bf16[1,26,16,128]{3,2,1,0:T(8,128)(2,1)S(1)}, u32[]{:S(2)}, u32[]{:S(2)}) collective-permute-start(bf16[1,26,16,128]{3,2,1,0:T(8,128)(2,1)} %get-tuple-element.15), channel_id=1, source_target_pairs={{0,1},{1,0},{2,3},{3,2},{4,5},{5,4},{6,7},{7,6},{8,9},{9,8},{10,11... | collective-permute-start | bytes 319496 | tf_op jit(solution)/shard_map/ppermute | solution.py:273
  21.0 13.8 %collective-permute-start.6 = (bf16[1,26,16,128]{3,2,1,0:T(8,128)(2,1)}, bf16[1,26,16,128]{3,2,1,0:T(8,128)(2,1)S(1)}, u32[]{:S(2)}, u32[]{:S(2)}) collective-permute-start(bf16[1,26,16,128]{3,2,1,0:T(8,128)(2,1)} %get-tuple-element.16), channel_id=1, source_target_pairs={{0,3},{1,2},{2,1},{3,0},{4,7},{5,6},{6,5},{7,4},{8,11},{9,10},{10,... | collective-permute-start | bytes 319496 | tf_op jit(solution)/shard_map/ppermute | solution.py:274
  23.0 0.7 %copy-start.1 = (s32[16,128]{1,0:T(8,128)S(1)}, s32[16,128]{1,0:T(8,128)}, u32[]{:S(2)}) copy-start(s32[16,128]{1,0:T(8,128)} %fusion.2.offset_ref) | copy-start | bytes 24580
  23.7 11.0 %copy-start.3 = (bf16[48,48]{1,0:T(8,128)(2,1)S(1)}, bf16[48,48]{1,0:T(8,128)(2,1)}, u32[]{:S(2)}) copy-start(bf16[48,48]{1,0:T(8,128)(2,1)} %copy-done.2) | copy-start | bytes 13828
  26.0 3.9 %collective-permute-start.7 = (bf16[7,16,128]{2,1,0:T(8,128)(2,1)S(1)}, bf16[7,16,128]{2,1,0:T(8,128)(2,1)S(1)}, u32[]{:S(2)}, u32[]{:S(2)}) collective-permute-start(bf16[7,16,128]{2,1,0:T(8,128)(2,1)S(1)} %get-tuple-element.18), channel_id=1, source_target_pairs={{0,1},{1,0},{2,3},{3,2},{4,5},{5,4},{6,7},{7,6},{8,9},{9,8},{10,11... | collective-permute-start | bytes 86024 | tf_op jit(solution)/shard_map/ppermute | solution.py:285
  30.0 4.8 %collective-permute-start.8 = (bf16[7,16,128]{2,1,0:T(8,128)(2,1)S(1)}, bf16[7,16,128]{2,1,0:T(8,128)(2,1)S(1)}, u32[]{:S(2)}, u32[]{:S(2)}) collective-permute-start(bf16[7,16,128]{2,1,0:T(8,128)(2,1)S(1)} %get-tuple-element.19), channel_id=1, source_target_pairs={{0,3},{1,2},{2,1},{3,0},{4,7},{5,6},{6,5},{7,4},{8,11},{9,10},{10,... | collective-permute-start | bytes 86024 | tf_op jit(solution)/shard_map/ppermute | solution.py:286
  37.2 8.3 %collective-permute-start.9 = (f32[52,16,128]{2,1,0:T(8,128)S(1)}, f32[52,16,128]{2,1,0:T(8,128)S(1)}, u32[]{:S(2)}, u32[]{:S(2)}) collective-permute-start(f32[52,16,128]{2,1,0:T(8,128)S(1)} %get-tuple-element.23), channel_id=1, source_target_pairs={{0,4},{4,0},{8,12},{12,8},{1,5},{5,1},{9,13},{13,9},{2,6},{6,2},{1... | collective-permute-start | bytes 1277960 | tf_op jit(solution)/shard_map/ppermute | solution.py:291
  39.3 10.0 %collective-permute-start.10 = (f32[52,16,128]{2,1,0:T(8,128)S(1)}, f32[52,16,128]{2,1,0:T(8,128)S(1)}, u32[]{:S(2)}, u32[]{:S(2)}) collective-permute-start(f32[52,16,128]{2,1,0:T(8,128)S(1)} %get-tuple-element.24), channel_id=1, source_target_pairs={{4,8},{8,4},{5,9},{9,5},{6,10},{10,6},{7,11},{11,7},{20,24},{24,20... | collective-permute-start | bytes 1277960 | tf_op jit(solution)/shard_map/ppermute | solution.py:291

commit v4 on v3

v4 whole, which is shorter than its diff:
```python
import functools

import jax
import jax.numpy as jnp
from jax import lax
from jax.experimental import pallas as pl
from jax.experimental.pallas import tpu as pltpu
from jax.sharding import PartitionSpec as P


LANES = 128
F32 = jnp.float32
BF16 = jnp.bfloat16
UNIT = 7
STEPS = 32760.0
GRANT = 24 << 20


def whole(n):
    return [pl.BlockSpec(memory_space=pltpu.VMEM)] * n


def dot(a, b):
    return lax.dot_general(a, b, (((1,), (0,)), ((), ())), preferred_element_type=F32)


def split(v):
    hi = v.astype(BF16)
    return hi, (v - hi.astype(F32)).astype(BF16)


def band(taps, offset):
    total = jnp.zeros(offset.shape, F32)
    for k, tap in enumerate(taps):
        total = jnp.where(offset == k, tap, total)
    return total


def fill_matrices(strip, lat_count, rows, lat_taps_ref, lon_taps_ref, matrix_ref):
    cols = matrix_ref.shape[1] // 2
    count = lon_taps_ref.shape[0]
    iota = lax.broadcasted_iota
    taps = [lon_taps_ref[k] for k in range(count)]
    half = [sum(taps[a] * taps[a - d] for a in range(d, count)) for d in range(count)]
    both = half[:0:-1] + half
    place = iota(jnp.int32, (2 * LANES, cols), 0)
    inner = place % strip
    even = lax.rem(lax.axis_index("lon"), 2) == 0
    after = (place < cols + LANES // 2) == even
    source = jnp.where(place < cols, place, jnp.where(after, cols + inner, inner - strip))
    hi, lo = split(band(both, source - iota(jnp.int32, (2 * LANES, cols), 1) + count - 1))
    matrix_ref[: 2 * LANES, :] = jnp.concatenate([hi, lo], axis=1)
    count = lat_taps_ref.shape[0]
    radius = (count - 1) // 2
    taps = [lat_taps_ref[k] for k in range(count)]
    middle = rows + 2 * radius
    toward = jnp.where(lax.rem(lax.axis_index("lat"), 2) == 0, rows, -rows)
    place = iota(jnp.int32, (3 * rows, middle), 0)
    out_row = place % rows + (1 - place // rows) * toward
    mid_row = iota(jnp.int32, (3 * rows, middle), 1) - radius
    spread = band(taps, mid_row - out_row + radius)
    mid_row = iota(jnp.int32, (middle, rows), 0) - radius
    gather = band(taps[::-1], iota(jnp.int32, (middle, rows), 1) - mid_row + radius)
    whole_row = lax.axis_index("lat") * rows + mid_row
    gather = jnp.where((whole_row >= 0) & (whole_row < lat_count * rows), gather, 0.0)
    hi, lo = split(jnp.dot(spread, gather, precision=lax.Precision.HIGHEST, preferred_element_type=F32))
    matrix_ref[2 * LANES :, : 3 * rows] = jnp.concatenate([hi, lo, hi], axis=1)


def pick_matrix(slot, strip, cols):
    even = lax.rem(lax.axis_index("lon"), 2) == 0
    last = cols - strip
    lane = lax.broadcasted_iota(jnp.int32, (cols, 2 * LANES), 1)
    row = lax.broadcasted_iota(jnp.int32, (cols, 2 * LANES), 0)
    first = jnp.where((lane < LANES) == even, last, 0)
    chosen = (lane % LANES // strip == slot) & (row == first + lane % strip)
    return jnp.where(chosen, 1.0, 0.0).astype(BF16)


def prepare_kernel(strip, slots, lat_count, parts, *refs):
    w_refs, (lat_taps_ref, lon_taps_ref, a_ref, b_ref, matrix_ref) = refs[:parts], refs[parts:]
    each, channels, rows, cols = w_refs[0].shape
    fill_matrices(strip, lat_count, rows, lat_taps_ref, lon_taps_ref, matrix_ref)
    members = each * parts
    per = max(1, slots // members)
    for h in range(max(1, members // slots)):
        total = None
        for k in range(slots):
            c2, m = (k // members, k % members) if members <= slots else (0, h * slots + k)
            plane = w_refs[m // each][m % each].reshape(channels // per, per, rows, cols)[:, c2]
            part = dot(plane.reshape(-1, cols), pick_matrix(k, strip, cols))
            total = part if total is None else total + part
        total = total.astype(BF16)
        a_ref[h] = total[:, :LANES].reshape(channels // per, rows, LANES)
        b_ref[h] = total[:, LANES:].reshape(channels // per, rows, LANES)


def gather_kernel(strip, slots, lon_count, piece, moved_ref, index_ref, grid_ref, a_ref, b_ref, scratch):
    pieces, channels, width = moved_ref.shape
    rows, cols = index_ref.shape
    cells = rows * cols
    block = lax.axis_index("lat") * lon_count + lax.axis_index("lon")
    index = index_ref[...]
    offset = lax.div(index, cells) * piece + lax.rem(index, cells) - block * piece
    scratch[channels:] = jnp.zeros((scratch.shape[0] - channels, rows, cols), F32)
    tokens = jnp.concatenate([moved_ref[n] for n in range(pieces)], axis=1)
    token = lax.broadcasted_iota(jnp.int32, (pieces * width, 2 * cols), 0)
    for i in range(0, rows, 2):
        wanted = jnp.concatenate([offset[i : i + 1], offset[i + 1 : i + 2]], axis=1)
        chosen = jnp.where(token == wanted, 1.0, 0.0).astype(BF16)
        found = dot(tokens, chosen)
        scratch[:channels, i, :] = found[:, :cols]
        scratch[:channels, i + 1, :] = found[:, cols:]
    grid = scratch[...].astype(BF16)
    grid_ref[...] = grid[:channels]
    groups = scratch.shape[0] // slots
    planes = grid.reshape(groups, slots, rows, cols)
    total = None
    for k in range(slots):
        part = dot(planes[:, k].reshape(-1, cols), pick_matrix(k, strip, cols))
        total = part if total is None else total + part
    total = total.astype(BF16)
    a_ref[...] = total[:, :LANES].reshape(groups, rows, LANES)
    b_ref[...] = total[:, LANES:].reshape(groups, rows, LANES)


class Planes:
    def __init__(self, slots, members, channels):
        self.slots, self.members = slots, members
        self.per, self.folds = max(1, slots // members), max(1, members // slots)
        self.groups = channels // self.per * self.folds

    def place(self, n):
        first, h = n // self.folds * self.per, n % self.folds
        if self.folds == 1:
            return first, h, [(k // self.members, k % self.members) for k in range(self.slots)]
        return first, h, [(0, h * self.slots + k) for k in range(self.slots)]

    def stages(self, unit, *steps):
        units = [range(n, min(n + unit, self.groups)) for n in range(0, self.groups, unit)]
        for n in range(len(units) + len(steps) - 1):
            for behind, step in enumerate(steps):
                if 0 <= n - behind < len(units):
                    step(units[n - behind])


def member(refs, m, c):
    each = refs[0].shape[0]
    return refs[m // each][m % each, c].astype(F32)


def inner_kernel(slots, unit, parts, *refs):
    own_refs, (grid_ref, matrix_ref, part_ref, hi_ref, lo_ref) = refs[:parts], refs[parts:]
    each, channels, rows, cols = own_refs[0].shape
    planes = Planes(slots, each * parts, channels)
    height = slots * rows

    def weigh(unit):
        for n in unit:
            first, _, where = planes.place(n)
            for k, (c, m) in enumerate(where):
                at = pl.ds(n * height + k * rows, rows)
                product = member(own_refs, m, first + c) * grid_ref[first + c].astype(F32)
                hi_ref[at, :], lo_ref[at, :] = split(product)

    def along_lon(unit):
        at = pl.ds(unit[0] * height, len(unit) * height)
        big = dot(hi_ref[at, :], matrix_ref[:cols, :])
        small = dot(lo_ref[at, :], matrix_ref[:cols, :cols])
        part_ref[at, :] = big[:, :cols] + big[:, cols:] + small

    planes.stages(unit, weigh, along_lon)


def smooth_kernel(strip, slots, unit, parts, *refs):
    own_refs, a_refs, b_refs = (refs[n * parts : (n + 1) * parts] for n in range(3))
    (strip_a_ref, strip_b_ref, grid_a_ref, grid_b_ref, matrix_ref, part_ref) = refs[3 * parts : 3 * parts + 6]
    out_a_ref, out_ref, out_b_ref, hi_ref, lo_ref, mid_ref, sum_ref, scale_ref = refs[3 * parts + 6 :]
    each, channels, rows, cols = own_refs[0].shape
    members = each * parts
    planes = Planes(slots, members, channels)
    per, folds = planes.per, planes.folds
    half = LANES // 2
    height = slots * rows
    src = lax.broadcasted_iota(jnp.int32, (LANES, LANES), 0)
    dst = lax.broadcasted_iota(jnp.int32, (LANES, LANES), 1)
    dst_channel = dst // strip // members if folds == 1 else jnp.zeros_like(dst)
    lane = lax.broadcasted_iota(jnp.int32, (rows, LANES), 1)
    low = lane < half
    slot_of = (lane % half) // strip
    scale_ref[...] = jnp.zeros_like(scale_ref)

    def weigh(unit):
        for n in unit:
            first, h, _ = planes.place(n)
            expand = src == ((first + dst_channel) % slots) * strip + dst % strip
            expand = jnp.where(expand, 1.0, 0.0).astype(BF16)
            edge_a = strip_a_ref[h, first // per].astype(F32) * dot(grid_a_ref[first // slots], expand)
            edge_b = strip_b_ref[h, first // per].astype(F32) * dot(grid_b_ref[first // slots], expand)
            sides = (
                split(jnp.where(low, edge_a, pltpu.roll(edge_b, half, 1))),
                split(jnp.where(low, pltpu.roll(edge_a, half, 1), edge_b)),
            )
            for k in range(slots):
                side = sides[k * 2 // slots]
                keep = slot_of == k % (slots // 2)
                at = pl.ds(n * height + k * rows, rows)
                for p, ref in enumerate((hi_ref, lo_ref)):
                    ref[at, :] = jnp.where(keep, side[p], jnp.zeros_like(side[p]))

    def along_lon(unit):
        n, many = unit[0], len(unit)
        at = pl.ds(n * height, many * height)
        edge = pl.ds(cols, LANES)
        big = dot(hi_ref[at, :], matrix_ref[edge, :])
        small = dot(lo_ref[at, :], matrix_ref[edge, :cols])
        hi, lo = split(part_ref[at, :] + big[:, :cols] + big[:, cols:] + small)
        for k in range(many * slots):
            to = pl.ds((n * slots + k) * cols, cols)
            rest = slice(k * rows, (k + 1) * rows)
            mid_ref[:rows, to] = hi[rest]
            mid_ref[rows : 2 * rows, to] = hi[rest]
            mid_ref[2 * rows :, to] = lo[rest]

    def send(side, ref, c, total):
        level = code_of(jnp.max(jnp.abs(total), axis=0, keepdims=True))
        scale_ref[side, c : c + 1, :] = level
        ref[c] = to_int16(jnp.floor(total * (STEPS * scale_of(-level)) + 0.5))

    def along_lat(unit):
        for n in unit:
            first, h, where = planes.place(n)
            spread = dot(matrix_ref[cols + LANES :, : 3 * rows], mid_ref[:, pl.ds(n * slots * cols, slots * cols)])
            for r, weights in enumerate((a_refs, own_refs, b_refs)):
                sums = {}
                for k, (c, m) in enumerate(where):
                    piece = spread[r * rows : (r + 1) * rows, k * cols : (k + 1) * cols]
                    term = piece * member(weights, m, first + c)
                    sums[c] = sums[c] + term if c in sums else term
                for c, total in sums.items():
                    at = first + c
                    if h:
                        total = total + sum_ref[r, at]
                    if h < folds - 1:
                        sum_ref[r, at] = total
                    elif r == 1:
                        out_ref[at] = total
                    else:
                        send(r // 2, (out_a_ref, out_b_ref)[r // 2], at, total)

    planes.stages(unit, weigh, along_lon, along_lat)
    for side, ref in enumerate((out_a_ref, out_b_ref)):
        for n in range(channels, ref.shape[0]):
            at = pl.ds((n - channels) * rows, rows)
            ref[n] = to_int16(scale_ref[side, at, :])


def code_of(largest):
    return jnp.ceil(jnp.log2(jnp.maximum(largest, 1e-36)) * 64.0)


def scale_of(level):
    return jnp.exp2(level * (1.0 / 64.0))


def to_int16(v):
    return v.astype(jnp.int32).astype(jnp.int16)


def add_kernel(total, out_ref, a_ref, b_ref, sum_ref, scale_ref):
    channels, rows, _ = out_ref.shape
    for side, ref in enumerate((a_ref, b_ref)):
        for n in range(channels, ref.shape[0]):
            at = pl.ds((n - channels) * rows, rows)
            scale_ref[side, at, :] = scale_of(ref[n].astype(F32)) * (1.0 / STEPS)
    for c in range(channels):
        added = out_ref[c]
        for side, ref in enumerate((a_ref, b_ref)):
            added = added + ref[c].astype(F32) * scale_ref[side, c : c + 1, :]
        sum_ref[c] = added / total


def call(kernel, out_shape, scratch_shapes=(), smem=0):
    def run(*args):
        n = len(args) - smem
        return pl.pallas_call(
            kernel,
            out_shape=out_shape,
            in_specs=whole(n) + [pl.BlockSpec(memory_space=pltpu.SMEM)] * smem,
            out_specs=whole(len(out_shape)) if isinstance(out_shape, tuple) else whole(1)[0],
            scratch_shapes=scratch_shapes,
            compiler_params=pltpu.CompilerParams(vmem_limit_bytes=GRANT),
        )(*args)

    return run


def inner_call(slots, channels, members, rows, cols, parts):
    high = channels * members * rows
    return call(
        functools.partial(inner_kernel, slots, UNIT, parts),
        jax.ShapeDtypeStruct((high, cols), F32),
        [pltpu.VMEM((high, cols), BF16)] * 2,
    )


def smooth_call(strip, slots, channels, members, rows, cols, parts):
    high = channels * members * rows
    extra = -(-channels // rows)
    side = jax.ShapeDtypeStruct((channels + extra, rows, cols), jnp.int16)
    return call(
        functools.partial(smooth_kernel, strip, slots, UNIT, parts),
        (side, jax.ShapeDtypeStruct((channels, rows, cols), F32), side),
        [
            pltpu.VMEM((high, LANES), BF16),
            pltpu.VMEM((high, LANES), BF16),
            pltpu.VMEM((3 * rows, channels * members * cols), BF16),
            pltpu.VMEM((3, channels if members > slots else 1, rows, cols), F32),
            pltpu.VMEM((2, extra * rows, cols), F32),
        ],
    )


def add_call(total, channels, rows, cols):
    return call(
        functools.partial(add_kernel, total),
        jax.ShapeDtypeStruct((channels, rows, cols), F32),
        [pltpu.VMEM((2, -(-channels // rows) * rows, cols), F32)],
    )


def partners(count, first, closed):
    pairs = [(i, (i + 1) % count) for i in range(first, count if closed else count - 1, 2)]
    return sorted(set(pairs + [(j, i) for i, j in pairs]))


def local(grad_tokens, token_index, members, lat_taps, lon_taps):
    ens, lat_count, lon_count = (lax.axis_size(a) for a in ("ens", "lat", "lon"))
    ens_pos = lax.axis_index("ens")
    channels, cells = grad_tokens.shape
    rows, cols = token_index.shape
    own_channels = channels // ens
    blocks = lat_count * lon_count
    piece = cells // blocks
    strip = lon_taps.shape[0] - 1
    slots = LANES // strip
    assert cols == LANES and lon_count % 2 == 0 and lat_taps.shape[0] - 1 <= rows

    tokens = lax.dynamic_slice_in_dim(grad_tokens, ens_pos * own_channels, own_channels, 0)
    tokens = tokens.reshape(own_channels, blocks, piece).transpose(1, 0, 2)
    moved = lax.all_to_all(tokens, ("lat", "lon"), split_axis=0, concat_axis=0, tiled=True)
    if piece != LANES:
        moved = moved.transpose(1, 0, 2).reshape(own_channels, cells // LANES, LANES).transpose(1, 0, 2)

    lat_a, lat_b = partners(lat_count, 0, False), partners(lat_count, 1, False)
    lon_a, lon_b = partners(lon_count, 0, True), partners(lon_count, 1, True)
    if ens == 2:
        given = lax.dynamic_slice_in_dim(members, (1 - ens_pos) * own_channels, own_channels, 1)
        kept = lax.dynamic_slice_in_dim(members, ens_pos * own_channels, own_channels, 1)
        taken = lax.ppermute(given, "ens", [(0, 1), (1, 0)])
        w = [kept, taken]
    else:
        w = [lax.all_to_all(members, "ens", split_axis=1, concat_axis=0, tiled=True)]
    w_a, w_b = [], []
    for block in w:
        w_a.append(lax.ppermute(block, "lat", lat_a))
        w_b.append(lax.ppermute(block, "lat", lat_b))
    count = len(w) * w[0].shape[0]
    per = max(1, slots // count)

    strips = jax.ShapeDtypeStruct((max(1, count // slots), own_channels // per, rows, LANES), BF16)
    smem = pl.BlockSpec(memory_space=pltpu.SMEM)
    strip_a, strip_b, matrix = pl.pallas_call(
        functools.partial(prepare_kernel, strip, slots, lat_count, len(w)),
        out_shape=(
            strips,
            strips,
            jax.ShapeDtypeStruct((2 * LANES + 3 * rows, 2 * cols), BF16),
        ),
        in_specs=whole(len(w)) + [smem] * 2, out_specs=whole(3), name="prepare",
        compiler_params=pltpu.CompilerParams(vmem_limit_bytes=GRANT),
    )(*w, lat_taps, lon_taps)
    strip_a = lax.ppermute(strip_a, "lon", lon_a)
    strip_b = lax.ppermute(strip_b, "lon", lon_b)

    padded = -(-own_channels // slots) * slots
    edges = jax.ShapeDtypeStruct((padded // slots, rows, LANES), BF16)
    grid, grid_a, grid_b = pl.pallas_call(
        functools.partial(gather_kernel, strip, slots, lon_count, piece),
        out_shape=(jax.ShapeDtypeStruct((own_channels, rows, cols), BF16), edges, edges),
        in_specs=whole(2), out_specs=whole(3),
        scratch_shapes=[pltpu.VMEM((padded, rows, cols), F32)], name="gather",
        compiler_params=pltpu.CompilerParams(vmem_limit_bytes=GRANT),
    )(moved, token_index)
    grid_a = lax.ppermute(grid_a, "lon", lon_a)
    grid_b = lax.ppermute(grid_b, "lon", lon_b)

    sizes = (own_channels, count, rows, cols, len(w))
    part = inner_call(slots, *sizes)(*w, grid, matrix)
    out_a, out, out_b = smooth_call(strip, slots, *sizes)(
        *w, *w_a, *w_b, strip_a, strip_b, grid_a, grid_b, matrix, part
    )
    out_a = lax.ppermute(out_a, "lat", lat_a)
    out_b = lax.ppermute(out_b, "lat", lat_b)
    return add_call(count - 1, own_channels, rows, cols)(out, out_a, out_b)


def solution(mesh):
    in_specs = (P(None, ("lat", "lon")), P("lat", "lon"), P("ens", None, "lat", "lon"), P(), P())
    out_specs = P("ens", "lat", "lon")

    return jax.shard_map(local, mesh=mesh, in_specs=in_specs, out_specs=out_specs, check_vma=False)
```

time: 50.5 us -> 47.5 us (0.941)
  the two profiles are of different devices: /device:TPU:8 before, /device:TPU:16 now
where the time goes in v4:
time: 47.5 us; the launch traced here: 47.2 us
  starting transfers between devices  22.3 us (47%)
  waiting for transfers between devices  12.9 us (27%)
  Pallas kernels  9.62 us (20%)
  local copies, waits for them, and re-layouts  2.22 us (5%)
    all_to_all x1, starting transfers between devices, local(): lax.all_to_all(tokens, ('lat', 'lon'), split_axis=0, concat_axis=0, tiled...  7.53 us
    pallas_call x3, Pallas kernels, run(): pl.pallas_call(kernel, out_shape=out_shape, in_specs=whole(n) + [pl.Block...  4.95 us
    ppermute x2, starting transfers between devices, local(): w_b.append(lax.ppermute(block, 'lat', lat_b))  4.83 us
    ppermute x1, waiting for transfers between devices, local(): out_b = lax.ppermute(out_b, 'lat', lat_b)  3.9 us
    ppermute x1, waiting for transfers between devices, local(): grid_b = lax.ppermute(grid_b, 'lon', lon_b)  2.84 us
    ppermute x1, waiting for transfers between devices, local(): grid_a = lax.ppermute(grid_a, 'lon', lon_a)  2.4 us
    pallas_call x1, Pallas kernels, local(): pl.pallas_call(functools.partial(prepare_kernel, strip, slots, lat_count,...  2.34 us
    pallas_call x1, Pallas kernels, local(): pl.pallas_call(functools.partial(gather_kernel, strip, slots, lon_count,...  2.34 us
  transfers between devices with their start and end apart: 12, of which 5 were waited for; matrix products, arithmetic and copies ran while one was open for 2% of the time, Pallas kernels for 12%

profile of v4, /device:TPU:16, one launch (start us, length us, event | category | flops | bytes accessed | tf_op | source)
XLA Modules:
  0.0 47.2 jit_solution(4766006461424762999)
XLA Ops:
  0.0 1.3 %constant_dynamic-slice_fusion.1 = (bf16[2,52,16,128]{3,2,1,0:T(8,128)(2,1)S(1)}, bf16[2,52,16,128]{3,2,1,0:T(8,128)(2,1)S(1)}) fusion(bf16[2,104,16,128]{3,2,1,0:T(8,128)(2,1)} %param.7, s32[]{:T(128)S(6)} %select_n.8, s32[]{:T(128)S(6)} %select_n.7), kind=kLoop, calls=%fused_computation.2 | loop fusion | bytes 1703944 | tf_op jit(solution)/shard_map/dynamic_slice | solution.py:358
  1.4 0.0 copy-start.1
  1.4 0.1 collective-permute-start
  1.4 2.4 %collective-permute-start.3 = (bf16[2,52,16,128]{3,2,1,0:T(8,128)(2,1)S(1)}, bf16[2,52,16,128]{3,2,1,0:T(8,128)(2,1)S(1)}, u32[]{:S(2)}, u32[]{:S(2)}) collective-permute-start(bf16[2,52,16,128]{3,2,1,0:T(8,128)(2,1)S(1)} %get-tuple-element.24.refs_0_), channel_id=1, source_target_pairs={{4,8},{8,4},{5,9},{9,5},{6,10},{10,6},{7,11},{11,7},{20,24},{24,20... | collective-permute-start | bytes 1277960 | tf_op jit(solution)/shard_map/ppermute | solution.py:367
  3.8 0.1 collective-permute-start.1
  3.9 0.1 constant_dynamic-slice_fusion
  4.0 0.7 %copy.9 = bf16[52,16,128]{2,0,1:T(8,128)(2,1)} copy(bf16[52,16,128]{2,1,0:T(8,128)(2,1)S(1)} %slice) | data formatting | bytes 425984 | tf_op jit(solution)/shard_map/reshape | solution.py:350
  4.8 7.5 %all-to-all-start = ((bf16[16,52,128]{2,1,0:T(8,128)(2,1)}), bf16[16,52,128]{2,1,0:T(8,128)(2,1)S(1)}, u32[]{:S(2)}, u32[]{:S(2)}) async-start(bf16[16,52,128]{2,1,0:T(8,128)(2,1)} %bitcast.5), calls=%async_computation | async-start | bytes 458752 | tf_op jit(solution)/shard_map/all_to_all | solution.py:351
  12.3 0.0 collective-permute-done.refs_1_
  12.3 2.5 %collective-permute-start.4 = (bf16[2,52,16,128]{3,2,1,0:T(8,128)(2,1)S(1)}, bf16[2,52,16,128]{3,2,1,0:T(8,128)(2,1)S(1)}, u32[]{:S(2)}, u32[]{:S(2)}) collective-permute-start(bf16[2,52,16,128]{3,2,1,0:T(8,128)(2,1)S(1)} %collective-permute-done.refs_1_), channel_id=1, source_target_pairs={{4,8},{8,4},{5,9},{9,5},{6,10},{10,6},{7,11},{11,7},{20,24},{24,20... | collective-permute-start | bytes 1277960 | tf_op jit(solution)/shard_map/ppermute | solution.py:367
  14.8 0.1 collective-permute-start.2
  14.9 2.3 %prepare.1 = (bf16[1,26,16,128]{3,2,1,0:T(8,128)(2,1)}, bf16[1,26,16,128]{3,2,1,0:T(8,128)(2,1)}, bf16[304,256]{1,0:T(8,128)(2,1)S(1)}) custom-call(bf16[2,52,16,128]{3,2,1,0:T(8,128)(2,1)S(1)} %get-tuple-element.24.refs_0_, bf16[2,52,16,128]{3,2,1,0:T(8,128)(2,1)S(1)} %collective-permute-done.refs_1_, f32[17]{0:T(128)S(1)} %copy-done.2, f32[17]{0:T(128)S(1)} %copy-done.3), custom_call_target="tpu_custom_call" | custom-call | tf_op jit(solution)/shard_map/prepare/pallas_call | solution.py:373
  17.2 1.5 %collective-permute-start.5 = (bf16[1,26,16,128]{3,2,1,0:T(8,128)(2,1)}, bf16[1,26,16,128]{3,2,1,0:T(8,128)(2,1)S(1)}, u32[]{:S(2)}, u32[]{:S(2)}) collective-permute-start(bf16[1,26,16,128]{3,2,1,0:T(8,128)(2,1)} %get-tuple-element.14), channel_id=1, source_target_pairs={{0,1},{1,0},{2,3},{3,2},{4,5},{5,4},{6,7},{7,6},{8,9},{9,8},{10,11... | collective-permute-start | bytes 319496 | tf_op jit(solution)/shard_map/ppermute | solution.py:383
  18.7 0.0 collective-permute-done.3.refs_4_
  18.7 1.5 %collective-permute-start.6 = (bf16[1,26,16,128]{3,2,1,0:T(8,128)(2,1)}, bf16[1,26,16,128]{3,2,1,0:T(8,128)(2,1)}, u32[]{:S(2)}, u32[]{:S(2)}) collective-permute-start(bf16[1,26,16,128]{3,2,1,0:T(8,128)(2,1)} %get-tuple-element.15), channel_id=1, source_target_pairs={{0,3},{1,2},{2,1},{3,0},{4,7},{5,6},{6,5},{7,4},{8,11},{9,10},{10,... | collective-permute-start | bytes 319496 | tf_op jit(solution)/shard_map/ppermute | solution.py:384
  20.2 1.8 %all-to-all-done.moved_ref = bf16[16,52,128]{2,1,0:T(8,128)(2,1)S(1)} async-done(((bf16[16,52,128]{2,1,0:T(8,128)(2,1)}), bf16[16,52,128]{2,1,0:T(8,128)(2,1)S(1)}, u32[]{:S(2)}, u32[]{:S(2)}) %all-to-all-start) | async-done | bytes 213024 | tf_op jit(solution)/shard_map/all_to_all | solution.py:351
  21.9 2.3 %gather.1 = (bf16[52,16,128]{2,1,0:T(8,128)(2,1)S(1)}, bf16[7,16,128]{2,1,0:T(8,128)(2,1)S(1)}, bf16[7,16,128]{2,1,0:T(8,128)(2,1)S(1)}) custom-call(bf16[16,52,128]{2,1,0:T(8,128)(2,1)S(1)} %all-to-all-done.moved_ref, s32[16,128]{1,0:T(8,128)S(1)} %copy-done.1), custom_call_target="tpu_custom_call" | custom-call | tf_op jit(solution)/shard_map/gather/pallas_call | solution.py:388
  24.3 0.0 collective-permute-done.1.refs_2_
  24.3 1.5 %collective-permute-start.7 = (bf16[7,16,128]{2,1,0:T(8,128)(2,1)S(1)}, bf16[7,16,128]{2,1,0:T(8,128)(2,1)S(1)}, u32[]{:S(2)}, u32[]{:S(2)}) collective-permute-start(bf16[7,16,128]{2,1,0:T(8,128)(2,1)S(1)} %get-tuple-element.16), channel_id=1, source_target_pairs={{0,1},{1,0},{2,3},{3,2},{4,5},{5,4},{6,7},{7,6},{8,9},{9,8},{10,11... | collective-permute-start | bytes 86024 | tf_op jit(solution)/shard_map/ppermute | solution.py:395
  25.8 2.4 %collective-permute-done.7.refs_8_ = bf16[7,16,128]{2,1,0:T(8,128)(2,1)S(1)} collective-permute-done((bf16[7,16,128]{2,1,0:T(8,128)(2,1)S(1)}, bf16[7,16,128]{2,1,0:T(8,128)(2,1)S(1)}, u32[]{:S(2)}, u32[]{:S(2)}) %collective-permute-start.7) | collective-permute-done | bytes 28704 | tf_op jit(solution)/shard_map/ppermute | solution.py:395
  28.2 1.1 %collective-permute-start.8 = (bf16[7,16,128]{2,1,0:T(8,128)(2,1)S(1)}, bf16[7,16,128]{2,1,0:T(8,128)(2,1)S(1)}, u32[]{:S(2)}, u32[]{:S(2)}) collective-permute-start(bf16[7,16,128]{2,1,0:T(8,128)(2,1)S(1)} %get-tuple-element.17), channel_id=1, source_target_pairs={{0,3},{1,2},{2,1},{3,0},{4,7},{5,6},{6,5},{7,4},{8,11},{9,10},{10,... | collective-permute-start | bytes 86024 | tf_op jit(solution)/shard_map/ppermute | solution.py:396
  29.3 0.8 %shard_map.55.refs_11_ = f32[3328,128]{1,0:T(8,128)S(1)} custom-call(bf16[2,52,16,128]{3,2,1,0:T(8,128)(2,1)S(1)} %get-tuple-element.24.refs_0_, bf16[2,52,16,128]{3,2,1,0:T(8,128)(2,1)S(1)} %collective-permute-done.refs_1_, bf16[52,16,128]{2,1,0:T(8,128)(2,1)S(1)} %get-tuple-element.19.refs_2_, bf16[304,256]{1,0:T(8,128)(2,1)S(1)} %get-tuple-element.18.refs_3_.refs_10_), custom_call_target="tpu_custom_call" | custom-call | tf_op jit(solution)/shard_map/pallas_call | solution.py:286
  30.1 2.8 %collective-permute-done.8.refs_9_ = bf16[7,16,128]{2,1,0:T(8,128)(2,1)S(1)} collective-permute-done((bf16[7,16,128]{2,1,0:T(8,128)(2,1)S(1)}, bf16[7,16,128]{2,1,0:T(8,128)(2,1)S(1)}, u32[]{:S(2)}, u32[]{:S(2)}) %collective-permute-start.8) | collective-permute-done | bytes 28704 | tf_op jit(solution)/shard_map/ppermute | solution.py:396
  33.0 0.0 collective-permute-done.5.refs_6_
  33.0 0.0 collective-permute-done.6.refs_7_
  33.0 0.0 collective-permute-done.4.refs_5_
  33.0 3.2 %shard_map.56 = (s16[56,16,128]{2,1,0:T(8,128)(2,1)S(1)}, f32[52,16,128]{2,1,0:T(8,128)S(1)}, s16[56,16,128]{2,1,0:T(8,128)(2,1)S(1)}) custom-call(bf16[2,52,16,128]{3,2,1,0:T(8,128)(2,1)S(1)} %get-tuple-element.24.refs_0_, bf16[2,52,16,128]{3,2,1,0:T(8,128)(2,1)S(1)} %collective-permute-done.refs_1_, ...), custom_call_target="tpu_custom_call" | custom-call | tf_op jit(solution)/shard_map/pallas_call | solution.py:286
  36.2 2.1 %collective-permute-start.9 = (s16[56,16,128]{2,1,0:T(8,128)(2,1)S(1)}, s16[56,16,128]{2,1,0:T(8,128)(2,1)S(1)}, u32[]{:S(2)}, u32[]{:S(2)}) collective-permute-start(s16[56,16,128]{2,1,0:T(8,128)(2,1)S(1)} %get-tuple-element.21), channel_id=1, source_target_pairs={{0,4},{4,0},{8,12},{12,8},{1,5},{5,1},{9,13},{13,9},{2,6},{6,2},{1... | collective-permute-start | bytes 688136 | tf_op jit(solution)/shard_map/ppermute | solution.py:403
  38.4 2.0 %collective-permute-start.10 = (s16[56,16,128]{2,1,0:T(8,128)(2,1)S(1)}, s16[56,16,128]{2,1,0:T(8,128)(2,1)S(1)}, u32[]{:S(2)}, u32[]{:S(2)}) collective-permute-start(s16[56,16,128]{2,1,0:T(8,128)(2,1)S(1)} %get-tuple-element.22), channel_id=1, source_target_pairs={{4,8},{8,4},{5,9},{9,5},{6,10},{10,6},{7,11},{11,7},{20,24},{24,20... | collective-permute-start | bytes 688136 | tf_op jit(solution)/shard_map/ppermute | solution.py:404
  40.4 2.0 %collective-permute-done.9.a_ref = s16[56,16,128]{2,1,0:T(8,128)(2,1)S(1)} collective-permute-done((s16[56,16,128]{2,1,0:T(8,128)(2,1)S(1)}, s16[56,16,128]{2,1,0:T(8,128)(2,1)S(1)}, u32[]{:S(2)}, u32[]{:S(2)}) %collective-permute-start.9) | collective-permute-done | bytes 229408 | tf_op jit(solution)/shard_map/ppermute | solution.py:403
  42.4 3.9 %collective-permute-done.10.b_ref = s16[56,16,128]{2,1,0:T(8,128)(2,1)S(1)} collective-permute-done((s16[56,16,128]{2,1,0:T(8,128)(2,1)S(1)}, s16[56,16,128]{2,1,0:T(8,128)(2,1)S(1)}, u32[]{:S(2)}, u32[]{:S(2)}) %collective-permute-start.10) | collective-permute-done | bytes 229408 | tf_op jit(solution)/shard_map/ppermute | solution.py:404
  46.3 0.9 %shard_map.57 = f32[52,16,128]{2,1,0:T(8,128)} custom-call(f32[52,16,128]{2,1,0:T(8,128)S(1)} %get-tuple-element.20.out_ref, s16[56,16,128]{2,1,0:T(8,128)(2,1)S(1)} %collective-permute-done.9.a_ref, s16[56,16,128]{2,1,0:T(8,128)(2,1)S(1)} %collective-permute-done.10.b_ref), custom_call_target="tpu_custom_call" | custom-call | tf_op jit(solution)/shard_map/pallas_call | solution.py:286
  (10 shorter events, 0.1 us)
Async XLA Ops:
  0.0 3.9 %copy-start = (bf16[104,2048]{1,0:T(8,128)(2,1)S(1)}, bf16[104,2048]{1,0:T(8,128)(2,1)}, u32[]{:S(2)}) copy-start(bf16[104,2048]{1,0:T(8,128)(2,1)} %param.5) | copy-start | bytes 1277956
  0.0 14.9 %copy-start.2 = (f32[17]{0:T(128)S(1)}, f32[17]{0:T(128)}, u32[]{:S(2)}) copy-start(f32[17]{0:T(128)} %refs_2_.1) | copy-start | bytes 208
  0.0 14.9 %copy-start.3 = (f32[17]{0:T(128)S(1)}, f32[17]{0:T(128)}, u32[]{:S(2)}) copy-start(f32[17]{0:T(128)} %refs_3_.1) | copy-start | bytes 208
  1.4 20.6 %copy-start.1 = (s32[16,128]{1,0:T(8,128)S(1)}, s32[16,128]{1,0:T(8,128)}, u32[]{:S(2)}) copy-start(s32[16,128]{1,0:T(8,128)} %index_ref.1) | copy-start | bytes 24580
  1.4 11.0 %collective-permute-start = (bf16[2,52,16,128]{3,2,1,0:T(8,128)(2,1)S(1)}, bf16[2,52,16,128]{3,2,1,0:T(8,128)(2,1)S(1)}, u32[]{:S(2)}, u32[]{:S(2)}) collective-permute-start(bf16[2,52,16,128]{3,2,1,0:T(8,128)(2,1)S(1)} %get-tuple-element.23), channel_id=1, source_target_pairs={{0,16},{16,0},{1,17},{17,1},{2,18},{18,2},{3,19},{19,3},{4,20},{20... | collective-permute-start | bytes 1277960 | tf_op jit(solution)/shard_map/ppermute | solution.py:360
  1.4 17.3 %collective-permute-start.3 = (bf16[2,52,16,128]{3,2,1,0:T(8,128)(2,1)S(1)}, bf16[2,52,16,128]{3,2,1,0:T(8,128)(2,1)S(1)}, u32[]{:S(2)}, u32[]{:S(2)}) collective-permute-start(bf16[2,52,16,128]{3,2,1,0:T(8,128)(2,1)S(1)} %get-tuple-element.24.refs_0_), channel_id=1, source_target_pairs={{4,8},{8,4},{5,9},{9,5},{6,10},{10,6},{7,11},{11,7},{20,24},{24,20... | collective-permute-start | bytes 1277960 | tf_op jit(solution)/shard_map/ppermute | solution.py:367
  3.8 20.5 %collective-permute-start.1 = (bf16[2,52,16,128]{3,2,1,0:T(8,128)(2,1)S(1)}, bf16[2,52,16,128]{3,2,1,0:T(8,128)(2,1)S(1)}, u32[]{:S(2)}, u32[]{:S(2)}) collective-permute-start(bf16[2,52,16,128]{3,2,1,0:T(8,128)(2,1)S(1)} %get-tuple-element.24.refs_0_), channel_id=1, source_target_pairs={{0,4},{4,0},{8,12},{12,8},{1,5},{5,1},{9,13},{13,9},{2,6},{6,2},{1... | collective-permute-start | bytes 1277960 | tf_op jit(solution)/shard_map/ppermute | solution.py:366
  4.8 17.1 %all-to-all-start = ((bf16[16,52,128]{2,1,0:T(8,128)(2,1)}), bf16[16,52,128]{2,1,0:T(8,128)(2,1)S(1)}, u32[]{:S(2)}, u32[]{:S(2)}) async-start(bf16[16,52,128]{2,1,0:T(8,128)(2,1)} %bitcast.5), calls=%async_computation | async-start | bytes 458752 | tf_op jit(solution)/shard_map/all_to_all | solution.py:351
  12.3 20.7 %collective-permute-start.4 = (bf16[2,52,16,128]{3,2,1,0:T(8,128)(2,1)S(1)}, bf16[2,52,16,128]{3,2,1,0:T(8,128)(2,1)S(1)}, u32[]{:S(2)}, u32[]{:S(2)}) collective-permute-start(bf16[2,52,16,128]{3,2,1,0:T(8,128)(2,1)S(1)} %collective-permute-done.refs_1_), channel_id=1, source_target_pairs={{4,8},{8,4},{5,9},{9,5},{6,10},{10,6},{7,11},{11,7},{20,24},{24,20... | collective-permute-start | bytes 1277960 | tf_op jit(solution)/shard_map/ppermute | solution.py:367
  14.8 18.2 %collective-permute-start.2 = (bf16[2,52,16,128]{3,2,1,0:T(8,128)(2,1)S(1)}, bf16[2,52,16,128]{3,2,1,0:T(8,128)(2,1)S(1)}, u32[]{:S(2)}, u32[]{:S(2)}) collective-permute-start(bf16[2,52,16,128]{3,2,1,0:T(8,128)(2,1)S(1)} %collective-permute-done.refs_1_), channel_id=1, source_target_pairs={{0,4},{4,0},{8,12},{12,8},{1,5},{5,1},{9,13},{13,9},{2,6},{6,2},{1... | collective-permute-start | bytes 1277960 | tf_op jit(solution)/shard_map/ppermute | solution.py:366
  17.2 15.8 %collective-permute-start.5 = (bf16[1,26,16,128]{3,2,1,0:T(8,128)(2,1)}, bf16[1,26,16,128]{3,2,1,0:T(8,128)(2,1)S(1)}, u32[]{:S(2)}, u32[]{:S(2)}) collective-permute-start(bf16[1,26,16,128]{3,2,1,0:T(8,128)(2,1)} %get-tuple-element.14), channel_id=1, source_target_pairs={{0,1},{1,0},{2,3},{3,2},{4,5},{5,4},{6,7},{7,6},{8,9},{9,8},{10,11... | collective-permute-start | bytes 319496 | tf_op jit(solution)/shard_map/ppermute | solution.py:383
  18.7 14.3 %collective-permute-start.6 = (bf16[1,26,16,128]{3,2,1,0:T(8,128)(2,1)}, bf16[1,26,16,128]{3,2,1,0:T(8,128)(2,1)}, u32[]{:S(2)}, u32[]{:S(2)}) collective-permute-start(bf16[1,26,16,128]{3,2,1,0:T(8,128)(2,1)} %get-tuple-element.15), channel_id=1, source_target_pairs={{0,3},{1,2},{2,1},{3,0},{4,7},{5,6},{6,5},{7,4},{8,11},{9,10},{10,... | collective-permute-start | bytes 319496 | tf_op jit(solution)/shard_map/ppermute | solution.py:384
  24.3 3.9 %collective-permute-start.7 = (bf16[7,16,128]{2,1,0:T(8,128)(2,1)S(1)}, bf16[7,16,128]{2,1,0:T(8,128)(2,1)S(1)}, u32[]{:S(2)}, u32[]{:S(2)}) collective-permute-start(bf16[7,16,128]{2,1,0:T(8,128)(2,1)S(1)} %get-tuple-element.16), channel_id=1, source_target_pairs={{0,1},{1,0},{2,3},{3,2},{4,5},{5,4},{6,7},{7,6},{8,9},{9,8},{10,11... | collective-permute-start | bytes 86024 | tf_op jit(solution)/shard_map/ppermute | solution.py:395
  28.2 4.8 %collective-permute-start.8 = (bf16[7,16,128]{2,1,0:T(8,128)(2,1)S(1)}, bf16[7,16,128]{2,1,0:T(8,128)(2,1)S(1)}, u32[]{:S(2)}, u32[]{:S(2)}) collective-permute-start(bf16[7,16,128]{2,1,0:T(8,128)(2,1)S(1)} %get-tuple-element.17), channel_id=1, source_target_pairs={{0,3},{1,2},{2,1},{3,0},{4,7},{5,6},{6,5},{7,4},{8,11},{9,10},{10,... | collective-permute-start | bytes 86024 | tf_op jit(solution)/shard_map/ppermute | solution.py:396
  36.2 6.1 %collective-permute-start.9 = (s16[56,16,128]{2,1,0:T(8,128)(2,1)S(1)}, s16[56,16,128]{2,1,0:T(8,128)(2,1)S(1)}, u32[]{:S(2)}, u32[]{:S(2)}) collective-permute-start(s16[56,16,128]{2,1,0:T(8,128)(2,1)S(1)} %get-tuple-element.21), channel_id=1, source_target_pairs={{0,4},{4,0},{8,12},{12,8},{1,5},{5,1},{9,13},{13,9},{2,6},{6,2},{1... | collective-permute-start | bytes 688136 | tf_op jit(solution)/shard_map/ppermute | solution.py:403
  38.4 7.9 %collective-permute-start.10 = (s16[56,16,128]{2,1,0:T(8,128)(2,1)S(1)}, s16[56,16,128]{2,1,0:T(8,128)(2,1)S(1)}, u32[]{:S(2)}, u32[]{:S(2)}) collective-permute-start(s16[56,16,128]{2,1,0:T(8,128)(2,1)S(1)} %get-tuple-element.22), channel_id=1, source_target_pairs={{4,8},{8,4},{5,9},{9,5},{6,10},{10,6},{7,11},{11,7},{20,24},{24,20... | collective-permute-start | bytes 688136 | tf_op jit(solution)/shard_map/ppermute | solution.py:404

commit v5 on v4

--- a/solution.py
+++ b/solution.py
@@ -13,7 +13,7 @@
 BF16 = jnp.bfloat16
 UNIT = 7
 STEPS = 32760.0
-GRANT = 24 << 20
+GRANT = 8 << 20
 
 
 def whole(n):
@@ -37,7 +37,7 @@
 
 
 def fill_matrices(strip, lat_count, rows, lat_taps_ref, lon_taps_ref, matrix_ref):
-    cols = matrix_ref.shape[1] // 2
+    cols = matrix_ref.shape[1]
     count = lon_taps_ref.shape[0]
     iota = lax.broadcasted_iota
     taps = [lon_taps_ref[k] for k in range(count)]
@@ -49,7 +49,9 @@
     after = (place < cols + LANES // 2) == even
     source = jnp.where(place < cols, place, jnp.where(after, cols + inner, inner - strip))
     hi, lo = split(band(both, source - iota(jnp.int32, (2 * LANES, cols), 1) + count - 1))
-    matrix_ref[: 2 * LANES, :] = jnp.concatenate([hi, lo], axis=1)
+    for n, side in enumerate((slice(0, cols), slice(cols, None))):
+        stacked = jnp.concatenate([hi[side], lo[side], hi[side]], axis=0)
+        matrix_ref[3 * cols * n : 3 * cols * (n + 1), :] = stacked
     count = lat_taps_ref.shape[0]
     radius = (count - 1) // 2
     taps = [lat_taps_ref[k] for k in range(count)]
@@ -64,7 +66,7 @@
     whole_row = lax.axis_index("lat") * rows + mid_row
     gather = jnp.where((whole_row >= 0) & (whole_row < lat_count * rows), gather, 0.0)
     hi, lo = split(jnp.dot(spread, gather, precision=lax.Precision.HIGHEST, preferred_element_type=F32))
-    matrix_ref[2 * LANES :, : 3 * rows] = jnp.concatenate([hi, lo, hi], axis=1)
+    matrix_ref[6 * cols :, : 3 * rows] = jnp.concatenate([hi, lo, hi], axis=1)
 
 
 def pick_matrix(slot, strip, cols):
@@ -95,7 +97,7 @@
         b_ref[h] = total[:, LANES:].reshape(channels // per, rows, LANES)
 
 
-def gather_kernel(strip, slots, lon_count, piece, moved_ref, index_ref, grid_ref, a_ref, b_ref, scratch):
+def gather_kernel(strip, slots, lon_count, piece, moved_ref, index_ref, grid_ref, a_ref, b_ref, scratch, stack):
     pieces, channels, width = moved_ref.shape
     rows, cols = index_ref.shape
     cells = rows * cols
@@ -103,14 +105,22 @@
     index = index_ref[...]
     offset = lax.div(index, cells) * piece + lax.rem(index, cells) - block * piece
     scratch[channels:] = jnp.zeros((scratch.shape[0] - channels, rows, cols), F32)
-    tokens = jnp.concatenate([moved_ref[n] for n in range(pieces)], axis=1)
-    token = lax.broadcasted_iota(jnp.int32, (pieces * width, 2 * cols), 0)
+    high = -(-channels // 8) * 8
+    for n in range(pieces):
+        stack[n * high : n * high + channels, :] = moved_ref[n]
+    place = lax.broadcasted_iota(jnp.int32, (width, 2 * cols), 0)
+    many = next(n for n in (8, 4, 2, 1) if pieces % n == 0)
     for i in range(0, rows, 2):
         wanted = jnp.concatenate([offset[i : i + 1], offset[i + 1 : i + 2]], axis=1)
-        chosen = jnp.where(token == wanted, 1.0, 0.0).astype(BF16)
-        found = dot(tokens, chosen)
-        scratch[:channels, i, :] = found[:, :cols]
-        scratch[:channels, i + 1, :] = found[:, cols:]
+        chosen = jnp.where(place == lax.rem(wanted, width), 1.0, 0.0).astype(BF16)
+        source = jnp.broadcast_to(lax.div(wanted, width), (high, 2 * cols))
+        found = jnp.zeros((high, 2 * cols), F32)
+        for n in range(0, pieces, many):
+            some = dot(stack[n * high : (n + many) * high, :], chosen)
+            for q in range(many):
+                found = jnp.where(source == n + q, some[q * high : (q + 1) * high], found)
+        scratch[:channels, i, :] = found[:channels, :cols]
+        scratch[:channels, i + 1, :] = found[:channels, cols:]
     grid = scratch[...].astype(BF16)
     grid_ref[...] = grid[:channels]
     groups = scratch.shape[0] // slots
@@ -150,7 +160,7 @@
 
 
 def inner_kernel(slots, unit, parts, *refs):
-    own_refs, (grid_ref, matrix_ref, part_ref, hi_ref, lo_ref) = refs[:parts], refs[parts:]
+    own_refs, (grid_ref, matrix_ref, part_ref, product_ref) = refs[:parts], refs[parts:]
     each, channels, rows, cols = own_refs[0].shape
     planes = Planes(slots, each * parts, channels)
     height = slots * rows
@@ -160,26 +170,24 @@
             first, _, where = planes.place(n)
             for k, (c, m) in enumerate(where):
                 at = pl.ds(n * height + k * rows, rows)
-                product = member(own_refs, m, first + c) * grid_ref[first + c].astype(F32)
-                hi_ref[at, :], lo_ref[at, :] = split(product)
+                product_ref[at, :] = member(own_refs, m, first + c) * grid_ref[first + c].astype(F32)
 
     def along_lon(unit):
         at = pl.ds(unit[0] * height, len(unit) * height)
-        big = dot(hi_ref[at, :], matrix_ref[:cols, :])
-        small = dot(lo_ref[at, :], matrix_ref[:cols, :cols])
-        part_ref[at, :] = big[:, :cols] + big[:, cols:] + small
+        hi, lo = split(product_ref[at, :])
+        part_ref[at, :] = dot(jnp.concatenate([hi, hi, lo], axis=1), matrix_ref[: 3 * cols, :])
 
     planes.stages(unit, weigh, along_lon)
 
 
-def smooth_kernel(strip, slots, unit, parts, *refs):
-    own_refs, a_refs, b_refs = (refs[n * parts : (n + 1) * parts] for n in range(3))
-    (strip_a_ref, strip_b_ref, grid_a_ref, grid_b_ref, matrix_ref, part_ref) = refs[3 * parts : 3 * parts + 6]
-    out_a_ref, out_ref, out_b_ref, hi_ref, lo_ref, mid_ref, sum_ref, scale_ref = refs[3 * parts + 6 :]
-    each, channels, rows, cols = own_refs[0].shape
-    members = each * parts
-    planes = Planes(slots, members, channels)
-    per, folds = planes.per, planes.folds
+def outer_kernel(
+    strip, slots, unit, members, strip_a_ref, strip_b_ref, grid_a_ref, grid_b_ref, matrix_ref, part_ref,
+    mid_ref, side_ref,
+):
+    cols = part_ref.shape[1]
+    folds, pairs, rows, _ = strip_a_ref.shape
+    planes = Planes(slots, members, pairs * max(1, slots // members))
+    per = planes.per
     half = LANES // 2
     height = slots * rows
     src = lax.broadcasted_iota(jnp.int32, (LANES, LANES), 0)
@@ -188,49 +196,55 @@
     lane = lax.broadcasted_iota(jnp.int32, (rows, LANES), 1)
     low = lane < half
     slot_of = (lane % half) // strip
-    scale_ref[...] = jnp.zeros_like(scale_ref)
+    expands = {}
 
     def weigh(unit):
         for n in unit:
             first, h, _ = planes.place(n)
-            expand = src == ((first + dst_channel) % slots) * strip + dst % strip
-            expand = jnp.where(expand, 1.0, 0.0).astype(BF16)
+            if first % slots not in expands:
+                expand = src == ((first + dst_channel) % slots) * strip + dst % strip
+                expands[first % slots] = jnp.where(expand, 1.0, 0.0).astype(BF16)
+            expand = expands[first % slots]
             edge_a = strip_a_ref[h, first // per].astype(F32) * dot(grid_a_ref[first // slots], expand)
             edge_b = strip_b_ref[h, first // per].astype(F32) * dot(grid_b_ref[first // slots], expand)
-            sides = (
-                split(jnp.where(low, edge_a, pltpu.roll(edge_b, half, 1))),
-                split(jnp.where(low, pltpu.roll(edge_a, half, 1), edge_b)),
-            )
-            for k in range(slots):
-                side = sides[k * 2 // slots]
-                keep = slot_of == k % (slots // 2)
-                at = pl.ds(n * height + k * rows, rows)
-                for p, ref in enumerate((hi_ref, lo_ref)):
-                    ref[at, :] = jnp.where(keep, side[p], jnp.zeros_like(side[p]))
+            side_ref[2 * n] = jnp.where(low, edge_a, pltpu.roll(edge_b, half, 1))
+            side_ref[2 * n + 1] = jnp.where(low, pltpu.roll(edge_a, half, 1), edge_b)
 
     def along_lon(unit):
-        n, many = unit[0], len(unit)
-        at = pl.ds(n * height, many * height)
-        edge = pl.ds(cols, LANES)
-        big = dot(hi_ref[at, :], matrix_ref[edge, :])
-        small = dot(lo_ref[at, :], matrix_ref[edge, :cols])
-        hi, lo = split(part_ref[at, :] + big[:, :cols] + big[:, cols:] + small)
-        for k in range(many * slots):
-            to = pl.ds((n * slots + k) * cols, cols)
-            rest = slice(k * rows, (k + 1) * rows)
-            mid_ref[:rows, to] = hi[rest]
-            mid_ref[rows : 2 * rows, to] = hi[rest]
-            mid_ref[2 * rows :, to] = lo[rest]
-
-    def send(side, ref, c, total):
-        level = code_of(jnp.max(jnp.abs(total), axis=0, keepdims=True))
-        scale_ref[side, c : c + 1, :] = level
-        ref[c] = to_int16(jnp.floor(total * (STEPS * scale_of(-level)) + 0.5))
+        at = pl.ds(unit[0] * height, len(unit) * height)
+        edges = []
+        for n in unit:
+            for s in range(2):
+                hi, lo = split(side_ref[2 * n + s])
+                none = jnp.zeros_like(hi)
+                for k in range(slots // 2):
+                    keep = slot_of == k
+                    one, two = jnp.where(keep, hi, none), jnp.where(keep, lo, none)
+                    edges.append(jnp.concatenate([one, one, two], axis=1))
+        edges = jnp.concatenate(edges, axis=0)
+        mid_ref[at, :] = part_ref[at, :] + dot(edges, matrix_ref[3 * cols : 6 * cols, :])
+
+    planes.stages(unit, weigh, along_lon)
+
+
+def spread_kernel(slots, unit, parts, *refs):
+    own_refs, a_refs, b_refs = (refs[n * parts : (n + 1) * parts] for n in range(3))
+    matrix_ref, mid_ref, out_a_ref, out_ref, out_b_ref, sum_ref, scale_ref = refs[3 * parts :]
+    each, channels, rows, cols = own_refs[0].shape
+    planes = Planes(slots, each * parts, channels)
+    per, folds = planes.per, planes.folds
+    height = slots * rows
+    scale_ref[...] = jnp.zeros_like(scale_ref)
 
     def along_lat(unit):
         for n in unit:
             first, h, where = planes.place(n)
-            spread = dot(matrix_ref[cols + LANES :, : 3 * rows], mid_ref[:, pl.ds(n * slots * cols, slots * cols)])
+            hi, lo = split(mid_ref[pl.ds(n * height, height), :])
+            stack = []
+            for k in range(slots):
+                at = slice(k * rows, (k + 1) * rows)
+                stack.append(jnp.concatenate([hi[at], hi[at], lo[at]], axis=0))
+            spread = dot(matrix_ref[6 * cols :, : 3 * rows], jnp.concatenate(stack, axis=1))
             for r, weights in enumerate((a_refs, own_refs, b_refs)):
                 sums = {}
                 for k, (c, m) in enumerate(where):
@@ -241,14 +255,24 @@
                     at = first + c
                     if h:
                         total = total + sum_ref[r, at]
-                    if h < folds - 1:
-                        sum_ref[r, at] = total
-                    elif r == 1:
+                    if r == 1 and h == folds - 1:
                         out_ref[at] = total
-                    else:
-                        send(r // 2, (out_a_ref, out_b_ref)[r // 2], at, total)
-
-    planes.stages(unit, weigh, along_lon, along_lat)
+                        continue
+                    sum_ref[r, at] = total
+                    if h == folds - 1:
+                        scale_ref[r // 2, at : at + 1, :] = jnp.max(jnp.abs(total), axis=0, keepdims=True)
+
+    def send(unit):
+        first, last = planes.place(unit[0])[0], planes.place(unit[-1])[0] + per
+        for side, ref in enumerate((out_a_ref, out_b_ref)):
+            level = code_of(scale_ref[side, first:last, :])
+            scale_ref[side, first:last, :] = level
+            factor = STEPS * scale_of(-level)
+            for c in range(first, last):
+                total = sum_ref[2 * side, c] * factor[c - first : c - first + 1]
+                ref[c] = to_int16(jnp.floor(total + 0.5))
+
+    planes.stages(unit, along_lat, send)
     for side, ref in enumerate((out_a_ref, out_b_ref)):
         for n in range(channels, ref.shape[0]):
             at = pl.ds((n - channels) * rows, rows)
@@ -300,22 +324,27 @@
     return call(
         functools.partial(inner_kernel, slots, UNIT, parts),
         jax.ShapeDtypeStruct((high, cols), F32),
-        [pltpu.VMEM((high, cols), BF16)] * 2,
+        [pltpu.VMEM((high, cols), F32)],
     )
 
 
-def smooth_call(strip, slots, channels, members, rows, cols, parts):
+def outer_call(strip, slots, channels, members, rows, cols):
     high = channels * members * rows
+    return call(
+        functools.partial(outer_kernel, strip, slots, UNIT, members),
+        jax.ShapeDtypeStruct((high, cols), F32),
+        [pltpu.VMEM((2 * channels * members // slots, rows, LANES), F32)],
+    )
+
+
+def spread_call(slots, channels, members, rows, cols, parts):
     extra = -(-channels // rows)
     side = jax.ShapeDtypeStruct((channels + extra, rows, cols), jnp.int16)
     return call(
-        functools.partial(smooth_kernel, strip, slots, UNIT, parts),
+        functools.partial(spread_kernel, slots, UNIT, parts),
         (side, jax.ShapeDtypeStruct((channels, rows, cols), F32), side),
         [
-            pltpu.VMEM((high, LANES), BF16),
-            pltpu.VMEM((high, LANES), BF16),
-            pltpu.VMEM((3 * rows, channels * members * cols), BF16),
-            pltpu.VMEM((3, channels if members > slots else 1, rows, cols), F32),
+            pltpu.VMEM((3, channels, rows, cols), F32),
             pltpu.VMEM((2, extra * rows, cols), F32),
         ],
     )
@@ -363,8 +392,8 @@
         w = [lax.all_to_all(members, "ens", split_axis=1, concat_axis=0, tiled=True)]
     w_a, w_b = [], []
     for block in w:
+        w_b.append(lax.ppermute(block, "lat", lat_b))
         w_a.append(lax.ppermute(block, "lat", lat_a))
-        w_b.append(lax.ppermute(block, "lat", lat_b))
     count = len(w) * w[0].shape[0]
     per = max(1, slots // count)
 
@@ -375,13 +404,13 @@
         out_shape=(
             strips,
             strips,
-            jax.ShapeDtypeStruct((2 * LANES + 3 * rows, 2 * cols), BF16),
+            jax.ShapeDtypeStruct((6 * cols + 3 * rows, cols), BF16),
         ),
         in_specs=whole(len(w)) + [smem] * 2, out_specs=whole(3), name="prepare",
         compiler_params=pltpu.CompilerParams(vmem_limit_bytes=GRANT),
     )(*w, lat_taps, lon_taps)
+    strip_b = lax.ppermute(strip_b, "lon", lon_b)
     strip_a = lax.ppermute(strip_a, "lon", lon_a)
-    strip_b = lax.ppermute(strip_b, "lon", lon_b)
 
     padded = -(-own_channels // slots) * slots
     edges = jax.ShapeDtypeStruct((padded // slots, rows, LANES), BF16)
@@ -389,19 +418,21 @@
         functools.partial(gather_kernel, strip, slots, lon_count, piece),
         out_shape=(jax.ShapeDtypeStruct((own_channels, rows, cols), BF16), edges, edges),
         in_specs=whole(2), out_specs=whole(3),
-        scratch_shapes=[pltpu.VMEM((padded, rows, cols), F32)], name="gather",
+        scratch_shapes=[
+            pltpu.VMEM((padded, rows, cols), F32),
+            pltpu.VMEM((cells // LANES * (-(-own_channels // 8) * 8), LANES), BF16),
+        ], name="gather",
         compiler_params=pltpu.CompilerParams(vmem_limit_bytes=GRANT),
     )(moved, token_index)
+    grid_b = lax.ppermute(grid_b, "lon", lon_b)
     grid_a = lax.ppermute(grid_a, "lon", lon_a)
-    grid_b = lax.ppermute(grid_b, "lon", lon_b)
 
     sizes = (own_channels, count, rows, cols, len(w))
     part = inner_call(slots, *sizes)(*w, grid, matrix)
-    out_a, out, out_b = smooth_call(strip, slots, *sizes)(
-        *w, *w_a, *w_b, strip_a, strip_b, grid_a, grid_b, matrix, part
-    )
+    mid = outer_call(strip, slots, *sizes[:4])(strip_a, strip_b, grid_a, grid_b, matrix, part)
+    out_a, out, out_b = spread_call(slots, *sizes)(*w, *w_a, *w_b, matrix, mid)
+    out_b = lax.ppermute(out_b, "lat", lat_b)
     out_a = lax.ppermute(out_a, "lat", lat_a)
-    out_b = lax.ppermute(out_b, "lat", lat_b)
     return add_call(count - 1, own_channels, rows, cols)(out, out_a, out_b)
 
 

time: 47.5 us -> 53.6 us (1.13)
  the two profiles are of different devices: /device:TPU:16 before, /device:TPU:0 now
where the time goes in v5:
time: 53.6 us; the launch traced here: 53.3 us
  starting transfers between devices  24.1 us (45%)
  waiting for transfers between devices  19.3 us (36%)
  Pallas kernels  7.53 us (14%)
  local copies, waits for them, and re-layouts  2.21 us (4%)
    all_to_all x1, starting transfers between devices, local(): lax.all_to_all(tokens, ('lat', 'lon'), split_axis=0, concat_axis=0, tiled...  7.88 us
    ppermute x2, starting transfers between devices, local(): w_a.append(lax.ppermute(block, 'lat', lat_a))  6.14 us
    pallas_call x4, Pallas kernels, run(): pl.pallas_call(kernel, out_shape=out_shape, in_specs=whole(n) + [pl.Block...  4.25 us
    ppermute x1, waiting for transfers between devices, local(): out_a = lax.ppermute(out_a, 'lat', lat_a)  4 us
    ppermute x1, waiting for transfers between devices, local(): strip_a = lax.ppermute(strip_a, 'lon', lon_a)  3.9 us
    ppermute x1, waiting for transfers between devices, local(): strip_b = lax.ppermute(strip_b, 'lon', lon_b)  3.47 us
    ppermute x1, starting transfers between devices, local(): out_a = lax.ppermute(out_a, 'lat', lat_a)  3.04 us
    ppermute x1, waiting for transfers between devices, local(): grid_a = lax.ppermute(grid_a, 'lon', lon_a)  2.76 us
  transfers between devices with their start and end apart: 12, of which 6 were waited for; matrix products, arithmetic and copies ran while one was open for 2% of the time, Pallas kernels for 10%

profile of v5, /device:TPU:0, one launch (start us, length us, event | category | flops | bytes accessed | tf_op | source)
XLA Modules:
  0.0 53.3 jit_solution(15851554002056457544)
XLA Ops:
  0.0 1.3 %constant_dynamic-slice_fusion.1 = (bf16[2,52,16,128]{3,2,1,0:T(8,128)(2,1)S(1)}, bf16[2,52,16,128]{3,2,1,0:T(8,128)(2,1)S(1)}) fusion(bf16[2,104,16,128]{3,2,1,0:T(8,128)(2,1)} %param.7, s32[]{:T(128)S(6)} %select_n.8, s32[]{:T(128)S(6)} %select_n.7), kind=kLoop, calls=%fused_computation.2 | loop fusion | bytes 1703944 | tf_op jit(solution)/shard_map/dynamic_slice | solution.py:387
  1.4 0.6 %collective-permute-start = (bf16[2,52,16,128]{3,2,1,0:T(8,128)(2,1)S(1)}, bf16[2,52,16,128]{3,2,1,0:T(8,128)(2,1)S(1)}, u32[]{:S(2)}, u32[]{:S(2)}) collective-permute-start(bf16[2,52,16,128]{3,2,1,0:T(8,128)(2,1)S(1)} %get-tuple-element.23), channel_id=1, source_target_pairs={{0,16},{16,0},{1,17},{17,1},{2,18},{18,2},{3,19},{19,3},{4,20},{20... | collective-permute-start | bytes 1277960 | tf_op jit(solution)/shard_map/ppermute | solution.py:389
  1.9 0.1 constant_dynamic-slice_fusion
  2.1 0.7 %copy.9 = bf16[52,16,128]{2,0,1:T(8,128)(2,1)} copy(bf16[52,16,128]{2,1,0:T(8,128)(2,1)S(1)} %slice) | data formatting | bytes 425984 | tf_op jit(solution)/shard_map/reshape | solution.py:379
  2.8 7.9 %all-to-all-start = ((bf16[16,52,128]{2,1,0:T(8,128)(2,1)}), bf16[16,52,128]{2,1,0:T(8,128)(2,1)S(1)}, u32[]{:S(2)}, u32[]{:S(2)}) async-start(bf16[16,52,128]{2,1,0:T(8,128)(2,1)} %bitcast.5), calls=%async_computation | async-start | bytes 458752 | tf_op jit(solution)/shard_map/all_to_all | solution.py:380
  10.7 1.9 %collective-permute-start.1 = (bf16[2,52,16,128]{3,2,1,0:T(8,128)(2,1)S(1)}, bf16[2,52,16,128]{3,2,1,0:T(8,128)(2,1)S(1)}, u32[]{:S(2)}, u32[]{:S(2)}) collective-permute-start(bf16[2,52,16,128]{3,2,1,0:T(8,128)(2,1)S(1)} %get-tuple-element.24.refs_0_), channel_id=1, source_target_pairs={{0,4},{4,0},{8,12},{12,8},{1,5},{5,1},{9,13},{13,9},{2,6},{6,2},{1... | collective-permute-start | bytes 1277960 | tf_op jit(solution)/shard_map/ppermute | solution.py:396
  12.6 0.7 %collective-permute-start.3 = (bf16[2,52,16,128]{3,2,1,0:T(8,128)(2,1)S(1)}, bf16[2,52,16,128]{3,2,1,0:T(8,128)(2,1)S(1)}, u32[]{:S(2)}, u32[]{:S(2)}) collective-permute-start(bf16[2,52,16,128]{3,2,1,0:T(8,128)(2,1)S(1)} %get-tuple-element.24.refs_0_), channel_id=1, source_target_pairs={{4,8},{8,4},{5,9},{9,5},{6,10},{10,6},{7,11},{11,7},{20,24},{24,20... | collective-permute-start | bytes 1277960 | tf_op jit(solution)/shard_map/ppermute | solution.py:395
  13.3 0.0 collective-permute-done.refs_1_
  13.3 4.2 %collective-permute-start.2 = (bf16[2,52,16,128]{3,2,1,0:T(8,128)(2,1)S(1)}, bf16[2,52,16,128]{3,2,1,0:T(8,128)(2,1)S(1)}, u32[]{:S(2)}, u32[]{:S(2)}) collective-permute-start(bf16[2,52,16,128]{3,2,1,0:T(8,128)(2,1)S(1)} %collective-permute-done.refs_1_), channel_id=1, source_target_pairs={{0,4},{4,0},{8,12},{12,8},{1,5},{5,1},{9,13},{13,9},{2,6},{6,2},{1... | collective-permute-start | bytes 1277960 | tf_op jit(solution)/shard_map/ppermute | solution.py:396
  17.5 0.7 %collective-permute-start.4 = (bf16[2,52,16,128]{3,2,1,0:T(8,128)(2,1)S(1)}, bf16[2,52,16,128]{3,2,1,0:T(8,128)(2,1)S(1)}, u32[]{:S(2)}, u32[]{:S(2)}) collective-permute-start(bf16[2,52,16,128]{3,2,1,0:T(8,128)(2,1)S(1)} %collective-permute-done.refs_1_), channel_id=1, source_target_pairs={{4,8},{8,4},{5,9},{9,5},{6,10},{10,6},{7,11},{11,7},{20,24},{24,20... | collective-permute-start | bytes 1277960 | tf_op jit(solution)/shard_map/ppermute | solution.py:395
  18.2 2.7 %all-to-all-done.moved_ref = bf16[16,52,128]{2,1,0:T(8,128)(2,1)S(1)} async-done(((bf16[16,52,128]{2,1,0:T(8,128)(2,1)}), bf16[16,52,128]{2,1,0:T(8,128)(2,1)S(1)}, u32[]{:S(2)}, u32[]{:S(2)}) %all-to-all-start) | async-done | bytes 213024 | tf_op jit(solution)/shard_map/all_to_all | solution.py:380
  20.9 1.6 %gather.1 = (bf16[52,16,128]{2,1,0:T(8,128)(2,1)S(1)}, bf16[7,16,128]{2,1,0:T(8,128)(2,1)S(1)}, bf16[7,16,128]{2,1,0:T(8,128)(2,1)S(1)}) custom-call(bf16[16,52,128]{2,1,0:T(8,128)(2,1)S(1)} %all-to-all-done.moved_ref, s32[16,128]{1,0:T(8,128)S(1)} %copy-done.1), custom_call_target="tpu_custom_call" | custom-call | tf_op jit(solution)/shard_map/gather/pallas_call | solution.py:417
  22.5 1.4 %collective-permute-start.7 = (bf16[7,16,128]{2,1,0:T(8,128)(2,1)S(1)}, bf16[7,16,128]{2,1,0:T(8,128)(2,1)S(1)}, u32[]{:S(2)}, u32[]{:S(2)}) collective-permute-start(bf16[7,16,128]{2,1,0:T(8,128)(2,1)S(1)} %get-tuple-element.17), channel_id=1, source_target_pairs={{0,1},{1,0},{2,3},{3,2},{4,5},{5,4},{6,7},{7,6},{8,9},{9,8},{10,11... | collective-permute-start | bytes 86024 | tf_op jit(solution)/shard_map/ppermute | solution.py:428
  23.9 2.8 %collective-permute-done.7.grid_a_ref = bf16[7,16,128]{2,1,0:T(8,128)(2,1)S(1)} collective-permute-done((bf16[7,16,128]{2,1,0:T(8,128)(2,1)S(1)}, bf16[7,16,128]{2,1,0:T(8,128)(2,1)S(1)}, u32[]{:S(2)}, u32[]{:S(2)}) %collective-permute-start.7) | collective-permute-done | bytes 28704 | tf_op jit(solution)/shard_map/ppermute | solution.py:428
  26.7 0.8 %collective-permute-start.8 = (bf16[7,16,128]{2,1,0:T(8,128)(2,1)S(1)}, bf16[7,16,128]{2,1,0:T(8,128)(2,1)S(1)}, u32[]{:S(2)}, u32[]{:S(2)}) collective-permute-start(bf16[7,16,128]{2,1,0:T(8,128)(2,1)S(1)} %get-tuple-element.18), channel_id=1, source_target_pairs={{0,3},{1,2},{2,1},{3,0},{4,7},{5,6},{6,5},{7,4},{8,11},{9,10},{10,... | collective-permute-start | bytes 86024 | tf_op jit(solution)/shard_map/ppermute | solution.py:427
  27.5 1.6 %prepare.1 = (bf16[1,26,16,128]{3,2,1,0:T(8,128)(2,1)S(1)}, bf16[1,26,16,128]{3,2,1,0:T(8,128)(2,1)S(1)}, bf16[816,128]{1,0:T(8,128)(2,1)S(1)}) custom-call(bf16[2,52,16,128]{3,2,1,0:T(8,128)(2,1)S(1)} %get-tuple-element.24.refs_0_, bf16[2,52,16,128]{3,2,1,0:T(8,128)(2,1)S(1)} %collective-permute-done.refs_1_, f32[17]{0:T(128)S(1)} %copy-done.2, f32[17]{0:T(128)S(1)} %copy-done.3), custom_call_target="tpu_custom_call" | custom-call | tf_op jit(solution)/shard_map/prepare/pallas_call | solution.py:402
  29.2 2.5 %collective-permute-done.8.grid_b_ref = bf16[7,16,128]{2,1,0:T(8,128)(2,1)S(1)} collective-permute-done((bf16[7,16,128]{2,1,0:T(8,128)(2,1)S(1)}, bf16[7,16,128]{2,1,0:T(8,128)(2,1)S(1)}, u32[]{:S(2)}, u32[]{:S(2)}) %collective-permute-start.8) | collective-permute-done | bytes 28704 | tf_op jit(solution)/shard_map/ppermute | solution.py:427
  31.6 0.9 %collective-permute-start.5 = (bf16[1,26,16,128]{3,2,1,0:T(8,128)(2,1)S(1)}, bf16[1,26,16,128]{3,2,1,0:T(8,128)(2,1)S(1)}, u32[]{:S(2)}, u32[]{:S(2)}) collective-permute-start(bf16[1,26,16,128]{3,2,1,0:T(8,128)(2,1)S(1)} %get-tuple-element.15), channel_id=1, source_target_pairs={{0,1},{1,0},{2,3},{3,2},{4,5},{5,4},{6,7},{7,6},{8,9},{9,8},{10,11... | collective-permute-start | bytes 319496 | tf_op jit(solution)/shard_map/ppermute | solution.py:413
  32.6 3.9 %collective-permute-done.5.strip_a_ref = bf16[1,26,16,128]{3,2,1,0:T(8,128)(2,1)S(1)} collective-permute-done((bf16[1,26,16,128]{3,2,1,0:T(8,128)(2,1)S(1)}, bf16[1,26,16,128]{3,2,1,0:T(8,128)(2,1)S(1)}, u32[]{:S(2)}, u32[]{:S(2)}) %collective-permute-start.5) | collective-permute-done | bytes 106528 | tf_op jit(solution)/shard_map/ppermute | solution.py:413
  36.5 1.3 %collective-permute-start.6 = (bf16[1,26,16,128]{3,2,1,0:T(8,128)(2,1)S(1)}, bf16[1,26,16,128]{3,2,1,0:T(8,128)(2,1)S(1)}, u32[]{:S(2)}, u32[]{:S(2)}) collective-permute-start(bf16[1,26,16,128]{3,2,1,0:T(8,128)(2,1)S(1)} %get-tuple-element.16), channel_id=1, source_target_pairs={{0,3},{1,2},{2,1},{3,0},{4,7},{5,6},{6,5},{7,4},{8,11},{9,10},{10,... | collective-permute-start | bytes 319496 | tf_op jit(solution)/shard_map/ppermute | solution.py:412
  37.8 0.8 %shard_map.55.part_ref = f32[3328,128]{1,0:T(8,128)S(1)} custom-call(bf16[2,52,16,128]{3,2,1,0:T(8,128)(2,1)S(1)} %get-tuple-element.24.refs_0_, bf16[2,52,16,128]{3,2,1,0:T(8,128)(2,1)S(1)} %collective-permute-done.refs_1_, bf16[52,16,128]{2,1,0:T(8,128)(2,1)S(1)} %get-tuple-element.19.refs_2_, bf16[816,128]{1,0:T(8,128)(2,1)S(1)} %get-tuple-element.14.refs_3_.matrix_ref.refs_6_), custom_call_target="tpu_custom_call" | custom-call | tf_op jit(solution)/shard_map/pallas_call | solution.py:310
  38.6 3.5 %collective-permute-done.6.strip_b_ref = bf16[1,26,16,128]{3,2,1,0:T(8,128)(2,1)S(1)} collective-permute-done((bf16[1,26,16,128]{3,2,1,0:T(8,128)(2,1)S(1)}, bf16[1,26,16,128]{3,2,1,0:T(8,128)(2,1)S(1)}, u32[]{:S(2)}, u32[]{:S(2)}) %collective-permute-start.6) | collective-permute-done | bytes 106528 | tf_op jit(solution)/shard_map/ppermute | solution.py:412
  42.1 1.3 %shard_map.56.refs_7_ = f32[3328,128]{1,0:T(8,128)S(1)} custom-call(bf16[1,26,16,128]{3,2,1,0:T(8,128)(2,1)S(1)} %collective-permute-done.5.strip_a_ref, bf16[1,26,16,128]{3,2,1,0:T(8,128)(2,1)S(1)} %collective-permute-done.6.strip_b_ref, bf16[7,16,128]{2,1,0:T(8,128)(2,1)S(1)} %collective-permute-done.7.grid_a_ref, ...), custom_call_target="tpu_custom_call" | custom-call | tf_op jit(solution)/shard_map/pallas_call | solution.py:310
  43.4 0.0 collective-permute-done.1.refs_2_
  43.4 0.0 collective-permute-done.3.refs_4_
  43.4 0.0 collective-permute-done.2.refs_3_
  43.4 0.0 collective-permute-done.4.refs_5_
  43.4 1.2 %shard_map.57 = (s16[56,16,128]{2,1,0:T(8,128)(2,1)S(1)}, f32[52,16,128]{2,1,0:T(8,128)S(1)}, s16[56,16,128]{2,1,0:T(8,128)(2,1)S(1)}) custom-call(bf16[2,52,16,128]{3,2,1,0:T(8,128)(2,1)S(1)} %get-tuple-element.24.refs_0_, bf16[2,52,16,128]{3,2,1,0:T(8,128)(2,1)S(1)} %collective-permute-done.refs_1_, ...), custom_call_target="tpu_custom_call" | custom-call | tf_op jit(solution)/shard_map/pallas_call | solution.py:310
  44.6 0.7 %collective-permute-start.10 = (s16[56,16,128]{2,1,0:T(8,128)(2,1)S(1)}, s16[56,16,128]{2,1,0:T(8,128)(2,1)S(1)}, u32[]{:S(2)}, u32[]{:S(2)}) collective-permute-start(s16[56,16,128]{2,1,0:T(8,128)(2,1)S(1)} %get-tuple-element.22), channel_id=1, source_target_pairs={{4,8},{8,4},{5,9},{9,5},{6,10},{10,6},{7,11},{11,7},{20,24},{24,20... | collective-permute-start | bytes 688136 | tf_op jit(solution)/shard_map/ppermute | solution.py:434
  45.3 3.0 %collective-permute-start.9 = (s16[56,16,128]{2,1,0:T(8,128)(2,1)S(1)}, s16[56,16,128]{2,1,0:T(8,128)(2,1)S(1)}, u32[]{:S(2)}, u32[]{:S(2)}) collective-permute-start(s16[56,16,128]{2,1,0:T(8,128)(2,1)S(1)} %get-tuple-element.21), channel_id=1, source_target_pairs={{0,4},{4,0},{8,12},{12,8},{1,5},{5,1},{9,13},{13,9},{2,6},{6,2},{1... | collective-permute-start | bytes 688136 | tf_op jit(solution)/shard_map/ppermute | solution.py:435
  48.4 4.0 %collective-permute-done.9.a_ref = s16[56,16,128]{2,1,0:T(8,128)(2,1)S(1)} collective-permute-done((s16[56,16,128]{2,1,0:T(8,128)(2,1)S(1)}, s16[56,16,128]{2,1,0:T(8,128)(2,1)S(1)}, u32[]{:S(2)}, u32[]{:S(2)}) %collective-permute-start.9) | collective-permute-done | bytes 229408 | tf_op jit(solution)/shard_map/ppermute | solution.py:435
  52.4 0.9 %shard_map.58 = f32[52,16,128]{2,1,0:T(8,128)} custom-call(f32[52,16,128]{2,1,0:T(8,128)S(1)} %get-tuple-element.20.out_ref, s16[56,16,128]{2,1,0:T(8,128)(2,1)S(1)} %collective-permute-done.9.a_ref, s16[56,16,128]{2,1,0:T(8,128)(2,1)S(1)} %collective-permute-done.10.b_ref), custom_call_target="tpu_custom_call" | custom-call | tf_op jit(solution)/shard_map/pallas_call | solution.py:310
  (11 shorter events, 0.1 us)
Async XLA Ops:
  0.0 1.9 %copy-start = (bf16[104,2048]{1,0:T(8,128)(2,1)S(1)}, bf16[104,2048]{1,0:T(8,128)(2,1)}, u32[]{:S(2)}) copy-start(bf16[104,2048]{1,0:T(8,128)(2,1)} %param.5) | copy-start | bytes 1277956
  0.0 20.9 %copy-start.1 = (s32[16,128]{1,0:T(8,128)S(1)}, s32[16,128]{1,0:T(8,128)}, u32[]{:S(2)}) copy-start(s32[16,128]{1,0:T(8,128)} %index_ref.1) | copy-start | bytes 24580
  0.0 27.5 %copy-start.2 = (f32[17]{0:T(128)S(1)}, f32[17]{0:T(128)}, u32[]{:S(2)}) copy-start(f32[17]{0:T(128)} %refs_2_.1) | copy-start | bytes 208
  0.0 27.5 %copy-start.3 = (f32[17]{0:T(128)S(1)}, f32[17]{0:T(128)}, u32[]{:S(2)}) copy-start(f32[17]{0:T(128)} %refs_3_.1) | copy-start | bytes 208
  1.4 11.9 %collective-permute-start = (bf16[2,52,16,128]{3,2,1,0:T(8,128)(2,1)S(1)}, bf16[2,52,16,128]{3,2,1,0:T(8,128)(2,1)S(1)}, u32[]{:S(2)}, u32[]{:S(2)}) collective-permute-start(bf16[2,52,16,128]{3,2,1,0:T(8,128)(2,1)S(1)} %get-tuple-element.23), channel_id=1, source_target_pairs={{0,16},{16,0},{1,17},{17,1},{2,18},{18,2},{3,19},{19,3},{4,20},{20... | collective-permute-start | bytes 1277960 | tf_op jit(solution)/shard_map/ppermute | solution.py:389
  2.8 18.1 %all-to-all-start = ((bf16[16,52,128]{2,1,0:T(8,128)(2,1)}), bf16[16,52,128]{2,1,0:T(8,128)(2,1)S(1)}, u32[]{:S(2)}, u32[]{:S(2)}) async-start(bf16[16,52,128]{2,1,0:T(8,128)(2,1)} %bitcast.5), calls=%async_computation | async-start | bytes 458752 | tf_op jit(solution)/shard_map/all_to_all | solution.py:380
  10.7 32.7 %collective-permute-start.1 = (bf16[2,52,16,128]{3,2,1,0:T(8,128)(2,1)S(1)}, bf16[2,52,16,128]{3,2,1,0:T(8,128)(2,1)S(1)}, u32[]{:S(2)}, u32[]{:S(2)}) collective-permute-start(bf16[2,52,16,128]{3,2,1,0:T(8,128)(2,1)S(1)} %get-tuple-element.24.refs_0_), channel_id=1, source_target_pairs={{0,4},{4,0},{8,12},{12,8},{1,5},{5,1},{9,13},{13,9},{2,6},{6,2},{1... | collective-permute-start | bytes 1277960 | tf_op jit(solution)/shard_map/ppermute | solution.py:396
  12.6 30.8 %collective-permute-start.3 = (bf16[2,52,16,128]{3,2,1,0:T(8,128)(2,1)S(1)}, bf16[2,52,16,128]{3,2,1,0:T(8,128)(2,1)S(1)}, u32[]{:S(2)}, u32[]{:S(2)}) collective-permute-start(bf16[2,52,16,128]{3,2,1,0:T(8,128)(2,1)S(1)} %get-tuple-element.24.refs_0_), channel_id=1, source_target_pairs={{4,8},{8,4},{5,9},{9,5},{6,10},{10,6},{7,11},{11,7},{20,24},{24,20... | collective-permute-start | bytes 1277960 | tf_op jit(solution)/shard_map/ppermute | solution.py:395
  13.3 30.1 %collective-permute-start.2 = (bf16[2,52,16,128]{3,2,1,0:T(8,128)(2,1)S(1)}, bf16[2,52,16,128]{3,2,1,0:T(8,128)(2,1)S(1)}, u32[]{:S(2)}, u32[]{:S(2)}) collective-permute-start(bf16[2,52,16,128]{3,2,1,0:T(8,128)(2,1)S(1)} %collective-permute-done.refs_1_), channel_id=1, source_target_pairs={{0,4},{4,0},{8,12},{12,8},{1,5},{5,1},{9,13},{13,9},{2,6},{6,2},{1... | collective-permute-start | bytes 1277960 | tf_op jit(solution)/shard_map/ppermute | solution.py:396
  17.5 25.9 %collective-permute-start.4 = (bf16[2,52,16,128]{3,2,1,0:T(8,128)(2,1)S(1)}, bf16[2,52,16,128]{3,2,1,0:T(8,128)(2,1)S(1)}, u32[]{:S(2)}, u32[]{:S(2)}) collective-permute-start(bf16[2,52,16,128]{3,2,1,0:T(8,128)(2,1)S(1)} %collective-permute-done.refs_1_), channel_id=1, source_target_pairs={{4,8},{8,4},{5,9},{9,5},{6,10},{10,6},{7,11},{11,7},{20,24},{24,20... | collective-permute-start | bytes 1277960 | tf_op jit(solution)/shard_map/ppermute | solution.py:395
  22.5 4.1 %collective-permute-start.7 = (bf16[7,16,128]{2,1,0:T(8,128)(2,1)S(1)}, bf16[7,16,128]{2,1,0:T(8,128)(2,1)S(1)}, u32[]{:S(2)}, u32[]{:S(2)}) collective-permute-start(bf16[7,16,128]{2,1,0:T(8,128)(2,1)S(1)} %get-tuple-element.17), channel_id=1, source_target_pairs={{0,1},{1,0},{2,3},{3,2},{4,5},{5,4},{6,7},{7,6},{8,9},{9,8},{10,11... | collective-permute-start | bytes 86024 | tf_op jit(solution)/shard_map/ppermute | solution.py:428
  26.7 4.9 %collective-permute-start.8 = (bf16[7,16,128]{2,1,0:T(8,128)(2,1)S(1)}, bf16[7,16,128]{2,1,0:T(8,128)(2,1)S(1)}, u32[]{:S(2)}, u32[]{:S(2)}) collective-permute-start(bf16[7,16,128]{2,1,0:T(8,128)(2,1)S(1)} %get-tuple-element.18), channel_id=1, source_target_pairs={{0,3},{1,2},{2,1},{3,0},{4,7},{5,6},{6,5},{7,4},{8,11},{9,10},{10,... | collective-permute-start | bytes 86024 | tf_op jit(solution)/shard_map/ppermute | solution.py:427
  31.6 4.8 %collective-permute-start.5 = (bf16[1,26,16,128]{3,2,1,0:T(8,128)(2,1)S(1)}, bf16[1,26,16,128]{3,2,1,0:T(8,128)(2,1)S(1)}, u32[]{:S(2)}, u32[]{:S(2)}) collective-permute-start(bf16[1,26,16,128]{3,2,1,0:T(8,128)(2,1)S(1)} %get-tuple-element.15), channel_id=1, source_target_pairs={{0,1},{1,0},{2,3},{3,2},{4,5},{5,4},{6,7},{7,6},{8,9},{9,8},{10,11... | collective-permute-start | bytes 319496 | tf_op jit(solution)/shard_map/ppermute | solution.py:413
  36.5 5.6 %collective-permute-start.6 = (bf16[1,26,16,128]{3,2,1,0:T(8,128)(2,1)S(1)}, bf16[1,26,16,128]{3,2,1,0:T(8,128)(2,1)S(1)}, u32[]{:S(2)}, u32[]{:S(2)}) collective-permute-start(bf16[1,26,16,128]{3,2,1,0:T(8,128)(2,1)S(1)} %get-tuple-element.16), channel_id=1, source_target_pairs={{0,3},{1,2},{2,1},{3,0},{4,7},{5,6},{6,5},{7,4},{8,11},{9,10},{10,... | collective-permute-start | bytes 319496 | tf_op jit(solution)/shard_map/ppermute | solution.py:412
  44.6 3.7 %collective-permute-start.10 = (s16[56,16,128]{2,1,0:T(8,128)(2,1)S(1)}, s16[56,16,128]{2,1,0:T(8,128)(2,1)S(1)}, u32[]{:S(2)}, u32[]{:S(2)}) collective-permute-start(s16[56,16,128]{2,1,0:T(8,128)(2,1)S(1)} %get-tuple-element.22), channel_id=1, source_target_pairs={{4,8},{8,4},{5,9},{9,5},{6,10},{10,6},{7,11},{11,7},{20,24},{24,20... | collective-permute-start | bytes 688136 | tf_op jit(solution)/shard_map/ppermute | solution.py:434
  45.3 7.0 %collective-permute-start.9 = (s16[56,16,128]{2,1,0:T(8,128)(2,1)S(1)}, s16[56,16,128]{2,1,0:T(8,128)(2,1)S(1)}, u32[]{:S(2)}, u32[]{:S(2)}) collective-permute-start(s16[56,16,128]{2,1,0:T(8,128)(2,1)S(1)} %get-tuple-element.21), channel_id=1, source_target_pairs={{0,4},{4,0},{8,12},{12,8},{1,5},{5,1},{9,13},{13,9},{2,6},{6,2},{1... | collective-permute-start | bytes 688136 | tf_op jit(solution)/shard_map/ppermute | solution.py:435

commit v6 on v5

--- a/solution.py
+++ b/solution.py
@@ -36,7 +36,7 @@
     return total
 
 
-def fill_matrices(strip, lat_count, rows, lat_taps_ref, lon_taps_ref, matrix_ref):
+def fill_matrices(strip, lat_count, rows, lat_taps_ref, lon_taps_ref, matrix_ref, edge_ref):
     cols = matrix_ref.shape[1]
     count = lon_taps_ref.shape[0]
     iota = lax.broadcasted_iota
@@ -49,9 +49,11 @@
     after = (place < cols + LANES // 2) == even
     source = jnp.where(place < cols, place, jnp.where(after, cols + inner, inner - strip))
     hi, lo = split(band(both, source - iota(jnp.int32, (2 * LANES, cols), 1) + count - 1))
-    for n, side in enumerate((slice(0, cols), slice(cols, None))):
-        stacked = jnp.concatenate([hi[side], lo[side], hi[side]], axis=0)
-        matrix_ref[3 * cols * n : 3 * cols * (n + 1), :] = stacked
+    matrix_ref[: 3 * cols, :] = jnp.concatenate([hi[:cols], lo[:cols], hi[:cols]], axis=0)
+    slot = iota(jnp.int32, (LANES, cols), 0) % (LANES // 2) // strip
+    for k in range(LANES // 2 // strip):
+        one, two = (jnp.where(slot == k, v[cols:], jnp.zeros_like(v[cols:])) for v in (hi, lo))
+        edge_ref[:, k * cols : (k + 1) * cols] = jnp.concatenate([one, two, one], axis=0)
     count = lat_taps_ref.shape[0]
     radius = (count - 1) // 2
     taps = [lat_taps_ref[k] for k in range(count)]
@@ -66,7 +68,7 @@
     whole_row = lax.axis_index("lat") * rows + mid_row
     gather = jnp.where((whole_row >= 0) & (whole_row < lat_count * rows), gather, 0.0)
     hi, lo = split(jnp.dot(spread, gather, precision=lax.Precision.HIGHEST, preferred_element_type=F32))
-    matrix_ref[6 * cols :, : 3 * rows] = jnp.concatenate([hi, lo, hi], axis=1)
+    matrix_ref[3 * cols :, : 3 * rows] = jnp.concatenate([hi, lo, hi], axis=1)
 
 
 def pick_matrix(slot, strip, cols):
@@ -80,9 +82,9 @@
 
 
 def prepare_kernel(strip, slots, lat_count, parts, *refs):
-    w_refs, (lat_taps_ref, lon_taps_ref, a_ref, b_ref, matrix_ref) = refs[:parts], refs[parts:]
+    w_refs, (lat_taps_ref, lon_taps_ref, a_ref, b_ref, matrix_ref, edge_ref) = refs[:parts], refs[parts:]
     each, channels, rows, cols = w_refs[0].shape
-    fill_matrices(strip, lat_count, rows, lat_taps_ref, lon_taps_ref, matrix_ref)
+    fill_matrices(strip, lat_count, rows, lat_taps_ref, lon_taps_ref, matrix_ref, edge_ref)
     members = each * parts
     per = max(1, slots // members)
     for h in range(max(1, members // slots)):
@@ -109,7 +111,7 @@
     for n in range(pieces):
         stack[n * high : n * high + channels, :] = moved_ref[n]
     place = lax.broadcasted_iota(jnp.int32, (width, 2 * cols), 0)
-    many = next(n for n in (8, 4, 2, 1) if pieces % n == 0)
+    many = next(n for n in (16, 8, 4, 2, 1) if pieces % n == 0)
     for i in range(0, rows, 2):
         wanted = jnp.concatenate([offset[i : i + 1], offset[i + 1 : i + 2]], axis=1)
         chosen = jnp.where(place == lax.rem(wanted, width), 1.0, 0.0).astype(BF16)
@@ -160,7 +162,9 @@
 
 
 def inner_kernel(slots, unit, parts, *refs):
-    own_refs, (grid_ref, matrix_ref, part_ref, product_ref) = refs[:parts], refs[parts:]
+    own_refs = refs[:parts]
+    grid_ref, matrix_ref, strip_a_ref, strip_b_ref, part_ref, near_a_ref, near_b_ref, product_ref = refs[parts:]
+    near_a_ref[...], near_b_ref[...] = strip_a_ref[...], strip_b_ref[...]
     each, channels, rows, cols = own_refs[0].shape
     planes = Planes(slots, each * parts, channels)
     height = slots * rows
@@ -181,7 +185,7 @@
 
 
 def outer_kernel(
-    strip, slots, unit, members, strip_a_ref, strip_b_ref, grid_a_ref, grid_b_ref, matrix_ref, part_ref,
+    strip, slots, unit, members, strip_a_ref, strip_b_ref, grid_a_ref, grid_b_ref, edge_ref, part_ref,
     mid_ref, side_ref,
 ):
     cols = part_ref.shape[1]
@@ -189,13 +193,11 @@
     planes = Planes(slots, members, pairs * max(1, slots // members))
     per = planes.per
     half = LANES // 2
-    height = slots * rows
     src = lax.broadcasted_iota(jnp.int32, (LANES, LANES), 0)
     dst = lax.broadcasted_iota(jnp.int32, (LANES, LANES), 1)
     dst_channel = dst // strip // members if folds == 1 else jnp.zeros_like(dst)
     lane = lax.broadcasted_iota(jnp.int32, (rows, LANES), 1)
     low = lane < half
-    slot_of = (lane % half) // strip
     expands = {}
 
     def weigh(unit):
@@ -207,22 +209,17 @@
             expand = expands[first % slots]
             edge_a = strip_a_ref[h, first // per].astype(F32) * dot(grid_a_ref[first // slots], expand)
             edge_b = strip_b_ref[h, first // per].astype(F32) * dot(grid_b_ref[first // slots], expand)
-            side_ref[2 * n] = jnp.where(low, edge_a, pltpu.roll(edge_b, half, 1))
-            side_ref[2 * n + 1] = jnp.where(low, pltpu.roll(edge_a, half, 1), edge_b)
+            side_ref[pl.ds(2 * n * rows, rows), :] = jnp.where(low, edge_a, pltpu.roll(edge_b, half, 1))
+            side_ref[pl.ds((2 * n + 1) * rows, rows), :] = jnp.where(low, pltpu.roll(edge_a, half, 1), edge_b)
 
     def along_lon(unit):
-        at = pl.ds(unit[0] * height, len(unit) * height)
-        edges = []
-        for n in unit:
-            for s in range(2):
-                hi, lo = split(side_ref[2 * n + s])
-                none = jnp.zeros_like(hi)
-                for k in range(slots // 2):
-                    keep = slot_of == k
-                    one, two = jnp.where(keep, hi, none), jnp.where(keep, lo, none)
-                    edges.append(jnp.concatenate([one, one, two], axis=1))
-        edges = jnp.concatenate(edges, axis=0)
-        mid_ref[at, :] = part_ref[at, :] + dot(edges, matrix_ref[3 * cols : 6 * cols, :])
+        hi, lo = split(side_ref[pl.ds(2 * unit[0] * rows, 2 * len(unit) * rows), :])
+        found = dot(jnp.concatenate([hi, hi, lo], axis=1), edge_ref[...])
+        for n in range(2 * len(unit)):
+            for k in range(slots // 2):
+                at = pl.ds(((2 * unit[0] + n) * (slots // 2) + k) * rows, rows)
+                piece = found[n * rows : (n + 1) * rows, k * cols : (k + 1) * cols]
+                mid_ref[at, :] = part_ref[at, :] + piece
 
     planes.stages(unit, weigh, along_lon)
 
@@ -244,7 +241,7 @@
             for k in range(slots):
                 at = slice(k * rows, (k + 1) * rows)
                 stack.append(jnp.concatenate([hi[at], hi[at], lo[at]], axis=0))
-            spread = dot(matrix_ref[6 * cols :, : 3 * rows], jnp.concatenate(stack, axis=1))
+            spread = dot(matrix_ref[3 * cols :, : 3 * rows], jnp.concatenate(stack, axis=1))
             for r, weights in enumerate((a_refs, own_refs, b_refs)):
                 sums = {}
                 for k, (c, m) in enumerate(where):
@@ -319,11 +316,11 @@
     return run
 
 
-def inner_call(slots, channels, members, rows, cols, parts):
+def inner_call(strips, slots, channels, members, rows, cols, parts):
     high = channels * members * rows
     return call(
         functools.partial(inner_kernel, slots, UNIT, parts),
-        jax.ShapeDtypeStruct((high, cols), F32),
+        (jax.ShapeDtypeStruct((high, cols), F32), strips, strips),
         [pltpu.VMEM((high, cols), F32)],
     )
 
@@ -333,7 +330,7 @@
     return call(
         functools.partial(outer_kernel, strip, slots, UNIT, members),
         jax.ShapeDtypeStruct((high, cols), F32),
-        [pltpu.VMEM((2 * channels * members // slots, rows, LANES), F32)],
+        [pltpu.VMEM((2 * channels * members // slots * rows, LANES), F32)],
     )
 
 
@@ -399,14 +396,15 @@
 
     strips = jax.ShapeDtypeStruct((max(1, count // slots), own_channels // per, rows, LANES), BF16)
     smem = pl.BlockSpec(memory_space=pltpu.SMEM)
-    strip_a, strip_b, matrix = pl.pallas_call(
+    strip_a, strip_b, matrix, edge_matrix = pl.pallas_call(
         functools.partial(prepare_kernel, strip, slots, lat_count, len(w)),
         out_shape=(
             strips,
             strips,
-            jax.ShapeDtypeStruct((6 * cols + 3 * rows, cols), BF16),
+            jax.ShapeDtypeStruct((3 * cols + 3 * rows, cols), BF16),
+            jax.ShapeDtypeStruct((3 * LANES, slots // 2 * cols), BF16),
         ),
-        in_specs=whole(len(w)) + [smem] * 2, out_specs=whole(3), name="prepare",
+        in_specs=whole(len(w)) + [smem] * 2, out_specs=whole(4), name="prepare",
         compiler_params=pltpu.CompilerParams(vmem_limit_bytes=GRANT),
     )(*w, lat_taps, lon_taps)
     strip_b = lax.ppermute(strip_b, "lon", lon_b)
@@ -428,8 +426,8 @@
     grid_a = lax.ppermute(grid_a, "lon", lon_a)
 
     sizes = (own_channels, count, rows, cols, len(w))
-    part = inner_call(slots, *sizes)(*w, grid, matrix)
-    mid = outer_call(strip, slots, *sizes[:4])(strip_a, strip_b, grid_a, grid_b, matrix, part)
+    part, strip_a, strip_b = inner_call(strips, slots, *sizes)(*w, grid, matrix, strip_a, strip_b)
+    mid = outer_call(strip, slots, *sizes[:4])(strip_a, strip_b, grid_a, grid_b, edge_matrix, part)
     out_a, out, out_b = spread_call(slots, *sizes)(*w, *w_a, *w_b, matrix, mid)
     out_b = lax.ppermute(out_b, "lat", lat_b)
     out_a = lax.ppermute(out_a, "lat", lat_a)

time: 53.6 us -> 53.9 us (level)
  waiting for transfers between devices: 19.3 us -> 20.5 us
  starting transfers between devices: 24.1 us -> 23.2 us
    ppermute x1, waiting for transfers between devices: 2.76 us -> 0.72 us  [local(): grid_a = lax.ppermute(grid_a, 'lon', lon_a)]
    ppermute x1, waiting for transfers between devices: 3.47 us -> 5.33 us  [local(): strip_b = lax.ppermute(strip_b, 'lon', lon_b)]
    ppermute x1, starting transfers between devices: 1.3 us -> 0.33 us  [local(): strip_b = lax.ppermute(strip_b, 'lon', lon_b)]
    ppermute x1, waiting for transfers between devices: 2.45 us -> 3.34 us  [local(): grid_b = lax.ppermute(grid_b, 'lon', lon_b)]
where the time goes in v6:
time: 53.9 us; the launch traced here: 53.7 us
  starting transfers between devices  23.2 us (43%)
  waiting for transfers between devices  20.5 us (38%)
  Pallas kernels  7.57 us (14%)
  local copies, waits for them, and re-layouts  2.21 us (4%)
    all_to_all x1, starting transfers between devices, local(): lax.all_to_all(tokens, ('lat', 'lon'), split_axis=0, concat_axis=0, tiled...  7.88 us
    ppermute x2, starting transfers between devices, local(): w_a.append(lax.ppermute(block, 'lat', lat_a))  6.14 us
    ppermute x1, waiting for transfers between devices, local(): strip_b = lax.ppermute(strip_b, 'lon', lon_b)  5.33 us
    ppermute x1, waiting for transfers between devices, local(): strip_a = lax.ppermute(strip_a, 'lon', lon_a)  4.39 us
    pallas_call x4, Pallas kernels, run(): pl.pallas_call(kernel, out_shape=out_shape, in_specs=whole(n) + [pl.Block...  4.11 us
    ppermute x1, waiting for transfers between devices, local(): out_a = lax.ppermute(out_a, 'lat', lat_a)  4 us
    ppermute x1, waiting for transfers between devices, local(): grid_b = lax.ppermute(grid_b, 'lon', lon_b)  3.34 us
    ppermute x1, starting transfers between devices, local(): out_a = lax.ppermute(out_a, 'lat', lat_a)  3.01 us
  transfers between devices with their start and end apart: 12, of which 6 were waited for; matrix products, arithmetic and copies ran while one was open for 2% of the time, Pallas kernels for 10%

profile of v6, /device:TPU:0, one launch (start us, length us, event | category | flops | bytes accessed | tf_op | source)
XLA Modules:
  0.0 53.7 jit_solution(7635094465233172289)
XLA Ops:
  0.0 1.3 %constant_dynamic-slice_fusion.1 = (bf16[2,52,16,128]{3,2,1,0:T(8,128)(2,1)S(1)}, bf16[2,52,16,128]{3,2,1,0:T(8,128)(2,1)S(1)}) fusion(bf16[2,104,16,128]{3,2,1,0:T(8,128)(2,1)} %param.7, s32[]{:T(128)S(6)} %select_n.8, s32[]{:T(128)S(6)} %select_n.7), kind=kLoop, calls=%fused_computation.2 | loop fusion | bytes 1703944 | tf_op jit(solution)/shard_map/dynamic_slice | solution.py:384
  1.4 0.6 %collective-permute-start = (bf16[2,52,16,128]{3,2,1,0:T(8,128)(2,1)S(1)}, bf16[2,52,16,128]{3,2,1,0:T(8,128)(2,1)S(1)}, u32[]{:S(2)}, u32[]{:S(2)}) collective-permute-start(bf16[2,52,16,128]{3,2,1,0:T(8,128)(2,1)S(1)} %get-tuple-element.31), channel_id=1, source_target_pairs={{0,16},{16,0},{1,17},{17,1},{2,18},{18,2},{3,19},{19,3},{4,20},{20... | collective-permute-start | bytes 1277960 | tf_op jit(solution)/shard_map/ppermute | solution.py:386
  1.9 0.1 constant_dynamic-slice_fusion
  2.1 0.7 %copy.9 = bf16[52,16,128]{2,0,1:T(8,128)(2,1)} copy(bf16[52,16,128]{2,1,0:T(8,128)(2,1)S(1)} %slice) | data formatting | bytes 425984 | tf_op jit(solution)/shard_map/reshape | solution.py:376
  2.8 7.9 %all-to-all-start = ((bf16[16,52,128]{2,1,0:T(8,128)(2,1)}), bf16[16,52,128]{2,1,0:T(8,128)(2,1)S(1)}, u32[]{:S(2)}, u32[]{:S(2)}) async-start(bf16[16,52,128]{2,1,0:T(8,128)(2,1)} %bitcast.5), calls=%async_computation | async-start | bytes 458752 | tf_op jit(solution)/shard_map/all_to_all | solution.py:377
  10.7 1.9 %collective-permute-start.1 = (bf16[2,52,16,128]{3,2,1,0:T(8,128)(2,1)S(1)}, bf16[2,52,16,128]{3,2,1,0:T(8,128)(2,1)S(1)}, u32[]{:S(2)}, u32[]{:S(2)}) collective-permute-start(bf16[2,52,16,128]{3,2,1,0:T(8,128)(2,1)S(1)} %get-tuple-element.32.refs_0_), channel_id=1, source_target_pairs={{0,4},{4,0},{8,12},{12,8},{1,5},{5,1},{9,13},{13,9},{2,6},{6,2},{1... | collective-permute-start | bytes 1277960 | tf_op jit(solution)/shard_map/ppermute | solution.py:393
  12.6 0.7 %collective-permute-start.3 = (bf16[2,52,16,128]{3,2,1,0:T(8,128)(2,1)S(1)}, bf16[2,52,16,128]{3,2,1,0:T(8,128)(2,1)S(1)}, u32[]{:S(2)}, u32[]{:S(2)}) collective-permute-start(bf16[2,52,16,128]{3,2,1,0:T(8,128)(2,1)S(1)} %get-tuple-element.32.refs_0_), channel_id=1, source_target_pairs={{4,8},{8,4},{5,9},{9,5},{6,10},{10,6},{7,11},{11,7},{20,24},{24,20... | collective-permute-start | bytes 1277960 | tf_op jit(solution)/shard_map/ppermute | solution.py:392
  13.3 0.0 collective-permute-done.refs_1_
  13.3 4.2 %collective-permute-start.2 = (bf16[2,52,16,128]{3,2,1,0:T(8,128)(2,1)S(1)}, bf16[2,52,16,128]{3,2,1,0:T(8,128)(2,1)S(1)}, u32[]{:S(2)}, u32[]{:S(2)}) collective-permute-start(bf16[2,52,16,128]{3,2,1,0:T(8,128)(2,1)S(1)} %collective-permute-done.refs_1_), channel_id=1, source_target_pairs={{0,4},{4,0},{8,12},{12,8},{1,5},{5,1},{9,13},{13,9},{2,6},{6,2},{1... | collective-permute-start | bytes 1277960 | tf_op jit(solution)/shard_map/ppermute | solution.py:393
  17.5 0.7 %collective-permute-start.4 = (bf16[2,52,16,128]{3,2,1,0:T(8,128)(2,1)S(1)}, bf16[2,52,16,128]{3,2,1,0:T(8,128)(2,1)S(1)}, u32[]{:S(2)}, u32[]{:S(2)}) collective-permute-start(bf16[2,52,16,128]{3,2,1,0:T(8,128)(2,1)S(1)} %collective-permute-done.refs_1_), channel_id=1, source_target_pairs={{4,8},{8,4},{5,9},{9,5},{6,10},{10,6},{7,11},{11,7},{20,24},{24,20... | collective-permute-start | bytes 1277960 | tf_op jit(solution)/shard_map/ppermute | solution.py:392
  18.2 2.7 %all-to-all-done.moved_ref = bf16[16,52,128]{2,1,0:T(8,128)(2,1)S(1)} async-done(((bf16[16,52,128]{2,1,0:T(8,128)(2,1)}), bf16[16,52,128]{2,1,0:T(8,128)(2,1)S(1)}, u32[]{:S(2)}, u32[]{:S(2)}) %all-to-all-start) | async-done | bytes 213024 | tf_op jit(solution)/shard_map/all_to_all | solution.py:377
  20.9 1.6 %gather.1 = (bf16[52,16,128]{2,1,0:T(8,128)(2,1)S(1)}, bf16[7,16,128]{2,1,0:T(8,128)(2,1)S(1)}, bf16[7,16,128]{2,1,0:T(8,128)(2,1)S(1)}) custom-call(bf16[16,52,128]{2,1,0:T(8,128)(2,1)S(1)} %all-to-all-done.moved_ref, s32[16,128]{1,0:T(8,128)S(1)} %copy-done.1), custom_call_target="tpu_custom_call" | custom-call | tf_op jit(solution)/shard_map/gather/pallas_call | solution.py:415
  22.5 1.4 %collective-permute-start.7 = (bf16[7,16,128]{2,1,0:T(8,128)(2,1)S(1)}, bf16[7,16,128]{2,1,0:T(8,128)(2,1)S(1)}, u32[]{:S(2)}, u32[]{:S(2)}) collective-permute-start(bf16[7,16,128]{2,1,0:T(8,128)(2,1)S(1)} %get-tuple-element.24), channel_id=1, source_target_pairs={{0,1},{1,0},{2,3},{3,2},{4,5},{5,4},{6,7},{7,6},{8,9},{9,8},{10,11... | collective-permute-start | bytes 86024 | tf_op jit(solution)/shard_map/ppermute | solution.py:426
  23.9 1.8 %prepare.1 = (bf16[1,26,16,128]{3,2,1,0:T(8,128)(2,1)S(1)}, bf16[1,26,16,128]{3,2,1,0:T(8,128)(2,1)S(1)}, bf16[432,128]{1,0:T(8,128)(2,1)S(1)}, bf16[384,512]{1,0:T(8,128)(2,1)S(1)}) custom-call(bf16[2,52,16,128]{3,2,1,0:T(8,128)(2,1)S(1)} %get-tuple-element.32.refs_0_, bf16[2,52,16,128]{3,2,1,0:T(8,128)(2,1)S(1)} %collective-permute-done.refs_1_, ...), custom_call_target="tpu_custom_call" | custom-call | tf_op jit(solution)/shard_map/prepare/pallas_call | solution.py:399
  25.8 0.7 %collective-permute-done.7.grid_a_ref = bf16[7,16,128]{2,1,0:T(8,128)(2,1)S(1)} collective-permute-done((bf16[7,16,128]{2,1,0:T(8,128)(2,1)S(1)}, bf16[7,16,128]{2,1,0:T(8,128)(2,1)S(1)}, u32[]{:S(2)}, u32[]{:S(2)}) %collective-permute-start.7) | collective-permute-done | bytes 28704 | tf_op jit(solution)/shard_map/ppermute | solution.py:426
  26.5 1.3 %collective-permute-start.5 = (bf16[1,26,16,128]{3,2,1,0:T(8,128)(2,1)S(1)}, bf16[1,26,16,128]{3,2,1,0:T(8,128)(2,1)S(1)}, u32[]{:S(2)}, u32[]{:S(2)}) collective-permute-start(bf16[1,26,16,128]{3,2,1,0:T(8,128)(2,1)S(1)} %get-tuple-element.20), channel_id=1, source_target_pairs={{0,1},{1,0},{2,3},{3,2},{4,5},{5,4},{6,7},{7,6},{8,9},{9,8},{10,11... | collective-permute-start | bytes 319496 | tf_op jit(solution)/shard_map/ppermute | solution.py:411
  27.8 4.4 %collective-permute-done.5.refs_4_ = bf16[1,26,16,128]{3,2,1,0:T(8,128)(2,1)S(1)} collective-permute-done((bf16[1,26,16,128]{3,2,1,0:T(8,128)(2,1)S(1)}, bf16[1,26,16,128]{3,2,1,0:T(8,128)(2,1)S(1)}, u32[]{:S(2)}, u32[]{:S(2)}) %collective-permute-start.5) | collective-permute-done | bytes 106528 | tf_op jit(solution)/shard_map/ppermute | solution.py:411
  32.2 0.3 collective-permute-start.6
  32.5 5.3 %collective-permute-done.6.refs_5_ = bf16[1,26,16,128]{3,2,1,0:T(8,128)(2,1)S(1)} collective-permute-done((bf16[1,26,16,128]{3,2,1,0:T(8,128)(2,1)S(1)}, bf16[1,26,16,128]{3,2,1,0:T(8,128)(2,1)S(1)}, u32[]{:S(2)}, u32[]{:S(2)}) %collective-permute-start.6) | collective-permute-done | bytes 106528 | tf_op jit(solution)/shard_map/ppermute | solution.py:410
  37.9 0.6 %collective-permute-start.8 = (bf16[7,16,128]{2,1,0:T(8,128)(2,1)S(1)}, bf16[7,16,128]{2,1,0:T(8,128)(2,1)S(1)}, u32[]{:S(2)}, u32[]{:S(2)}) collective-permute-start(bf16[7,16,128]{2,1,0:T(8,128)(2,1)S(1)} %get-tuple-element.25), channel_id=1, source_target_pairs={{0,3},{1,2},{2,1},{3,0},{4,7},{5,6},{6,5},{7,4},{8,11},{9,10},{10,... | collective-permute-start | bytes 86024 | tf_op jit(solution)/shard_map/ppermute | solution.py:425
  38.4 0.8 %shard_map.55 = (f32[3328,128]{1,0:T(8,128)S(1)}, bf16[1,26,16,128]{3,2,1,0:T(8,128)(2,1)S(1)}, bf16[1,26,16,128]{3,2,1,0:T(8,128)(2,1)S(1)}) custom-call(bf16[2,52,16,128]{3,2,1,0:T(8,128)(2,1)S(1)} %get-tuple-element.32.refs_0_, bf16[2,52,16,128]{3,2,1,0:T(8,128)(2,1)S(1)} %collective-permute-done.refs_1_, ...), custom_call_target="tpu_custom_call" | custom-call | tf_op jit(solution)/shard_map/pallas_call | solution.py:307
  39.3 3.3 %collective-permute-done.8.grid_b_ref = bf16[7,16,128]{2,1,0:T(8,128)(2,1)S(1)} collective-permute-done((bf16[7,16,128]{2,1,0:T(8,128)(2,1)S(1)}, bf16[7,16,128]{2,1,0:T(8,128)(2,1)S(1)}, u32[]{:S(2)}, u32[]{:S(2)}) %collective-permute-start.8) | collective-permute-done | bytes 28704 | tf_op jit(solution)/shard_map/ppermute | solution.py:425
  42.6 1.1 %shard_map.56.refs_7_ = f32[3328,128]{1,0:T(8,128)S(1)} custom-call(bf16[1,26,16,128]{3,2,1,0:T(8,128)(2,1)S(1)} %get-tuple-element.22.strip_a_ref, bf16[1,26,16,128]{3,2,1,0:T(8,128)(2,1)S(1)} %get-tuple-element.23.strip_b_ref, bf16[7,16,128]{2,1,0:T(8,128)(2,1)S(1)} %collective-permute-done.7.grid_a_ref, ...), custom_call_target="tpu_custom_call" | custom-call | tf_op jit(solution)/shard_map/pallas_call | solution.py:307
  43.8 0.0 collective-permute-done.1.refs_2_
  43.8 0.0 collective-permute-done.2.refs_3_
  43.8 0.0 collective-permute-done.4.refs_5_
  43.8 1.2 %shard_map.57 = (s16[56,16,128]{2,1,0:T(8,128)(2,1)S(1)}, f32[52,16,128]{2,1,0:T(8,128)S(1)}, s16[56,16,128]{2,1,0:T(8,128)(2,1)S(1)}) custom-call(bf16[2,52,16,128]{3,2,1,0:T(8,128)(2,1)S(1)} %get-tuple-element.32.refs_0_, bf16[2,52,16,128]{3,2,1,0:T(8,128)(2,1)S(1)} %collective-permute-done.refs_1_, ...), custom_call_target="tpu_custom_call" | custom-call | tf_op jit(solution)/shard_map/pallas_call | solution.py:307
  45.1 0.7 %collective-permute-start.10 = (s16[56,16,128]{2,1,0:T(8,128)(2,1)S(1)}, s16[56,16,128]{2,1,0:T(8,128)(2,1)S(1)}, u32[]{:S(2)}, u32[]{:S(2)}) collective-permute-start(s16[56,16,128]{2,1,0:T(8,128)(2,1)S(1)} %get-tuple-element.30), channel_id=1, source_target_pairs={{4,8},{8,4},{5,9},{9,5},{6,10},{10,6},{7,11},{11,7},{20,24},{24,20... | collective-permute-start | bytes 688136 | tf_op jit(solution)/shard_map/ppermute | solution.py:432
  45.7 3.0 %collective-permute-start.9 = (s16[56,16,128]{2,1,0:T(8,128)(2,1)S(1)}, s16[56,16,128]{2,1,0:T(8,128)(2,1)S(1)}, u32[]{:S(2)}, u32[]{:S(2)}) collective-permute-start(s16[56,16,128]{2,1,0:T(8,128)(2,1)S(1)} %get-tuple-element.29), channel_id=1, source_target_pairs={{0,4},{4,0},{8,12},{12,8},{1,5},{5,1},{9,13},{13,9},{2,6},{6,2},{1... | collective-permute-start | bytes 688136 | tf_op jit(solution)/shard_map/ppermute | solution.py:433
  48.8 0.0 collective-permute-done.10.b_ref
  48.8 4.0 %collective-permute-done.9.a_ref = s16[56,16,128]{2,1,0:T(8,128)(2,1)S(1)} collective-permute-done((s16[56,16,128]{2,1,0:T(8,128)(2,1)S(1)}, s16[56,16,128]{2,1,0:T(8,128)(2,1)S(1)}, u32[]{:S(2)}, u32[]{:S(2)}) %collective-permute-start.9) | collective-permute-done | bytes 229408 | tf_op jit(solution)/shard_map/ppermute | solution.py:433
  52.8 0.9 %shard_map.58 = f32[52,16,128]{2,1,0:T(8,128)} custom-call(f32[52,16,128]{2,1,0:T(8,128)S(1)} %get-tuple-element.28.out_ref, s16[56,16,128]{2,1,0:T(8,128)(2,1)S(1)} %collective-permute-done.9.a_ref, s16[56,16,128]{2,1,0:T(8,128)(2,1)S(1)} %collective-permute-done.10.b_ref), custom_call_target="tpu_custom_call" | custom-call | tf_op jit(solution)/shard_map/pallas_call | solution.py:307
  (11 shorter events, 0.1 us)
Async XLA Ops:
  0.0 1.9 %copy-start = (bf16[104,2048]{1,0:T(8,128)(2,1)S(1)}, bf16[104,2048]{1,0:T(8,128)(2,1)}, u32[]{:S(2)}) copy-start(bf16[104,2048]{1,0:T(8,128)(2,1)} %param.5) | copy-start | bytes 1277956
  0.0 20.9 %copy-start.1 = (s32[16,128]{1,0:T(8,128)S(1)}, s32[16,128]{1,0:T(8,128)}, u32[]{:S(2)}) copy-start(s32[16,128]{1,0:T(8,128)} %index_ref.1) | copy-start | bytes 24580
  0.0 23.9 %copy-start.2 = (f32[17]{0:T(128)S(1)}, f32[17]{0:T(128)}, u32[]{:S(2)}) copy-start(f32[17]{0:T(128)} %refs_2_.1) | copy-start | bytes 208
  0.0 23.9 %copy-start.3 = (f32[17]{0:T(128)S(1)}, f32[17]{0:T(128)}, u32[]{:S(2)}) copy-start(f32[17]{0:T(128)} %refs_3_.1) | copy-start | bytes 208
  1.4 11.9 %collective-permute-start = (bf16[2,52,16,128]{3,2,1,0:T(8,128)(2,1)S(1)}, bf16[2,52,16,128]{3,2,1,0:T(8,128)(2,1)S(1)}, u32[]{:S(2)}, u32[]{:S(2)}) collective-permute-start(bf16[2,52,16,128]{3,2,1,0:T(8,128)(2,1)S(1)} %get-tuple-element.31), channel_id=1, source_target_pairs={{0,16},{16,0},{1,17},{17,1},{2,18},{18,2},{3,19},{19,3},{4,20},{20... | collective-permute-start | bytes 1277960 | tf_op jit(solution)/shard_map/ppermute | solution.py:386
  2.8 18.1 %all-to-all-start = ((bf16[16,52,128]{2,1,0:T(8,128)(2,1)}), bf16[16,52,128]{2,1,0:T(8,128)(2,1)S(1)}, u32[]{:S(2)}, u32[]{:S(2)}) async-start(bf16[16,52,128]{2,1,0:T(8,128)(2,1)} %bitcast.5), calls=%async_computation | async-start | bytes 458752 | tf_op jit(solution)/shard_map/all_to_all | solution.py:377
  10.7 33.1 %collective-permute-start.1 = (bf16[2,52,16,128]{3,2,1,0:T(8,128)(2,1)S(1)}, bf16[2,52,16,128]{3,2,1,0:T(8,128)(2,1)S(1)}, u32[]{:S(2)}, u32[]{:S(2)}) collective-permute-start(bf16[2,52,16,128]{3,2,1,0:T(8,128)(2,1)S(1)} %get-tuple-element.32.refs_0_), channel_id=1, source_target_pairs={{0,4},{4,0},{8,12},{12,8},{1,5},{5,1},{9,13},{13,9},{2,6},{6,2},{1... | collective-permute-start | bytes 1277960 | tf_op jit(solution)/shard_map/ppermute | solution.py:393
  12.6 31.2 %collective-permute-start.3 = (bf16[2,52,16,128]{3,2,1,0:T(8,128)(2,1)S(1)}, bf16[2,52,16,128]{3,2,1,0:T(8,128)(2,1)S(1)}, u32[]{:S(2)}, u32[]{:S(2)}) collective-permute-start(bf16[2,52,16,128]{3,2,1,0:T(8,128)(2,1)S(1)} %get-tuple-element.32.refs_0_), channel_id=1, source_target_pairs={{4,8},{8,4},{5,9},{9,5},{6,10},{10,6},{7,11},{11,7},{20,24},{24,20... | collective-permute-start | bytes 1277960 | tf_op jit(solution)/shard_map/ppermute | solution.py:392
  13.3 30.5 %collective-permute-start.2 = (bf16[2,52,16,128]{3,2,1,0:T(8,128)(2,1)S(1)}, bf16[2,52,16,128]{3,2,1,0:T(8,128)(2,1)S(1)}, u32[]{:S(2)}, u32[]{:S(2)}) collective-permute-start(bf16[2,52,16,128]{3,2,1,0:T(8,128)(2,1)S(1)} %collective-permute-done.refs_1_), channel_id=1, source_target_pairs={{0,4},{4,0},{8,12},{12,8},{1,5},{5,1},{9,13},{13,9},{2,6},{6,2},{1... | collective-permute-start | bytes 1277960 | tf_op jit(solution)/shard_map/ppermute | solution.py:393
  17.5 26.3 %collective-permute-start.4 = (bf16[2,52,16,128]{3,2,1,0:T(8,128)(2,1)S(1)}, bf16[2,52,16,128]{3,2,1,0:T(8,128)(2,1)S(1)}, u32[]{:S(2)}, u32[]{:S(2)}) collective-permute-start(bf16[2,52,16,128]{3,2,1,0:T(8,128)(2,1)S(1)} %collective-permute-done.refs_1_), channel_id=1, source_target_pairs={{4,8},{8,4},{5,9},{9,5},{6,10},{10,6},{7,11},{11,7},{20,24},{24,20... | collective-permute-start | bytes 1277960 | tf_op jit(solution)/shard_map/ppermute | solution.py:392
  22.5 3.9 %collective-permute-start.7 = (bf16[7,16,128]{2,1,0:T(8,128)(2,1)S(1)}, bf16[7,16,128]{2,1,0:T(8,128)(2,1)S(1)}, u32[]{:S(2)}, u32[]{:S(2)}) collective-permute-start(bf16[7,16,128]{2,1,0:T(8,128)(2,1)S(1)} %get-tuple-element.24), channel_id=1, source_target_pairs={{0,1},{1,0},{2,3},{3,2},{4,5},{5,4},{6,7},{7,6},{8,9},{9,8},{10,11... | collective-permute-start | bytes 86024 | tf_op jit(solution)/shard_map/ppermute | solution.py:426
  26.5 5.7 %collective-permute-start.5 = (bf16[1,26,16,128]{3,2,1,0:T(8,128)(2,1)S(1)}, bf16[1,26,16,128]{3,2,1,0:T(8,128)(2,1)S(1)}, u32[]{:S(2)}, u32[]{:S(2)}) collective-permute-start(bf16[1,26,16,128]{3,2,1,0:T(8,128)(2,1)S(1)} %get-tuple-element.20), channel_id=1, source_target_pairs={{0,1},{1,0},{2,3},{3,2},{4,5},{5,4},{6,7},{7,6},{8,9},{9,8},{10,11... | collective-permute-start | bytes 319496 | tf_op jit(solution)/shard_map/ppermute | solution.py:411
  32.2 5.7 %collective-permute-start.6 = (bf16[1,26,16,128]{3,2,1,0:T(8,128)(2,1)S(1)}, bf16[1,26,16,128]{3,2,1,0:T(8,128)(2,1)S(1)}, u32[]{:S(2)}, u32[]{:S(2)}) collective-permute-start(bf16[1,26,16,128]{3,2,1,0:T(8,128)(2,1)S(1)} %get-tuple-element.21), channel_id=1, source_target_pairs={{0,3},{1,2},{2,1},{3,0},{4,7},{5,6},{6,5},{7,4},{8,11},{9,10},{10,... | collective-permute-start | bytes 319496 | tf_op jit(solution)/shard_map/ppermute | solution.py:410
  37.9 4.8 %collective-permute-start.8 = (bf16[7,16,128]{2,1,0:T(8,128)(2,1)S(1)}, bf16[7,16,128]{2,1,0:T(8,128)(2,1)S(1)}, u32[]{:S(2)}, u32[]{:S(2)}) collective-permute-start(bf16[7,16,128]{2,1,0:T(8,128)(2,1)S(1)} %get-tuple-element.25), channel_id=1, source_target_pairs={{0,3},{1,2},{2,1},{3,0},{4,7},{5,6},{6,5},{7,4},{8,11},{9,10},{10,... | collective-permute-start | bytes 86024 | tf_op jit(solution)/shard_map/ppermute | solution.py:425
  45.1 3.7 %collective-permute-start.10 = (s16[56,16,128]{2,1,0:T(8,128)(2,1)S(1)}, s16[56,16,128]{2,1,0:T(8,128)(2,1)S(1)}, u32[]{:S(2)}, u32[]{:S(2)}) collective-permute-start(s16[56,16,128]{2,1,0:T(8,128)(2,1)S(1)} %get-tuple-element.30), channel_id=1, source_target_pairs={{4,8},{8,4},{5,9},{9,5},{6,10},{10,6},{7,11},{11,7},{20,24},{24,20... | collective-permute-start | bytes 688136 | tf_op jit(solution)/shard_map/ppermute | solution.py:432
  45.7 7.0 %collective-permute-start.9 = (s16[56,16,128]{2,1,0:T(8,128)(2,1)S(1)}, s16[56,16,128]{2,1,0:T(8,128)(2,1)S(1)}, u32[]{:S(2)}, u32[]{:S(2)}) collective-permute-start(s16[56,16,128]{2,1,0:T(8,128)(2,1)S(1)} %get-tuple-element.29), channel_id=1, source_target_pairs={{0,4},{4,0},{8,12},{12,8},{1,5},{5,1},{9,13},{13,9},{2,6},{6,2},{1... | collective-permute-start | bytes 688136 | tf_op jit(solution)/shard_map/ppermute | solution.py:433

commit v7 on v6

--- a/solution.py
+++ b/solution.py
@@ -36,7 +36,7 @@
     return total
 
 
-def fill_matrices(strip, lat_count, rows, lat_taps_ref, lon_taps_ref, matrix_ref, edge_ref):
+def matrix_kernel(strip, lat_count, rows, lat_taps_ref, lon_taps_ref, matrix_ref, edge_ref):
     cols = matrix_ref.shape[1]
     count = lon_taps_ref.shape[0]
     iota = lax.broadcasted_iota
@@ -81,10 +81,11 @@
     return jnp.where(chosen, 1.0, 0.0).astype(BF16)
 
 
-def prepare_kernel(strip, slots, lat_count, parts, *refs):
-    w_refs, (lat_taps_ref, lon_taps_ref, a_ref, b_ref, matrix_ref, edge_ref) = refs[:parts], refs[parts:]
+def pack_kernel(strip, slots, parts, lon_count, piece, *refs):
+    w_refs, (index_ref, a_ref, b_ref, offset_ref, landed, sem) = refs[:parts], refs[parts:]
+    copy = pltpu.make_async_copy(index_ref, landed, sem)
+    copy.start()
     each, channels, rows, cols = w_refs[0].shape
-    fill_matrices(strip, lat_count, rows, lat_taps_ref, lon_taps_ref, matrix_ref, edge_ref)
     members = each * parts
     per = max(1, slots // members)
     for h in range(max(1, members // slots)):
@@ -97,15 +98,17 @@
         total = total.astype(BF16)
         a_ref[h] = total[:, :LANES].reshape(channels // per, rows, LANES)
         b_ref[h] = total[:, LANES:].reshape(channels // per, rows, LANES)
-
-
-def gather_kernel(strip, slots, lon_count, piece, moved_ref, index_ref, grid_ref, a_ref, b_ref, scratch, stack):
-    pieces, channels, width = moved_ref.shape
-    rows, cols = index_ref.shape
+    copy.wait()
     cells = rows * cols
     block = lax.axis_index("lat") * lon_count + lax.axis_index("lon")
-    index = index_ref[...]
-    offset = lax.div(index, cells) * piece + lax.rem(index, cells) - block * piece
+    index = landed[...]
+    offset_ref[...] = lax.div(index, cells) * piece + lax.rem(index, cells) - block * piece
+
+
+def gather_kernel(strip, slots, moved_ref, offset_ref, grid_ref, a_ref, b_ref, scratch, stack):
+    pieces, channels, width = moved_ref.shape
+    rows, cols = offset_ref.shape
+    offset = offset_ref[...]
     scratch[channels:] = jnp.zeros((scratch.shape[0] - channels, rows, cols), F32)
     high = -(-channels // 8) * 8
     for n in range(pieces):
@@ -395,25 +398,28 @@
     per = max(1, slots // count)
 
     strips = jax.ShapeDtypeStruct((max(1, count // slots), own_channels // per, rows, LANES), BF16)
-    smem = pl.BlockSpec(memory_space=pltpu.SMEM)
-    strip_a, strip_b, matrix, edge_matrix = pl.pallas_call(
-        functools.partial(prepare_kernel, strip, slots, lat_count, len(w)),
-        out_shape=(
-            strips,
-            strips,
+    strip_a, strip_b, offset = pl.pallas_call(
+        functools.partial(pack_kernel, strip, slots, len(w), lon_count, piece),
+        out_shape=(strips, strips, jax.ShapeDtypeStruct((rows, cols), jnp.int32)),
+        in_specs=whole(len(w)) + [pl.BlockSpec(memory_space=pl.ANY)], out_specs=whole(3), name="pack",
+        scratch_shapes=[pltpu.VMEM((rows, cols), jnp.int32), pltpu.SemaphoreType.DMA],
+        compiler_params=pltpu.CompilerParams(vmem_limit_bytes=GRANT),
+    )(*w, token_index)
+    matrix, edge_matrix = call(
+        functools.partial(matrix_kernel, strip, lat_count, rows),
+        (
             jax.ShapeDtypeStruct((3 * cols + 3 * rows, cols), BF16),
             jax.ShapeDtypeStruct((3 * LANES, slots // 2 * cols), BF16),
         ),
-        in_specs=whole(len(w)) + [smem] * 2, out_specs=whole(4), name="prepare",
-        compiler_params=pltpu.CompilerParams(vmem_limit_bytes=GRANT),
-    )(*w, lat_taps, lon_taps)
+        smem=2,
+    )(lat_taps, lon_taps)
     strip_b = lax.ppermute(strip_b, "lon", lon_b)
     strip_a = lax.ppermute(strip_a, "lon", lon_a)
 
     padded = -(-own_channels // slots) * slots
     edges = jax.ShapeDtypeStruct((padded // slots, rows, LANES), BF16)
     grid, grid_a, grid_b = pl.pallas_call(
-        functools.partial(gather_kernel, strip, slots, lon_count, piece),
+        functools.partial(gather_kernel, strip, slots),
         out_shape=(jax.ShapeDtypeStruct((own_channels, rows, cols), BF16), edges, edges),
         in_specs=whole(2), out_specs=whole(3),
         scratch_shapes=[
@@ -421,7 +427,7 @@
             pltpu.VMEM((cells // LANES * (-(-own_channels // 8) * 8), LANES), BF16),
         ], name="gather",
         compiler_params=pltpu.CompilerParams(vmem_limit_bytes=GRANT),
-    )(moved, token_index)
+    )(moved, offset)
     grid_b = lax.ppermute(grid_b, "lon", lon_b)
     grid_a = lax.ppermute(grid_a, "lon", lon_a)
 

time: 53.9 us -> 53.8 us (level)
  starting transfers between devices: 23.2 us -> 22.3 us
    ppermute x1, waiting for transfers between devices: 0.72 us -> 2.56 us  [local(): grid_a = lax.ppermute(grid_a, 'lon', lon_a)]
    pallas_call x4 -> x5, Pallas kernels: 4.11 us -> 5.51 us  [run(): pl.pallas_call(kernel, out_shape=out_shape, in_specs=whole(n) + [pl.Block...]
    pallas_call x2, Pallas kernels: 3.45 us -> 2.26 us  [the longest x1 1.63 us: local(): pl.pallas_call(functools.partial(gather_kernel, strip, slots), out_shape=...]
    ppermute x1, waiting for transfers between devices: 3.34 us -> 2.51 us  [local(): grid_b = lax.ppermute(grid_b, 'lon', lon_b)]
    all_to_all x1, waiting for transfers between devices: 2.69 us -> 2.04 us  [local(): lax.all_to_all(tokens, ('lat', 'lon'), split_axis=0, concat_axis=0, tiled...]
    ppermute x1, starting transfers between devices: 0.58 us -> 0.01 us  [local(): grid_b = lax.ppermute(grid_b, 'lon', lon_b)]
  transfers between devices with their start and end apart: 12 -> 12, of which waited for: 6 -> 6; matrix products, arithmetic and copies ran while one was open for 2% -> 2% of each run, Pallas kernels for 10% -> 11%
where the time goes in v7:
time: 53.8 us; the launch traced here: 53.5 us
  starting transfers between devices  22.3 us (41%)
  waiting for transfers between devices  21 us (39%)
  Pallas kernels  7.78 us (14%)
  local copies, waits for them, and re-layouts  2.21 us (4%)
    all_to_all x1, starting transfers between devices, local(): lax.all_to_all(tokens, ('lat', 'lon'), split_axis=0, concat_axis=0, tiled...  7.88 us
    ppermute x2, starting transfers between devices, local(): w_a.append(lax.ppermute(block, 'lat', lat_a))  6.14 us
    ppermute x1, waiting for transfers between devices, local(): strip_b = lax.ppermute(strip_b, 'lon', lon_b)  5.65 us
    pallas_call x5, Pallas kernels, run(): pl.pallas_call(kernel, out_shape=out_shape, in_specs=whole(n) + [pl.Block...  5.51 us
    ppermute x1, waiting for transfers between devices, local(): strip_a = lax.ppermute(strip_a, 'lon', lon_a)  4.26 us
    ppermute x1, waiting for transfers between devices, local(): out_a = lax.ppermute(out_a, 'lat', lat_a)  4 us
    ppermute x1, starting transfers between devices, local(): out_a = lax.ppermute(out_a, 'lat', lat_a)  2.85 us
    ppermute x1, waiting for transfers between devices, local(): grid_a = lax.ppermute(grid_a, 'lon', lon_a)  2.56 us
  transfers between devices with their start and end apart: 12, of which 6 were waited for; matrix products, arithmetic and copies ran while one was open for 2% of the time, Pallas kernels for 11%

profile of v7, /device:TPU:0, one launch (start us, length us, event | category | flops | bytes accessed | tf_op | source)
XLA Modules:
  0.0 53.5 jit_solution(11878307231460357004)
XLA Ops:
  0.0 1.3 %constant_dynamic-slice_fusion.1 = (bf16[2,52,16,128]{3,2,1,0:T(8,128)(2,1)S(1)}, bf16[2,52,16,128]{3,2,1,0:T(8,128)(2,1)S(1)}) fusion(bf16[2,104,16,128]{3,2,1,0:T(8,128)(2,1)} %param.7, s32[]{:T(128)S(6)} %select_n.8, s32[]{:T(128)S(6)} %select_n.7), kind=kLoop, calls=%fused_computation.2 | loop fusion | bytes 1703944 | tf_op jit(solution)/shard_map/dynamic_slice | solution.py:387
  1.3 0.0 copy-start.2
  1.4 0.0 copy-start.3
  1.4 0.6 %collective-permute-start = (bf16[2,52,16,128]{3,2,1,0:T(8,128)(2,1)S(1)}, bf16[2,52,16,128]{3,2,1,0:T(8,128)(2,1)S(1)}, u32[]{:S(2)}, u32[]{:S(2)}) collective-permute-start(bf16[2,52,16,128]{3,2,1,0:T(8,128)(2,1)S(1)} %get-tuple-element.33), channel_id=1, source_target_pairs={{0,16},{16,0},{1,17},{17,1},{2,18},{18,2},{3,19},{19,3},{4,20},{20... | collective-permute-start | bytes 1277960 | tf_op jit(solution)/shard_map/ppermute | solution.py:389
  1.9 0.1 constant_dynamic-slice_fusion
  2.1 0.7 %copy.9 = bf16[52,16,128]{2,0,1:T(8,128)(2,1)} copy(bf16[52,16,128]{2,1,0:T(8,128)(2,1)S(1)} %slice) | data formatting | bytes 425984 | tf_op jit(solution)/shard_map/reshape | solution.py:379
  2.8 7.9 %all-to-all-start = ((bf16[16,52,128]{2,1,0:T(8,128)(2,1)}), bf16[16,52,128]{2,1,0:T(8,128)(2,1)S(1)}, u32[]{:S(2)}, u32[]{:S(2)}) async-start(bf16[16,52,128]{2,1,0:T(8,128)(2,1)} %bitcast.5), calls=%async_computation | async-start | bytes 458752 | tf_op jit(solution)/shard_map/all_to_all | solution.py:380
  10.7 1.9 %collective-permute-start.1 = (bf16[2,52,16,128]{3,2,1,0:T(8,128)(2,1)S(1)}, bf16[2,52,16,128]{3,2,1,0:T(8,128)(2,1)S(1)}, u32[]{:S(2)}, u32[]{:S(2)}) collective-permute-start(bf16[2,52,16,128]{3,2,1,0:T(8,128)(2,1)S(1)} %get-tuple-element.34.refs_0_), channel_id=1, source_target_pairs={{0,4},{4,0},{8,12},{12,8},{1,5},{5,1},{9,13},{13,9},{2,6},{6,2},{1... | collective-permute-start | bytes 1277960 | tf_op jit(solution)/shard_map/ppermute | solution.py:396
  12.6 0.7 %collective-permute-start.3 = (bf16[2,52,16,128]{3,2,1,0:T(8,128)(2,1)S(1)}, bf16[2,52,16,128]{3,2,1,0:T(8,128)(2,1)S(1)}, u32[]{:S(2)}, u32[]{:S(2)}) collective-permute-start(bf16[2,52,16,128]{3,2,1,0:T(8,128)(2,1)S(1)} %get-tuple-element.34.refs_0_), channel_id=1, source_target_pairs={{4,8},{8,4},{5,9},{9,5},{6,10},{10,6},{7,11},{11,7},{20,24},{24,20... | collective-permute-start | bytes 1277960 | tf_op jit(solution)/shard_map/ppermute | solution.py:395
  13.3 0.0 collective-permute-done.refs_1_
  13.3 4.2 %collective-permute-start.2 = (bf16[2,52,16,128]{3,2,1,0:T(8,128)(2,1)S(1)}, bf16[2,52,16,128]{3,2,1,0:T(8,128)(2,1)S(1)}, u32[]{:S(2)}, u32[]{:S(2)}) collective-permute-start(bf16[2,52,16,128]{3,2,1,0:T(8,128)(2,1)S(1)} %collective-permute-done.refs_1_), channel_id=1, source_target_pairs={{0,4},{4,0},{8,12},{12,8},{1,5},{5,1},{9,13},{13,9},{2,6},{6,2},{1... | collective-permute-start | bytes 1277960 | tf_op jit(solution)/shard_map/ppermute | solution.py:396
  17.5 0.7 %collective-permute-start.4 = (bf16[2,52,16,128]{3,2,1,0:T(8,128)(2,1)S(1)}, bf16[2,52,16,128]{3,2,1,0:T(8,128)(2,1)S(1)}, u32[]{:S(2)}, u32[]{:S(2)}) collective-permute-start(bf16[2,52,16,128]{3,2,1,0:T(8,128)(2,1)S(1)} %collective-permute-done.refs_1_), channel_id=1, source_target_pairs={{4,8},{8,4},{5,9},{9,5},{6,10},{10,6},{7,11},{11,7},{20,24},{24,20... | collective-permute-start | bytes 1277960 | tf_op jit(solution)/shard_map/ppermute | solution.py:395
  18.2 0.6 %pack.1 = (bf16[1,26,16,128]{3,2,1,0:T(8,128)(2,1)S(1)}, bf16[1,26,16,128]{3,2,1,0:T(8,128)(2,1)S(1)}, s32[16,128]{1,0:T(8,128)S(1)}) custom-call(bf16[2,52,16,128]{3,2,1,0:T(8,128)(2,1)S(1)} %get-tuple-element.34.refs_0_, bf16[2,52,16,128]{3,2,1,0:T(8,128)(2,1)S(1)} %collective-permute-done.refs_1_, s32[16,128]{1,0:T(8,128)S(1)} %copy-done.1), custom_call_target="tpu_custom_call" | custom-call | tf_op jit(solution)/shard_map/pack/pallas_call | solution.py:401
  18.9 2.0 %all-to-all-done.moved_ref = bf16[16,52,128]{2,1,0:T(8,128)(2,1)S(1)} async-done(((bf16[16,52,128]{2,1,0:T(8,128)(2,1)}), bf16[16,52,128]{2,1,0:T(8,128)(2,1)S(1)}, u32[]{:S(2)}, u32[]{:S(2)}) %all-to-all-start) | async-done | bytes 213024 | tf_op jit(solution)/shard_map/all_to_all | solution.py:380
  20.9 1.6 %gather.1 = (bf16[52,16,128]{2,1,0:T(8,128)(2,1)S(1)}, bf16[7,16,128]{2,1,0:T(8,128)(2,1)S(1)}, bf16[7,16,128]{2,1,0:T(8,128)(2,1)S(1)}) custom-call(bf16[16,52,128]{2,1,0:T(8,128)(2,1)S(1)} %all-to-all-done.moved_ref, s32[16,128]{1,0:T(8,128)S(1)} %get-tuple-element.20.offset_ref), custom_call_target="tpu_custom_call" | custom-call | tf_op jit(solution)/shard_map/gather/pallas_call | solution.py:421
  22.5 1.4 %collective-permute-start.7 = (bf16[7,16,128]{2,1,0:T(8,128)(2,1)S(1)}, bf16[7,16,128]{2,1,0:T(8,128)(2,1)S(1)}, u32[]{:S(2)}, u32[]{:S(2)}) collective-permute-start(bf16[7,16,128]{2,1,0:T(8,128)(2,1)S(1)} %get-tuple-element.26), channel_id=1, source_target_pairs={{0,1},{1,0},{2,3},{3,2},{4,5},{5,4},{6,7},{7,6},{8,9},{9,8},{10,11... | collective-permute-start | bytes 86024 | tf_op jit(solution)/shard_map/ppermute | solution.py:432
  23.9 2.6 %collective-permute-done.7.grid_a_ref = bf16[7,16,128]{2,1,0:T(8,128)(2,1)S(1)} collective-permute-done((bf16[7,16,128]{2,1,0:T(8,128)(2,1)S(1)}, bf16[7,16,128]{2,1,0:T(8,128)(2,1)S(1)}, u32[]{:S(2)}, u32[]{:S(2)}) %collective-permute-start.7) | collective-permute-done | bytes 28704 | tf_op jit(solution)/shard_map/ppermute | solution.py:432
  26.5 1.3 %collective-permute-start.5 = (bf16[1,26,16,128]{3,2,1,0:T(8,128)(2,1)S(1)}, bf16[1,26,16,128]{3,2,1,0:T(8,128)(2,1)S(1)}, u32[]{:S(2)}, u32[]{:S(2)}) collective-permute-start(bf16[1,26,16,128]{3,2,1,0:T(8,128)(2,1)S(1)} %get-tuple-element.22), channel_id=1, source_target_pairs={{0,1},{1,0},{2,3},{3,2},{4,5},{5,4},{6,7},{7,6},{8,9},{9,8},{10,11... | collective-permute-start | bytes 319496 | tf_op jit(solution)/shard_map/ppermute | solution.py:417
  27.8 4.3 %collective-permute-done.5.refs_4_ = bf16[1,26,16,128]{3,2,1,0:T(8,128)(2,1)S(1)} collective-permute-done((bf16[1,26,16,128]{3,2,1,0:T(8,128)(2,1)S(1)}, bf16[1,26,16,128]{3,2,1,0:T(8,128)(2,1)S(1)}, u32[]{:S(2)}, u32[]{:S(2)}) %collective-permute-start.5) | collective-permute-done | bytes 106528 | tf_op jit(solution)/shard_map/ppermute | solution.py:417
  32.1 0.2 collective-permute-start.6
  32.2 5.6 %collective-permute-done.6.refs_5_ = bf16[1,26,16,128]{3,2,1,0:T(8,128)(2,1)S(1)} collective-permute-done((bf16[1,26,16,128]{3,2,1,0:T(8,128)(2,1)S(1)}, bf16[1,26,16,128]{3,2,1,0:T(8,128)(2,1)S(1)}, u32[]{:S(2)}, u32[]{:S(2)}) %collective-permute-start.6) | collective-permute-done | bytes 106528 | tf_op jit(solution)/shard_map/ppermute | solution.py:416
  37.9 1.4 %shard_map.55 = (bf16[432,128]{1,0:T(8,128)(2,1)S(1)}, bf16[384,512]{1,0:T(8,128)(2,1)S(1)}) custom-call(f32[17]{0:T(128)S(1)} %copy-done.2, f32[17]{0:T(128)S(1)} %copy-done.3), custom_call_target="tpu_custom_call" | custom-call | tf_op jit(solution)/shard_map/pallas_call | solution.py:310
  39.2 0.9 %shard_map.56 = (f32[3328,128]{1,0:T(8,128)S(1)}, bf16[1,26,16,128]{3,2,1,0:T(8,128)(2,1)S(1)}, bf16[1,26,16,128]{3,2,1,0:T(8,128)(2,1)S(1)}) custom-call(bf16[2,52,16,128]{3,2,1,0:T(8,128)(2,1)S(1)} %get-tuple-element.34.refs_0_, bf16[2,52,16,128]{3,2,1,0:T(8,128)(2,1)S(1)} %collective-permute-done.refs_1_, ...), custom_call_target="tpu_custom_call" | custom-call | tf_op jit(solution)/shard_map/pallas_call | solution.py:310
  40.1 2.5 %collective-permute-done.8.grid_b_ref = bf16[7,16,128]{2,1,0:T(8,128)(2,1)S(1)} collective-permute-done((bf16[7,16,128]{2,1,0:T(8,128)(2,1)S(1)}, bf16[7,16,128]{2,1,0:T(8,128)(2,1)S(1)}, u32[]{:S(2)}, u32[]{:S(2)}) %collective-permute-start.8) | collective-permute-done | bytes 28704 | tf_op jit(solution)/shard_map/ppermute | solution.py:431
  42.6 1.1 %shard_map.57.refs_7_ = f32[3328,128]{1,0:T(8,128)S(1)} custom-call(bf16[1,26,16,128]{3,2,1,0:T(8,128)(2,1)S(1)} %get-tuple-element.24.strip_a_ref, bf16[1,26,16,128]{3,2,1,0:T(8,128)(2,1)S(1)} %get-tuple-element.25.strip_b_ref, bf16[7,16,128]{2,1,0:T(8,128)(2,1)S(1)} %collective-permute-done.7.grid_a_ref, ...), custom_call_target="tpu_custom_call" | custom-call | tf_op jit(solution)/shard_map/pallas_call | solution.py:310
  43.8 0.0 collective-permute-done.1.refs_2_
  43.8 0.0 collective-permute-done.2.refs_3_
  43.8 1.2 %shard_map.58 = (s16[56,16,128]{2,1,0:T(8,128)(2,1)S(1)}, f32[52,16,128]{2,1,0:T(8,128)S(1)}, s16[56,16,128]{2,1,0:T(8,128)(2,1)S(1)}) custom-call(bf16[2,52,16,128]{3,2,1,0:T(8,128)(2,1)S(1)} %get-tuple-element.34.refs_0_, bf16[2,52,16,128]{3,2,1,0:T(8,128)(2,1)S(1)} %collective-permute-done.refs_1_, ...), custom_call_target="tpu_custom_call" | custom-call | tf_op jit(solution)/shard_map/pallas_call | solution.py:310
  45.0 0.7 %collective-permute-start.10 = (s16[56,16,128]{2,1,0:T(8,128)(2,1)S(1)}, s16[56,16,128]{2,1,0:T(8,128)(2,1)S(1)}, u32[]{:S(2)}, u32[]{:S(2)}) collective-permute-start(s16[56,16,128]{2,1,0:T(8,128)(2,1)S(1)} %get-tuple-element.32), channel_id=1, source_target_pairs={{4,8},{8,4},{5,9},{9,5},{6,10},{10,6},{7,11},{11,7},{20,24},{24,20... | collective-permute-start | bytes 688136 | tf_op jit(solution)/shard_map/ppermute | solution.py:438
  45.7 2.8 %collective-permute-start.9 = (s16[56,16,128]{2,1,0:T(8,128)(2,1)S(1)}, s16[56,16,128]{2,1,0:T(8,128)(2,1)S(1)}, u32[]{:S(2)}, u32[]{:S(2)}) collective-permute-start(s16[56,16,128]{2,1,0:T(8,128)(2,1)S(1)} %get-tuple-element.31), channel_id=1, source_target_pairs={{0,4},{4,0},{8,12},{12,8},{1,5},{5,1},{9,13},{13,9},{2,6},{6,2},{1... | collective-permute-start | bytes 688136 | tf_op jit(solution)/shard_map/ppermute | solution.py:439
  48.6 4.0 %collective-permute-done.9.a_ref = s16[56,16,128]{2,1,0:T(8,128)(2,1)S(1)} collective-permute-done((s16[56,16,128]{2,1,0:T(8,128)(2,1)S(1)}, s16[56,16,128]{2,1,0:T(8,128)(2,1)S(1)}, u32[]{:S(2)}, u32[]{:S(2)}) %collective-permute-start.9) | collective-permute-done | bytes 229408 | tf_op jit(solution)/shard_map/ppermute | solution.py:439
  52.6 0.9 %shard_map.59 = f32[52,16,128]{2,1,0:T(8,128)} custom-call(f32[52,16,128]{2,1,0:T(8,128)S(1)} %get-tuple-element.30.out_ref, s16[56,16,128]{2,1,0:T(8,128)(2,1)S(1)} %collective-permute-done.9.a_ref, s16[56,16,128]{2,1,0:T(8,128)(2,1)S(1)} %collective-permute-done.10.b_ref), custom_call_target="tpu_custom_call" | custom-call | tf_op jit(solution)/shard_map/pallas_call | solution.py:310
  (12 shorter events, 0.1 us)
Async XLA Ops:
  0.0 1.9 %copy-start = (bf16[104,2048]{1,0:T(8,128)(2,1)S(1)}, bf16[104,2048]{1,0:T(8,128)(2,1)}, u32[]{:S(2)}) copy-start(bf16[104,2048]{1,0:T(8,128)(2,1)} %param.5) | copy-start | bytes 1277956
  0.0 18.2 %copy-start.1 = (s32[16,128]{1,0:T(8,128)S(1)}, s32[16,128]{1,0:T(8,128)}, u32[]{:S(2)}) copy-start(s32[16,128]{1,0:T(8,128)} %refs_2_.1) | copy-start | bytes 24580
  1.3 36.5 %copy-start.2 = (f32[17]{0:T(128)S(1)}, f32[17]{0:T(128)}, u32[]{:S(2)}) copy-start(f32[17]{0:T(128)} %lat_taps_ref.1) | copy-start | bytes 208
  1.4 36.5 %copy-start.3 = (f32[17]{0:T(128)S(1)}, f32[17]{0:T(128)}, u32[]{:S(2)}) copy-start(f32[17]{0:T(128)} %lon_taps_ref.1) | copy-start | bytes 208
  1.4 11.9 %collective-permute-start = (bf16[2,52,16,128]{3,2,1,0:T(8,128)(2,1)S(1)}, bf16[2,52,16,128]{3,2,1,0:T(8,128)(2,1)S(1)}, u32[]{:S(2)}, u32[]{:S(2)}) collective-permute-start(bf16[2,52,16,128]{3,2,1,0:T(8,128)(2,1)S(1)} %get-tuple-element.33), channel_id=1, source_target_pairs={{0,16},{16,0},{1,17},{17,1},{2,18},{18,2},{3,19},{19,3},{4,20},{20... | collective-permute-start | bytes 1277960 | tf_op jit(solution)/shard_map/ppermute | solution.py:389
  2.8 18.1 %all-to-all-start = ((bf16[16,52,128]{2,1,0:T(8,128)(2,1)}), bf16[16,52,128]{2,1,0:T(8,128)(2,1)S(1)}, u32[]{:S(2)}, u32[]{:S(2)}) async-start(bf16[16,52,128]{2,1,0:T(8,128)(2,1)} %bitcast.5), calls=%async_computation | async-start | bytes 458752 | tf_op jit(solution)/shard_map/all_to_all | solution.py:380
  10.7 33.1 %collective-permute-start.1 = (bf16[2,52,16,128]{3,2,1,0:T(8,128)(2,1)S(1)}, bf16[2,52,16,128]{3,2,1,0:T(8,128)(2,1)S(1)}, u32[]{:S(2)}, u32[]{:S(2)}) collective-permute-start(bf16[2,52,16,128]{3,2,1,0:T(8,128)(2,1)S(1)} %get-tuple-element.34.refs_0_), channel_id=1, source_target_pairs={{0,4},{4,0},{8,12},{12,8},{1,5},{5,1},{9,13},{13,9},{2,6},{6,2},{1... | collective-permute-start | bytes 1277960 | tf_op jit(solution)/shard_map/ppermute | solution.py:396
  12.6 31.2 %collective-permute-start.3 = (bf16[2,52,16,128]{3,2,1,0:T(8,128)(2,1)S(1)}, bf16[2,52,16,128]{3,2,1,0:T(8,128)(2,1)S(1)}, u32[]{:S(2)}, u32[]{:S(2)}) collective-permute-start(bf16[2,52,16,128]{3,2,1,0:T(8,128)(2,1)S(1)} %get-tuple-element.34.refs_0_), channel_id=1, source_target_pairs={{4,8},{8,4},{5,9},{9,5},{6,10},{10,6},{7,11},{11,7},{20,24},{24,20... | collective-permute-start | bytes 1277960 | tf_op jit(solution)/shard_map/ppermute | solution.py:395
  13.3 30.5 %collective-permute-start.2 = (bf16[2,52,16,128]{3,2,1,0:T(8,128)(2,1)S(1)}, bf16[2,52,16,128]{3,2,1,0:T(8,128)(2,1)S(1)}, u32[]{:S(2)}, u32[]{:S(2)}) collective-permute-start(bf16[2,52,16,128]{3,2,1,0:T(8,128)(2,1)S(1)} %collective-permute-done.refs_1_), channel_id=1, source_target_pairs={{0,4},{4,0},{8,12},{12,8},{1,5},{5,1},{9,13},{13,9},{2,6},{6,2},{1... | collective-permute-start | bytes 1277960 | tf_op jit(solution)/shard_map/ppermute | solution.py:396
  17.5 26.3 %collective-permute-start.4 = (bf16[2,52,16,128]{3,2,1,0:T(8,128)(2,1)S(1)}, bf16[2,52,16,128]{3,2,1,0:T(8,128)(2,1)S(1)}, u32[]{:S(2)}, u32[]{:S(2)}) collective-permute-start(bf16[2,52,16,128]{3,2,1,0:T(8,128)(2,1)S(1)} %collective-permute-done.refs_1_), channel_id=1, source_target_pairs={{4,8},{8,4},{5,9},{9,5},{6,10},{10,6},{7,11},{11,7},{20,24},{24,20... | collective-permute-start | bytes 1277960 | tf_op jit(solution)/shard_map/ppermute | solution.py:395
  22.5 3.9 %collective-permute-start.7 = (bf16[7,16,128]{2,1,0:T(8,128)(2,1)S(1)}, bf16[7,16,128]{2,1,0:T(8,128)(2,1)S(1)}, u32[]{:S(2)}, u32[]{:S(2)}) collective-permute-start(bf16[7,16,128]{2,1,0:T(8,128)(2,1)S(1)} %get-tuple-element.26), channel_id=1, source_target_pairs={{0,1},{1,0},{2,3},{3,2},{4,5},{5,4},{6,7},{7,6},{8,9},{9,8},{10,11... | collective-permute-start | bytes 86024 | tf_op jit(solution)/shard_map/ppermute | solution.py:432
  26.5 5.6 %collective-permute-start.5 = (bf16[1,26,16,128]{3,2,1,0:T(8,128)(2,1)S(1)}, bf16[1,26,16,128]{3,2,1,0:T(8,128)(2,1)S(1)}, u32[]{:S(2)}, u32[]{:S(2)}) collective-permute-start(bf16[1,26,16,128]{3,2,1,0:T(8,128)(2,1)S(1)} %get-tuple-element.22), channel_id=1, source_target_pairs={{0,1},{1,0},{2,3},{3,2},{4,5},{5,4},{6,7},{7,6},{8,9},{9,8},{10,11... | collective-permute-start | bytes 319496 | tf_op jit(solution)/shard_map/ppermute | solution.py:417
  32.1 5.8 %collective-permute-start.6 = (bf16[1,26,16,128]{3,2,1,0:T(8,128)(2,1)S(1)}, bf16[1,26,16,128]{3,2,1,0:T(8,128)(2,1)S(1)}, u32[]{:S(2)}, u32[]{:S(2)}) collective-permute-start(bf16[1,26,16,128]{3,2,1,0:T(8,128)(2,1)S(1)} %get-tuple-element.23), channel_id=1, source_target_pairs={{0,3},{1,2},{2,1},{3,0},{4,7},{5,6},{6,5},{7,4},{8,11},{9,10},{10,... | collective-permute-start | bytes 319496 | tf_op jit(solution)/shard_map/ppermute | solution.py:416
  37.8 4.8 %collective-permute-start.8 = (bf16[7,16,128]{2,1,0:T(8,128)(2,1)S(1)}, bf16[7,16,128]{2,1,0:T(8,128)(2,1)S(1)}, u32[]{:S(2)}, u32[]{:S(2)}) collective-permute-start(bf16[7,16,128]{2,1,0:T(8,128)(2,1)S(1)} %get-tuple-element.27), channel_id=1, source_target_pairs={{0,3},{1,2},{2,1},{3,0},{4,7},{5,6},{6,5},{7,4},{8,11},{9,10},{10,... | collective-permute-start | bytes 86024 | tf_op jit(solution)/shard_map/ppermute | solution.py:431
  45.0 3.5 %collective-permute-start.10 = (s16[56,16,128]{2,1,0:T(8,128)(2,1)S(1)}, s16[56,16,128]{2,1,0:T(8,128)(2,1)S(1)}, u32[]{:S(2)}, u32[]{:S(2)}) collective-permute-start(s16[56,16,128]{2,1,0:T(8,128)(2,1)S(1)} %get-tuple-element.32), channel_id=1, source_target_pairs={{4,8},{8,4},{5,9},{9,5},{6,10},{10,6},{7,11},{11,7},{20,24},{24,20... | collective-permute-start | bytes 688136 | tf_op jit(solution)/shard_map/ppermute | solution.py:438
  45.7 6.8 %collective-permute-start.9 = (s16[56,16,128]{2,1,0:T(8,128)(2,1)S(1)}, s16[56,16,128]{2,1,0:T(8,128)(2,1)S(1)}, u32[]{:S(2)}, u32[]{:S(2)}) collective-permute-start(s16[56,16,128]{2,1,0:T(8,128)(2,1)S(1)} %get-tuple-element.31), channel_id=1, source_target_pairs={{0,4},{4,0},{8,12},{12,8},{1,5},{5,1},{9,13},{13,9},{2,6},{6,2},{1... | collective-permute-start | bytes 688136 | tf_op jit(solution)/shard_map/ppermute | solution.py:439

commit v8 on v7

--- a/solution.py
+++ b/solution.py
@@ -291,8 +291,9 @@
     return v.astype(jnp.int32).astype(jnp.int16)
 
 
-def add_kernel(total, out_ref, a_ref, b_ref, sum_ref, scale_ref):
+def add_kernel(total, out_ref, a_ref, b_ref, result_ref, sum_ref, scale_ref, sems):
     channels, rows, _ = out_ref.shape
+    size, copies = channels // sems.shape[0], []
     for side, ref in enumerate((a_ref, b_ref)):
         for n in range(channels, ref.shape[0]):
             at = pl.ds((n - channels) * rows, rows)
@@ -302,6 +303,12 @@
         for side, ref in enumerate((a_ref, b_ref)):
             added = added + ref[c].astype(F32) * scale_ref[side, c : c + 1, :]
         sum_ref[c] = added / total
+        if (c + 1) % size == 0:
+            at = pl.ds(c + 1 - size, size)
+            copies.append(pltpu.make_async_copy(sum_ref.at[at], result_ref.at[at], sems.at[c // size]))
+            copies[-1].start()
+    for copy in copies:
+        copy.wait()
 
 
 def call(kernel, out_shape, scratch_shapes=(), smem=0):
@@ -351,10 +358,17 @@
 
 
 def add_call(total, channels, rows, cols):
-    return call(
+    block = jax.ShapeDtypeStruct((channels, rows, cols), F32)
+    chunks = 4 if channels % 4 == 0 else 1
+    return pl.pallas_call(
         functools.partial(add_kernel, total),
-        jax.ShapeDtypeStruct((channels, rows, cols), F32),
-        [pltpu.VMEM((2, -(-channels // rows) * rows, cols), F32)],
+        out_shape=block, in_specs=whole(3), out_specs=pl.BlockSpec(memory_space=pl.ANY), name="add",
+        scratch_shapes=[
+            pltpu.VMEM((channels, rows, cols), F32),
+            pltpu.VMEM((2, -(-channels // rows) * rows, cols), F32),
+            pltpu.SemaphoreType.DMA((chunks,)),
+        ],
+        compiler_params=pltpu.CompilerParams(vmem_limit_bytes=GRANT),
     )
 
 

time: 53.8 us -> 53.7 us (level)
    pallas_call x5 -> x4, Pallas kernels: 5.51 us -> 4.61 us  [run(): pl.pallas_call(kernel, out_shape=out_shape, in_specs=whole(n) + [pl.Block...]
    pallas_call x0 -> x1, Pallas kernels: none -> 0.83 us  [local(): return add_call(count - 1, own_channels, rows, cols)(out, out_a, out_b)]
where the time goes in v8:
time: 53.7 us; the launch traced here: 53.4 us
  starting transfers between devices  22.3 us (42%)
  waiting for transfers between devices  21 us (39%)
  Pallas kernels  7.71 us (14%)
  local copies, waits for them, and re-layouts  2.21 us (4%)
    all_to_all x1, starting transfers between devices, local(): lax.all_to_all(tokens, ('lat', 'lon'), split_axis=0, concat_axis=0, tiled...  7.88 us
    ppermute x2, starting transfers between devices, local(): w_a.append(lax.ppermute(block, 'lat', lat_a))  6.14 us
    ppermute x1, waiting for transfers between devices, local(): strip_b = lax.ppermute(strip_b, 'lon', lon_b)  5.65 us
    pallas_call x4, Pallas kernels, run(): pl.pallas_call(kernel, out_shape=out_shape, in_specs=whole(n) + [pl.Block...  4.61 us
    ppermute x1, waiting for transfers between devices, local(): strip_a = lax.ppermute(strip_a, 'lon', lon_a)  4.26 us
    ppermute x1, waiting for transfers between devices, local(): out_a = lax.ppermute(out_a, 'lat', lat_a)  4 us
    ppermute x1, starting transfers between devices, local(): out_a = lax.ppermute(out_a, 'lat', lat_a)  2.85 us
    ppermute x1, waiting for transfers between devices, local(): grid_a = lax.ppermute(grid_a, 'lon', lon_a)  2.56 us
  transfers between devices with their start and end apart: 12, of which 6 were waited for; matrix products, arithmetic and copies ran while one was open for 2% of the time, Pallas kernels for 11%

profile of v8, /device:TPU:0, one launch (start us, length us, event | category | flops | bytes accessed | tf_op | source)
XLA Modules:
  0.0 53.4 jit_solution(16244521447750163487)
XLA Ops:
  0.0 1.3 %constant_dynamic-slice_fusion.1 = (bf16[2,52,16,128]{3,2,1,0:T(8,128)(2,1)S(1)}, bf16[2,52,16,128]{3,2,1,0:T(8,128)(2,1)S(1)}) fusion(bf16[2,104,16,128]{3,2,1,0:T(8,128)(2,1)} %param.7, s32[]{:T(128)S(6)} %select_n.8, s32[]{:T(128)S(6)} %select_n.7), kind=kLoop, calls=%fused_computation.2 | loop fusion | bytes 1703944 | tf_op jit(solution)/shard_map/dynamic_slice | solution.py:401
  1.3 0.0 copy-start.2
  1.4 0.0 copy-start.3
  1.4 0.6 %collective-permute-start = (bf16[2,52,16,128]{3,2,1,0:T(8,128)(2,1)S(1)}, bf16[2,52,16,128]{3,2,1,0:T(8,128)(2,1)S(1)}, u32[]{:S(2)}, u32[]{:S(2)}) collective-permute-start(bf16[2,52,16,128]{3,2,1,0:T(8,128)(2,1)S(1)} %get-tuple-element.33), channel_id=1, source_target_pairs={{0,16},{16,0},{1,17},{17,1},{2,18},{18,2},{3,19},{19,3},{4,20},{20... | collective-permute-start | bytes 1277960 | tf_op jit(solution)/shard_map/ppermute | solution.py:403
  1.9 0.1 constant_dynamic-slice_fusion
  2.1 0.7 %copy.9 = bf16[52,16,128]{2,0,1:T(8,128)(2,1)} copy(bf16[52,16,128]{2,1,0:T(8,128)(2,1)S(1)} %slice) | data formatting | bytes 425984 | tf_op jit(solution)/shard_map/reshape | solution.py:393
  2.8 7.9 %all-to-all-start = ((bf16[16,52,128]{2,1,0:T(8,128)(2,1)}), bf16[16,52,128]{2,1,0:T(8,128)(2,1)S(1)}, u32[]{:S(2)}, u32[]{:S(2)}) async-start(bf16[16,52,128]{2,1,0:T(8,128)(2,1)} %bitcast.5), calls=%async_computation | async-start | bytes 458752 | tf_op jit(solution)/shard_map/all_to_all | solution.py:394
  10.7 1.9 %collective-permute-start.1 = (bf16[2,52,16,128]{3,2,1,0:T(8,128)(2,1)S(1)}, bf16[2,52,16,128]{3,2,1,0:T(8,128)(2,1)S(1)}, u32[]{:S(2)}, u32[]{:S(2)}) collective-permute-start(bf16[2,52,16,128]{3,2,1,0:T(8,128)(2,1)S(1)} %get-tuple-element.34.refs_0_), channel_id=1, source_target_pairs={{0,4},{4,0},{8,12},{12,8},{1,5},{5,1},{9,13},{13,9},{2,6},{6,2},{1... | collective-permute-start | bytes 1277960 | tf_op jit(solution)/shard_map/ppermute | solution.py:410
  12.6 0.7 %collective-permute-start.3 = (bf16[2,52,16,128]{3,2,1,0:T(8,128)(2,1)S(1)}, bf16[2,52,16,128]{3,2,1,0:T(8,128)(2,1)S(1)}, u32[]{:S(2)}, u32[]{:S(2)}) collective-permute-start(bf16[2,52,16,128]{3,2,1,0:T(8,128)(2,1)S(1)} %get-tuple-element.34.refs_0_), channel_id=1, source_target_pairs={{4,8},{8,4},{5,9},{9,5},{6,10},{10,6},{7,11},{11,7},{20,24},{24,20... | collective-permute-start | bytes 1277960 | tf_op jit(solution)/shard_map/ppermute | solution.py:409
  13.3 0.0 collective-permute-done.refs_1_
  13.3 4.2 %collective-permute-start.2 = (bf16[2,52,16,128]{3,2,1,0:T(8,128)(2,1)S(1)}, bf16[2,52,16,128]{3,2,1,0:T(8,128)(2,1)S(1)}, u32[]{:S(2)}, u32[]{:S(2)}) collective-permute-start(bf16[2,52,16,128]{3,2,1,0:T(8,128)(2,1)S(1)} %collective-permute-done.refs_1_), channel_id=1, source_target_pairs={{0,4},{4,0},{8,12},{12,8},{1,5},{5,1},{9,13},{13,9},{2,6},{6,2},{1... | collective-permute-start | bytes 1277960 | tf_op jit(solution)/shard_map/ppermute | solution.py:410
  17.5 0.7 %collective-permute-start.4 = (bf16[2,52,16,128]{3,2,1,0:T(8,128)(2,1)S(1)}, bf16[2,52,16,128]{3,2,1,0:T(8,128)(2,1)S(1)}, u32[]{:S(2)}, u32[]{:S(2)}) collective-permute-start(bf16[2,52,16,128]{3,2,1,0:T(8,128)(2,1)S(1)} %collective-permute-done.refs_1_), channel_id=1, source_target_pairs={{4,8},{8,4},{5,9},{9,5},{6,10},{10,6},{7,11},{11,7},{20,24},{24,20... | collective-permute-start | bytes 1277960 | tf_op jit(solution)/shard_map/ppermute | solution.py:409
  18.2 0.6 %pack.1 = (bf16[1,26,16,128]{3,2,1,0:T(8,128)(2,1)S(1)}, bf16[1,26,16,128]{3,2,1,0:T(8,128)(2,1)S(1)}, s32[16,128]{1,0:T(8,128)S(1)}) custom-call(bf16[2,52,16,128]{3,2,1,0:T(8,128)(2,1)S(1)} %get-tuple-element.34.refs_0_, bf16[2,52,16,128]{3,2,1,0:T(8,128)(2,1)S(1)} %collective-permute-done.refs_1_, s32[16,128]{1,0:T(8,128)S(1)} %copy-done.1), custom_call_target="tpu_custom_call" | custom-call | tf_op jit(solution)/shard_map/pack/pallas_call | solution.py:415
  18.9 2.0 %all-to-all-done.moved_ref = bf16[16,52,128]{2,1,0:T(8,128)(2,1)S(1)} async-done(((bf16[16,52,128]{2,1,0:T(8,128)(2,1)}), bf16[16,52,128]{2,1,0:T(8,128)(2,1)S(1)}, u32[]{:S(2)}, u32[]{:S(2)}) %all-to-all-start) | async-done | bytes 213024 | tf_op jit(solution)/shard_map/all_to_all | solution.py:394
  20.9 1.6 %gather.1 = (bf16[52,16,128]{2,1,0:T(8,128)(2,1)S(1)}, bf16[7,16,128]{2,1,0:T(8,128)(2,1)S(1)}, bf16[7,16,128]{2,1,0:T(8,128)(2,1)S(1)}) custom-call(bf16[16,52,128]{2,1,0:T(8,128)(2,1)S(1)} %all-to-all-done.moved_ref, s32[16,128]{1,0:T(8,128)S(1)} %get-tuple-element.20.offset_ref), custom_call_target="tpu_custom_call" | custom-call | tf_op jit(solution)/shard_map/gather/pallas_call | solution.py:435
  22.5 1.4 %collective-permute-start.7 = (bf16[7,16,128]{2,1,0:T(8,128)(2,1)S(1)}, bf16[7,16,128]{2,1,0:T(8,128)(2,1)S(1)}, u32[]{:S(2)}, u32[]{:S(2)}) collective-permute-start(bf16[7,16,128]{2,1,0:T(8,128)(2,1)S(1)} %get-tuple-element.26), channel_id=1, source_target_pairs={{0,1},{1,0},{2,3},{3,2},{4,5},{5,4},{6,7},{7,6},{8,9},{9,8},{10,11... | collective-permute-start | bytes 86024 | tf_op jit(solution)/shard_map/ppermute | solution.py:446
  23.9 2.6 %collective-permute-done.7.grid_a_ref = bf16[7,16,128]{2,1,0:T(8,128)(2,1)S(1)} collective-permute-done((bf16[7,16,128]{2,1,0:T(8,128)(2,1)S(1)}, bf16[7,16,128]{2,1,0:T(8,128)(2,1)S(1)}, u32[]{:S(2)}, u32[]{:S(2)}) %collective-permute-start.7) | collective-permute-done | bytes 28704 | tf_op jit(solution)/shard_map/ppermute | solution.py:446
  26.5 1.3 %collective-permute-start.5 = (bf16[1,26,16,128]{3,2,1,0:T(8,128)(2,1)S(1)}, bf16[1,26,16,128]{3,2,1,0:T(8,128)(2,1)S(1)}, u32[]{:S(2)}, u32[]{:S(2)}) collective-permute-start(bf16[1,26,16,128]{3,2,1,0:T(8,128)(2,1)S(1)} %get-tuple-element.22), channel_id=1, source_target_pairs={{0,1},{1,0},{2,3},{3,2},{4,5},{5,4},{6,7},{7,6},{8,9},{9,8},{10,11... | collective-permute-start | bytes 319496 | tf_op jit(solution)/shard_map/ppermute | solution.py:431
  27.8 4.3 %collective-permute-done.5.refs_4_ = bf16[1,26,16,128]{3,2,1,0:T(8,128)(2,1)S(1)} collective-permute-done((bf16[1,26,16,128]{3,2,1,0:T(8,128)(2,1)S(1)}, bf16[1,26,16,128]{3,2,1,0:T(8,128)(2,1)S(1)}, u32[]{:S(2)}, u32[]{:S(2)}) %collective-permute-start.5) | collective-permute-done | bytes 106528 | tf_op jit(solution)/shard_map/ppermute | solution.py:431
  32.1 0.2 collective-permute-start.6
  32.2 5.6 %collective-permute-done.6.refs_5_ = bf16[1,26,16,128]{3,2,1,0:T(8,128)(2,1)S(1)} collective-permute-done((bf16[1,26,16,128]{3,2,1,0:T(8,128)(2,1)S(1)}, bf16[1,26,16,128]{3,2,1,0:T(8,128)(2,1)S(1)}, u32[]{:S(2)}, u32[]{:S(2)}) %collective-permute-start.6) | collective-permute-done | bytes 106528 | tf_op jit(solution)/shard_map/ppermute | solution.py:430
  37.9 1.4 %shard_map.55 = (bf16[432,128]{1,0:T(8,128)(2,1)S(1)}, bf16[384,512]{1,0:T(8,128)(2,1)S(1)}) custom-call(f32[17]{0:T(128)S(1)} %copy-done.2, f32[17]{0:T(128)S(1)} %copy-done.3), custom_call_target="tpu_custom_call" | custom-call | tf_op jit(solution)/shard_map/pallas_call | solution.py:317
  39.2 0.9 %shard_map.56 = (f32[3328,128]{1,0:T(8,128)S(1)}, bf16[1,26,16,128]{3,2,1,0:T(8,128)(2,1)S(1)}, bf16[1,26,16,128]{3,2,1,0:T(8,128)(2,1)S(1)}) custom-call(bf16[2,52,16,128]{3,2,1,0:T(8,128)(2,1)S(1)} %get-tuple-element.34.refs_0_, bf16[2,52,16,128]{3,2,1,0:T(8,128)(2,1)S(1)} %collective-permute-done.refs_1_, ...), custom_call_target="tpu_custom_call" | custom-call | tf_op jit(solution)/shard_map/pallas_call | solution.py:317
  40.1 2.5 %collective-permute-done.8.grid_b_ref = bf16[7,16,128]{2,1,0:T(8,128)(2,1)S(1)} collective-permute-done((bf16[7,16,128]{2,1,0:T(8,128)(2,1)S(1)}, bf16[7,16,128]{2,1,0:T(8,128)(2,1)S(1)}, u32[]{:S(2)}, u32[]{:S(2)}) %collective-permute-start.8) | collective-permute-done | bytes 28704 | tf_op jit(solution)/shard_map/ppermute | solution.py:445
  42.6 1.1 %shard_map.57.refs_7_ = f32[3328,128]{1,0:T(8,128)S(1)} custom-call(bf16[1,26,16,128]{3,2,1,0:T(8,128)(2,1)S(1)} %get-tuple-element.24.strip_a_ref, bf16[1,26,16,128]{3,2,1,0:T(8,128)(2,1)S(1)} %get-tuple-element.25.strip_b_ref, bf16[7,16,128]{2,1,0:T(8,128)(2,1)S(1)} %collective-permute-done.7.grid_a_ref, ...), custom_call_target="tpu_custom_call" | custom-call | tf_op jit(solution)/shard_map/pallas_call | solution.py:317
  43.8 0.0 collective-permute-done.1.refs_2_
  43.8 0.0 collective-permute-done.2.refs_3_
  43.8 1.2 %shard_map.58 = (s16[56,16,128]{2,1,0:T(8,128)(2,1)S(1)}, f32[52,16,128]{2,1,0:T(8,128)S(1)}, s16[56,16,128]{2,1,0:T(8,128)(2,1)S(1)}) custom-call(bf16[2,52,16,128]{3,2,1,0:T(8,128)(2,1)S(1)} %get-tuple-element.34.refs_0_, bf16[2,52,16,128]{3,2,1,0:T(8,128)(2,1)S(1)} %collective-permute-done.refs_1_, ...), custom_call_target="tpu_custom_call" | custom-call | tf_op jit(solution)/shard_map/pallas_call | solution.py:317
  45.0 0.7 %collective-permute-start.10 = (s16[56,16,128]{2,1,0:T(8,128)(2,1)S(1)}, s16[56,16,128]{2,1,0:T(8,128)(2,1)S(1)}, u32[]{:S(2)}, u32[]{:S(2)}) collective-permute-start(s16[56,16,128]{2,1,0:T(8,128)(2,1)S(1)} %get-tuple-element.32), channel_id=1, source_target_pairs={{4,8},{8,4},{5,9},{9,5},{6,10},{10,6},{7,11},{11,7},{20,24},{24,20... | collective-permute-start | bytes 688136 | tf_op jit(solution)/shard_map/ppermute | solution.py:452
  45.7 2.8 %collective-permute-start.9 = (s16[56,16,128]{2,1,0:T(8,128)(2,1)S(1)}, s16[56,16,128]{2,1,0:T(8,128)(2,1)S(1)}, u32[]{:S(2)}, u32[]{:S(2)}) collective-permute-start(s16[56,16,128]{2,1,0:T(8,128)(2,1)S(1)} %get-tuple-element.31), channel_id=1, source_target_pairs={{0,4},{4,0},{8,12},{12,8},{1,5},{5,1},{9,13},{13,9},{2,6},{6,2},{1... | collective-permute-start | bytes 688136 | tf_op jit(solution)/shard_map/ppermute | solution.py:453
  48.6 4.0 %collective-permute-done.9.a_ref = s16[56,16,128]{2,1,0:T(8,128)(2,1)S(1)} collective-permute-done((s16[56,16,128]{2,1,0:T(8,128)(2,1)S(1)}, s16[56,16,128]{2,1,0:T(8,128)(2,1)S(1)}, u32[]{:S(2)}, u32[]{:S(2)}) %collective-permute-start.9) | collective-permute-done | bytes 229408 | tf_op jit(solution)/shard_map/ppermute | solution.py:453
  52.6 0.8 %add.10 = f32[52,16,128]{2,1,0:T(8,128)} custom-call(f32[52,16,128]{2,1,0:T(8,128)S(1)} %get-tuple-element.30.out_ref, s16[56,16,128]{2,1,0:T(8,128)(2,1)S(1)} %collective-permute-done.9.a_ref, s16[56,16,128]{2,1,0:T(8,128)(2,1)S(1)} %collective-permute-done.10.b_ref), custom_call_target="tpu_custom_call" | custom-call | tf_op jit(solution)/shard_map/add/pallas_call | solution.py:454
  (12 shorter events, 0.1 us)
Async XLA Ops:
  0.0 1.9 %copy-start = (bf16[104,2048]{1,0:T(8,128)(2,1)S(1)}, bf16[104,2048]{1,0:T(8,128)(2,1)}, u32[]{:S(2)}) copy-start(bf16[104,2048]{1,0:T(8,128)(2,1)} %param.5) | copy-start | bytes 1277956
  0.0 18.2 %copy-start.1 = (s32[16,128]{1,0:T(8,128)S(1)}, s32[16,128]{1,0:T(8,128)}, u32[]{:S(2)}) copy-start(s32[16,128]{1,0:T(8,128)} %refs_2_.1) | copy-start | bytes 24580
  1.3 36.5 %copy-start.2 = (f32[17]{0:T(128)S(1)}, f32[17]{0:T(128)}, u32[]{:S(2)}) copy-start(f32[17]{0:T(128)} %lat_taps_ref.1) | copy-start | bytes 208
  1.4 36.5 %copy-start.3 = (f32[17]{0:T(128)S(1)}, f32[17]{0:T(128)}, u32[]{:S(2)}) copy-start(f32[17]{0:T(128)} %lon_taps_ref.1) | copy-start | bytes 208
  1.4 11.9 %collective-permute-start = (bf16[2,52,16,128]{3,2,1,0:T(8,128)(2,1)S(1)}, bf16[2,52,16,128]{3,2,1,0:T(8,128)(2,1)S(1)}, u32[]{:S(2)}, u32[]{:S(2)}) collective-permute-start(bf16[2,52,16,128]{3,2,1,0:T(8,128)(2,1)S(1)} %get-tuple-element.33), channel_id=1, source_target_pairs={{0,16},{16,0},{1,17},{17,1},{2,18},{18,2},{3,19},{19,3},{4,20},{20... | collective-permute-start | bytes 1277960 | tf_op jit(solution)/shard_map/ppermute | solution.py:403
  2.8 18.1 %all-to-all-start = ((bf16[16,52,128]{2,1,0:T(8,128)(2,1)}), bf16[16,52,128]{2,1,0:T(8,128)(2,1)S(1)}, u32[]{:S(2)}, u32[]{:S(2)}) async-start(bf16[16,52,128]{2,1,0:T(8,128)(2,1)} %bitcast.5), calls=%async_computation | async-start | bytes 458752 | tf_op jit(solution)/shard_map/all_to_all | solution.py:394
  10.7 33.1 %collective-permute-start.1 = (bf16[2,52,16,128]{3,2,1,0:T(8,128)(2,1)S(1)}, bf16[2,52,16,128]{3,2,1,0:T(8,128)(2,1)S(1)}, u32[]{:S(2)}, u32[]{:S(2)}) collective-permute-start(bf16[2,52,16,128]{3,2,1,0:T(8,128)(2,1)S(1)} %get-tuple-element.34.refs_0_), channel_id=1, source_target_pairs={{0,4},{4,0},{8,12},{12,8},{1,5},{5,1},{9,13},{13,9},{2,6},{6,2},{1... | collective-permute-start | bytes 1277960 | tf_op jit(solution)/shard_map/ppermute | solution.py:410
  12.6 31.2 %collective-permute-start.3 = (bf16[2,52,16,128]{3,2,1,0:T(8,128)(2,1)S(1)}, bf16[2,52,16,128]{3,2,1,0:T(8,128)(2,1)S(1)}, u32[]{:S(2)}, u32[]{:S(2)}) collective-permute-start(bf16[2,52,16,128]{3,2,1,0:T(8,128)(2,1)S(1)} %get-tuple-element.34.refs_0_), channel_id=1, source_target_pairs={{4,8},{8,4},{5,9},{9,5},{6,10},{10,6},{7,11},{11,7},{20,24},{24,20... | collective-permute-start | bytes 1277960 | tf_op jit(solution)/shard_map/ppermute | solution.py:409
  13.3 30.5 %collective-permute-start.2 = (bf16[2,52,16,128]{3,2,1,0:T(8,128)(2,1)S(1)}, bf16[2,52,16,128]{3,2,1,0:T(8,128)(2,1)S(1)}, u32[]{:S(2)}, u32[]{:S(2)}) collective-permute-start(bf16[2,52,16,128]{3,2,1,0:T(8,128)(2,1)S(1)} %collective-permute-done.refs_1_), channel_id=1, source_target_pairs={{0,4},{4,0},{8,12},{12,8},{1,5},{5,1},{9,13},{13,9},{2,6},{6,2},{1... | collective-permute-start | bytes 1277960 | tf_op jit(solution)/shard_map/ppermute | solution.py:410
  17.5 26.3 %collective-permute-start.4 = (bf16[2,52,16,128]{3,2,1,0:T(8,128)(2,1)S(1)}, bf16[2,52,16,128]{3,2,1,0:T(8,128)(2,1)S(1)}, u32[]{:S(2)}, u32[]{:S(2)}) collective-permute-start(bf16[2,52,16,128]{3,2,1,0:T(8,128)(2,1)S(1)} %collective-permute-done.refs_1_), channel_id=1, source_target_pairs={{4,8},{8,4},{5,9},{9,5},{6,10},{10,6},{7,11},{11,7},{20,24},{24,20... | collective-permute-start | bytes 1277960 | tf_op jit(solution)/shard_map/ppermute | solution.py:409
  22.5 3.9 %collective-permute-start.7 = (bf16[7,16,128]{2,1,0:T(8,128)(2,1)S(1)}, bf16[7,16,128]{2,1,0:T(8,128)(2,1)S(1)}, u32[]{:S(2)}, u32[]{:S(2)}) collective-permute-start(bf16[7,16,128]{2,1,0:T(8,128)(2,1)S(1)} %get-tuple-element.26), channel_id=1, source_target_pairs={{0,1},{1,0},{2,3},{3,2},{4,5},{5,4},{6,7},{7,6},{8,9},{9,8},{10,11... | collective-permute-start | bytes 86024 | tf_op jit(solution)/shard_map/ppermute | solution.py:446
  26.5 5.6 %collective-permute-start.5 = (bf16[1,26,16,128]{3,2,1,0:T(8,128)(2,1)S(1)}, bf16[1,26,16,128]{3,2,1,0:T(8,128)(2,1)S(1)}, u32[]{:S(2)}, u32[]{:S(2)}) collective-permute-start(bf16[1,26,16,128]{3,2,1,0:T(8,128)(2,1)S(1)} %get-tuple-element.22), channel_id=1, source_target_pairs={{0,1},{1,0},{2,3},{3,2},{4,5},{5,4},{6,7},{7,6},{8,9},{9,8},{10,11... | collective-permute-start | bytes 319496 | tf_op jit(solution)/shard_map/ppermute | solution.py:431
  32.1 5.8 %collective-permute-start.6 = (bf16[1,26,16,128]{3,2,1,0:T(8,128)(2,1)S(1)}, bf16[1,26,16,128]{3,2,1,0:T(8,128)(2,1)S(1)}, u32[]{:S(2)}, u32[]{:S(2)}) collective-permute-start(bf16[1,26,16,128]{3,2,1,0:T(8,128)(2,1)S(1)} %get-tuple-element.23), channel_id=1, source_target_pairs={{0,3},{1,2},{2,1},{3,0},{4,7},{5,6},{6,5},{7,4},{8,11},{9,10},{10,... | collective-permute-start | bytes 319496 | tf_op jit(solution)/shard_map/ppermute | solution.py:430
  37.8 4.8 %collective-permute-start.8 = (bf16[7,16,128]{2,1,0:T(8,128)(2,1)S(1)}, bf16[7,16,128]{2,1,0:T(8,128)(2,1)S(1)}, u32[]{:S(2)}, u32[]{:S(2)}) collective-permute-start(bf16[7,16,128]{2,1,0:T(8,128)(2,1)S(1)} %get-tuple-element.27), channel_id=1, source_target_pairs={{0,3},{1,2},{2,1},{3,0},{4,7},{5,6},{6,5},{7,4},{8,11},{9,10},{10,... | collective-permute-start | bytes 86024 | tf_op jit(solution)/shard_map/ppermute | solution.py:445
  45.0 3.5 %collective-permute-start.10 = (s16[56,16,128]{2,1,0:T(8,128)(2,1)S(1)}, s16[56,16,128]{2,1,0:T(8,128)(2,1)S(1)}, u32[]{:S(2)}, u32[]{:S(2)}) collective-permute-start(s16[56,16,128]{2,1,0:T(8,128)(2,1)S(1)} %get-tuple-element.32), channel_id=1, source_target_pairs={{4,8},{8,4},{5,9},{9,5},{6,10},{10,6},{7,11},{11,7},{20,24},{24,20... | collective-permute-start | bytes 688136 | tf_op jit(solution)/shard_map/ppermute | solution.py:452
  45.7 6.8 %collective-permute-start.9 = (s16[56,16,128]{2,1,0:T(8,128)(2,1)S(1)}, s16[56,16,128]{2,1,0:T(8,128)(2,1)S(1)}, u32[]{:S(2)}, u32[]{:S(2)}) collective-permute-start(s16[56,16,128]{2,1,0:T(8,128)(2,1)S(1)} %get-tuple-element.31), channel_id=1, source_target_pairs={{0,4},{4,0},{8,12},{12,8},{1,5},{5,1},{9,13},{13,9},{2,6},{6,2},{1... | collective-permute-start | bytes 688136 | tf_op jit(solution)/shard_map/ppermute | solution.py:453
